TPU v7x, 256 devices: a whole 4x4x8 slice. The times are simulated.
256 devices in a mesh: ctx: 16 (over y, x), head: 16 (over z, core).
Axes of the slice: x: 4, y: 4, z: 8, core: 2. Of those that a mesh axis runs over, the one named last changes fastest.
Arguments:
- queries: bfloat16 [2, 4096, 8192], P(None, 'ctx', 'head'), may hold values from -4.5 to 4.5
- key_rows: bfloat16 [2, 4096, 512], P(None, 'ctx'), may hold values from -4.5 to 4.5
- value_rows: bfloat16 [2, 4096, 512], P(None, 'ctx'), may hold values from -6 to 6
- out_weight: bfloat16 [8192, 8192], P('head'), may hold values from -0.0625 to 0.0625
- span_owner: int32 [2, 16], replicated, may hold values from 0 to 15, each once within a row
- vertical_blocks: int32 [64, 4], replicated, may hold values from 0 to 63, as said below
- slash_offsets: int32 [64, 4], replicated, may hold values from 1 to 63, as said below
Outputs:
- projected: bfloat16 [2, 4096, 8192], P(None, ('ctx', 'head'))
Inputs may be any that keep to these rules, and one draw needn't show every extreme that they name: `vertical_blocks`: the 4 entries of a head are distinct block numbers. `slash_offsets`: the 4 entries of a head are distinct.
All inputs are finite; a program needn't handle non-finite values.
Results may differ from a plain program's by a relative error of at most 0.017.
Values may be sent and summed in bfloat16 or wider, within the bound.
No kernel may reach another device: no remote copies, remote signals or barrier semaphores. Data moves between devices by JAX's collectives and lax.ppermute only.
A program may use at most 64 MiB of HBM per device.

v0:
```python
import functools
import math

import jax
import jax.numpy as jnp
from jax import lax
from jax.experimental import pallas as pl
from jax.experimental.pallas import tpu as pltpu
from jax.sharding import PartitionSpec as P


QH = 64
KVH = 4
HD = 128
BLK = 128
STEPS = 2
SPANS = 16
LOCAL_HEADS = 4
SPAN = 256
NV = 4
NS = 4
DW = 8192
TILE = 512
HALVES = 2
WIDTH = DW // HALVES
TILES = 1 + NV + NS
PAIRS = LOCAL_HEADS * 2
HIDDEN = -1e30
MIB = 1 << 20


ANYWHERE = pl.BlockSpec(memory_space=pl.ANY)
SCALARS = pl.BlockSpec(memory_space=pltpu.SMEM)
IN_HBM = pl.BlockSpec(memory_space=pltpu.HBM)
IN_VMEM = pl.BlockSpec(memory_space=pltpu.VMEM)


def core_swap(heads):
    return [(h, h ^ 1) for h in range(heads)]


def shift_z(heads, amount):
    chips = heads // 2
    return [(h, ((h // 2 + amount) % chips) * 2 + h % 2) for h in range(heads)]


def after(x, *earlier):
    return pl.pallas_call(
        lambda *refs: None,
        out_shape=jax.ShapeDtypeStruct(x.shape, x.dtype),
        in_specs=[ANYWHERE] * (1 + len(earlier)),
        out_specs=ANYWHERE,
        input_output_aliases={0: 0},
        compiler_params=pltpu.CompilerParams(vmem_limit_bytes=MIB),
        name="after",
    )(x, *earlier)


def plan_kernel(owner, vertical, slash, table):
    device = lax.axis_index("ctx")
    head_group = lax.axis_index("head")

    def one_pair(index, carry):
        step = index // PAIRS
        pair = lax.rem(index, PAIRS)
        head = head_group * LOCAL_HEADS + pair // 2

        def look(p, place):
            return place + jnp.where(owner[step, p] == device, p, 0)

        place = lax.fori_loop(0, SPANS, look, jnp.int32(0))
        block = (step * SPANS + place) * 2 + lax.rem(pair, 2)

        def put(slot, k, good):
            k = jnp.where(good, k, block)
            span = k // 2
            which = span // SPANS
            holder = owner[which, lax.rem(span, SPANS)]
            stored = (which * 2 + lax.rem(k, 2)) * SPANS + holder
            table[index * TILES + slot] = stored * 2 + jnp.where(good, 1, 0)

        put(0, block, block >= 0)
        picked = [vertical[head, n] for n in range(NV)]
        for n, k in enumerate(picked):
            put(1 + n, k, k < block)
        for n in range(NS):
            k = block - slash[head, n]
            good = k >= 0
            for other in picked:
                good = good & (k != other)
            put(1 + NV + n, k, good)
        return carry

    lax.fori_loop(0, STEPS * PAIRS, one_pair, 0)


def make_plan(owner, vertical, slash):
    return pl.pallas_call(
        plan_kernel,
        out_shape=jax.ShapeDtypeStruct((STEPS * PAIRS * TILES,), jnp.int32),
        in_specs=[SCALARS] * 3,
        out_specs=SCALARS,
        compiler_params=pltpu.CompilerParams(vmem_limit_bytes=MIB),
        name="plan",
    )(owner, vertical, slash)


def attend_kernel(step, *refs):
    stores = 2 * (step + 1)
    table, q_hbm, w_hbm = refs[:3]
    kv_hbm = refs[3 : 3 + stores]
    out, send, own, q_v, kv_v, w_v, sems = refs[-7:]
    core = lax.rem(lax.axis_index("head"), 2)

    copies = [pltpu.make_async_copy(q_hbm.at[step], q_v, sems.at[0])]
    for index in range(step + 1):
        for side in range(2):
            half = core if side == 0 else 1 - core
            start = pl.multiple_of((2 * index + half) * SPANS, SPANS)
            copies.append(
                pltpu.make_async_copy(
                    kv_hbm[2 * index + side],
                    kv_v.at[pl.ds(start, SPANS)],
                    sems.at[1 + 2 * index + side],
                )
            )
    w_copy = pltpu.make_async_copy(w_hbm.at[:, pl.ds(0, WIDTH)], w_v, sems.at[1 + stores])
    for copy in copies:
        copy.start()
    w_copy.start()
    for copy in copies:
        copy.wait()

    rows_at = lax.broadcasted_iota(jnp.int32, (BLK, BLK), 0)
    cols_at = lax.broadcasted_iota(jnp.int32, (BLK, BLK), 1)
    causal = cols_at <= rows_at
    scale = 1.0 / math.sqrt(HD)

    def one_pair(local_head, inner):
        q_cols = pl.ds(pl.multiple_of(local_head * HD, HD), HD)
        q = q_v[inner * BLK : (inner + 1) * BLK, q_cols]
        first = ((step * PAIRS) + local_head * 2 + inner) * TILES
        codes = [table[first + n] for n in range(TILES)]
        places = [lax.shift_right_logical(code, 1) for code in codes]
        keys = jnp.concatenate([kv_v[place, 0] for place in places], axis=0)
        all_scores = lax.dot_general(
            q, keys, (((1,), (1,)), ((), ())), preferred_element_type=jnp.float32
        )
        scores = []
        for n in range(TILES):
            s = all_scores[:, n * BLK : (n + 1) * BLK]
            good = causal if n == 0 else (codes[n] & 1) == 1
            scores.append(jnp.where(good, s, HIDDEN))
        largest = functools.reduce(jnp.maximum, scores)
        largest = jnp.max(largest, axis=1, keepdims=True)
        weights = [jnp.exp((s - largest) * scale) for s in scores]
        totals = jnp.sum(functools.reduce(jnp.add, weights), axis=1, keepdims=True)
        values = jnp.concatenate([kv_v[place, 1] for place in places], axis=0)
        mixed = jnp.dot(
            jnp.concatenate([w.astype(jnp.bfloat16) for w in weights], axis=1),
            values,
            preferred_element_type=jnp.float32,
        )
        result = (mixed / totals).astype(jnp.bfloat16)
        for group in range(BLK // 16):
            z = inner * 4 + group // 2
            start = jnp.where(core == group % 2, 128, 0) + z * 16
            out[pl.ds(pl.multiple_of(start, 16), 16), q_cols] = result[group * 16 : group * 16 + 16]

    def one_head(local_head, carry):
        for inner in range(2):
            one_pair(local_head, inner)
        return carry

    lax.fori_loop(0, LOCAL_HEADS, one_head, 0)
    w_copy.wait()
    project_tiles(out[...], w_v, send, own, lambda n: None)


def attend(step, table, queries, weight, stores, earlier):
    shape = jax.ShapeDtypeStruct((SPAN // 2, WIDTH), jnp.bfloat16)
    return pl.pallas_call(
        functools.partial(attend_kernel, step),
        out_shape=(jax.ShapeDtypeStruct((SPAN, LOCAL_HEADS * HD), jnp.bfloat16), shape, shape),
        in_specs=[SCALARS] + [IN_HBM] * 2 + [ANYWHERE] * (len(stores) + len(earlier)),
        out_specs=(IN_VMEM, IN_VMEM, IN_VMEM),
        scratch_shapes=[
            pltpu.VMEM((SPAN, LOCAL_HEADS * HD), jnp.bfloat16),
            pltpu.VMEM(((step + 1) * 2 * SPANS, 2, BLK, HD), jnp.bfloat16),
            pltpu.VMEM((LOCAL_HEADS * HD, WIDTH), jnp.bfloat16),
            pltpu.SemaphoreType.DMA((2 + 2 * (step + 1),)),
        ],
        cost_estimate=pl.CostEstimate(
            flops=4 * PAIRS * TILES * BLK * BLK * HD, bytes_accessed=8 * MIB, transcendentals=0
        ),
        compiler_params=pltpu.CompilerParams(vmem_limit_bytes=16 * MIB),
    )(table, queries, weight, *stores, *earlier)


def project_tiles(left, weight, send, own, ready):
    def one_tile(n, carry):
        cols = pl.ds(pl.multiple_of(n * TILE, TILE), TILE)
        ready(n)
        result = jnp.dot(left, weight[:, cols], preferred_element_type=jnp.float32)
        result = result.astype(jnp.bfloat16)
        send[:, cols] = result[: SPAN // 2]
        own[:, cols] = result[SPAN // 2 :]
        return carry

    lax.fori_loop(0, WIDTH // TILE, one_tile, 0)


def project_kernel(half, attended, w_hbm, send, own, w_v, sems):
    def copy_of(n):
        cols = pl.ds(pl.multiple_of(n * TILE, TILE), TILE)
        w_cols = pl.ds(pl.multiple_of(half * WIDTH + n * TILE, TILE), TILE)
        return pltpu.make_async_copy(w_hbm.at[:, w_cols], w_v.at[:, cols], sems.at[n])

    for n in range(WIDTH // TILE):
        copy_of(n).start()
    project_tiles(attended[...], w_v, send, own, lambda n: copy_of(n).wait())


def project(half, attended, weight):
    depth = LOCAL_HEADS * HD
    shape = jax.ShapeDtypeStruct((SPAN // 2, WIDTH), jnp.bfloat16)
    return pl.pallas_call(
        functools.partial(project_kernel, half),
        out_shape=(shape, shape),
        in_specs=[IN_VMEM, IN_HBM],
        out_specs=(IN_VMEM, IN_VMEM),
        scratch_shapes=[
            pltpu.VMEM((depth, WIDTH), jnp.bfloat16),
            pltpu.SemaphoreType.DMA((WIDTH // TILE,)),
        ],
        cost_estimate=pl.CostEstimate(
            flops=2 * SPAN * depth * WIDTH, bytes_accessed=6 * MIB, transcendentals=0
        ),
        compiler_params=pltpu.CompilerParams(vmem_limit_bytes=10 * MIB),
    )(attended, weight)


def local(queries, key_rows, value_rows, out_weight, span_owner, vertical_blocks, slash_offsets):
    heads = lax.axis_size("head")
    chips = heads // 2
    head_group = lax.axis_index("head")
    core = lax.rem(head_group, 2)
    z = head_group // 2
    kv_head = head_group * LOCAL_HEADS // (QH // KVH)
    swap = core_swap(heads)

    table = make_plan(span_owner, vertical_blocks, slash_offsets)

    def own_block(rows, step):
        return lax.dynamic_slice(rows, (step, core * BLK, kv_head * HD), (1, BLK, HD))

    gathered = []
    for step in range(STEPS):
        mine = jnp.concatenate([own_block(key_rows, step), own_block(value_rows, step)])
        mine = jnp.broadcast_to(mine[None], (SPANS, 2, BLK, HD))
        if gathered:
            mine = after(mine, gathered[0])
        gathered.append(lax.all_to_all(mine, "ctx", 0, 0, tiled=True))

    def chunk(stream, offset):
        index = lax.rem(z + offset + chips, chips)
        own, other = stream
        return lax.dynamic_index_in_dim(own, index, 0, False).astype(
            jnp.float32
        ) + lax.dynamic_index_in_dim(other, index, 0, False).astype(jnp.float32)

    moving = {}
    sent = {}

    def hop(step, half, distance):
        for direction in (1, -1):
            far = chips // 2 if (direction == 1) == (half == 0) else chips // 2 - 1
            if distance > far:
                continue
            key = (step, half, direction)
            total = chunk(streams[step, half], direction * distance)
            if key in moving:
                total = total + moving[key].astype(jnp.float32)
            total = total.astype(jnp.bfloat16)
            sent[key] = total
            moving[key] = lax.ppermute(total, "head", shift_z(heads, direction))

    def sent_by(step):
        return [value for key, value in sent.items() if key[0] == step]

    stores = []
    streams = {}
    far = chips // 2

    def compute(step, earlier):
        mine = gathered[step]
        stores.extend([mine, lax.ppermute(mine, "head", swap)])
        attended, send, own = attend(step, table, queries, out_weight, stores, earlier)
        for half in range(HALVES):
            if half > 0:
                send, own = project(half, attended, out_weight)
            other = lax.ppermute(send, "head", swap)
            streams[step, half] = (
                own.reshape(chips, 16, WIDTH),
                other.reshape(chips, 16, WIDTH),
            )

    def hops(step, distance):
        for half in range(HALVES):
            hop(step, half, distance)

    compute(0, [])
    hops(0, far)
    hops(0, far - 1)
    gathered[1] = after(gathered[1], *sent_by(0))
    compute(1, [])
    hops(1, far)
    hops(0, far - 2)
    hops(0, far - 3)
    for distance in range(far - 1, 0, -1):
        hops(1, distance)

    outputs = []
    for step in range(STEPS):
        columns = []
        for half in range(HALVES):
            total = chunk(streams[step, half], 0)
            for direction in (1, -1):
                total = total + moving[step, half, direction].astype(jnp.float32)
            columns.append(total.astype(jnp.bfloat16))
        outputs.append(jnp.concatenate(columns, axis=1)[None])
    return jnp.concatenate(outputs)


def solution(mesh):
    in_specs = (
        P(None, "ctx", "head"),
        P(None, "ctx", None),
        P(None, "ctx", None),
        P("head", None),
        P(),
        P(),
        P(),
    )
    out_specs = P(None, ("ctx", "head"), None)


    return jax.shard_map(
        local, mesh=mesh, in_specs=in_specs, out_specs=out_specs, check_vma=False
    )
```

profile of v0, /device:TPU:2, one launch (start us, length us, event | category | flops | bytes accessed | tf_op | source)
XLA Modules:
  0.0 162.9 jit_solution(1519764088409878807)
XLA Ops:
  1.1 23.1 %all_to_all.10.refs_3_.refs_1_ = bf16[16,2,128,128]{3,2,1,0:T(8,128)(2,1)S(1)} all-to-all(bf16[16,2,128,128]{3,2,1,0:T(8,128)(2,1)S(1)} %broadcast_in_dim.8), channel_id=1, replica_groups=mesh['ctx'=16,'head'=16] {'ctx'}, dimensions={0} | all-to-all | bytes 2097152 | tf_op jit(solution)/shard_map/all_to_all | solution.py:263
  26.4 7.9 %plan.1.refs_0_ = s32[144]{0:T(256)S(1)} custom-call(s32[2,16]{1,0:T(2,128)S(1)} %copy-done.10, s32[64,4]{1,0:T(8,128)S(1)} %copy.10.vertical, s32[64,4]{1,0:T(8,128)S(1)} %copy.11.slash), custom_call_target="tpu_custom_call" | custom-call | tf_op jit(solution)/shard_map/plan/pallas_call | solution.py:98
  34.3 3.4 %copy-done = bf16[512,8192]{1,0:T(8,128)(2,1)S(1)} copy-done((bf16[512,8192]{1,0:T(8,128)(2,1)S(1)}, bf16[512,8192]{1,0:T(8,128)(2,1)}, u32[]{:S(2)}) %copy-start) | copy-done | bytes 8388632
  38.7 9.1 %shard_map.73 = (bf16[256,512]{1,0:T(8,128)(2,1)S(1)}, bf16[128,4096]{1,0:T(8,128)(2,1)}, bf16[128,4096]{1,0:T(8,128)(2,1)S(1)}) custom-call(s32[144]{0:T(256)S(1)} %plan.1.refs_0_, bf16[2,256,512]{2,1,0:T(8,128)(2,1)S(1)} %copy-done.4, bf16[512,8192]{1,0:T(8,128)(2,1)S(1)} %copy-done, bf16[16,2,128,128]{3,2,1,0:T(8,128)(2,1)S(1)} %all_to_all.10.refs_3_.refs_1_, ...), custom_call_target="tpu_custom_call" | custom-call | flops 603979776 | bytes 8388608 | tf_op jit(solution)/shard_map/pallas_call | solution.py:182
  48.5 4.5 %shard_map.74 = (bf16[128,4096]{1,0:T(8,128)(2,1)}, bf16[128,4096]{1,0:T(8,128)(2,1)S(1)}) custom-call(bf16[256,512]{1,0:T(8,128)(2,1)S(1)} %get-tuple-element.17.attended, bf16[512,8192]{1,0:T(8,128)(2,1)S(1)} %copy-done.1), custom_call_target="tpu_custom_call" | custom-call | flops 1073741824 | bytes 6291456 | tf_op jit(solution)/shard_map/pallas_call | solution.py:227
  55.2 4.9 %all-to-all-start.1 = ((bf16[16,2,128,128]{3,2,1,0:T(8,128)(2,1)}), bf16[16,2,128,128]{3,2,1,0:T(8,128)(2,1)S(1)}, u32[]{:S(2)}, u32[]{:S(2)}) async-start(bf16[16,2,128,128]{3,2,1,0:T(8,128)(2,1)} %after.2), calls=%async_computation.1 | async-start | bytes 2097152 | tf_op jit(solution)/shard_map/all_to_all | solution.py:263
  63.3 4.0 %collective-permute-start.6 = (bf16[16,4096]{1,0:T(8,128)(2,1)S(1)}, bf16[16,4096]{1,0:T(8,128)(2,1)}, u32[]{:S(2)}, u32[]{:S(2)}) collective-permute-start(bf16[16,4096]{1,0:T(8,128)(2,1)S(1)} %get-tuple-element.39.refs_3_), channel_id=1, source_target_pairs={{0,14},{1,15},{2,0},{3,1},{4,2},{5,3},{6,4},{7,5},{8,6},{9,7},{10,... | collective-permute-start | bytes 393224 | tf_op jit(solution)/shard_map/ppermute | solution.py:286
  68.5 3.2 %collective-permute-start.13 = (bf16[16,4096]{1,0:T(8,128)(2,1)S(1)}, bf16[16,4096]{1,0:T(8,128)(2,1)S(1)}, u32[]{:S(2)}, u32[]{:S(2)}) collective-permute-start(bf16[16,4096]{1,0:T(8,128)(2,1)S(1)} %get-tuple-element.38), channel_id=1, source_target_pairs={{0,14},{1,15},{2,0},{3,1},{4,2},{5,3},{6,4},{7,5},{8,6},{9,7},{10,... | collective-permute-start | bytes 393224 | tf_op jit(solution)/shard_map/ppermute | solution.py:286
  76.2 2.9 %collective-permute-done.3 = bf16[16,4096]{1,0:T(8,128)(2,1)S(1)} collective-permute-done((bf16[16,4096]{1,0:T(8,128)(2,1)S(1)}, bf16[16,4096]{1,0:T(8,128)(2,1)S(1)}, u32[]{:S(2)}, u32[]{:S(2)}) %collective-permute-start.3) | collective-permute-done | bytes 131104 | tf_op jit(solution)/shard_map/ppermute | solution.py:286
  88.5 2.9 %collective-permute-start.7 = (bf16[16,4096]{1,0:T(8,128)(2,1)S(1)}, bf16[16,4096]{1,0:T(8,128)(2,1)S(1)}, u32[]{:S(2)}, u32[]{:S(2)}) collective-permute-start(bf16[16,4096]{1,0:T(8,128)(2,1)S(1)} %get-tuple-element.26), channel_id=1, source_target_pairs={{0,14},{1,15},{2,0},{3,1},{4,2},{5,3},{6,4},{7,5},{8,6},{9,7},{10,... | collective-permute-start | bytes 393224 | tf_op jit(solution)/shard_map/ppermute | solution.py:286
  92.5 3.3 %collective-permute-start.15 = (bf16[16,4096]{1,0:T(8,128)(2,1)S(1)}, bf16[16,4096]{1,0:T(8,128)(2,1)S(1)}, u32[]{:S(2)}, u32[]{:S(2)}) collective-permute-start(bf16[16,4096]{1,0:T(8,128)(2,1)S(1)} %fusion.15), channel_id=1, source_target_pairs={{0,14},{1,15},{2,0},{3,1},{4,2},{5,3},{6,4},{7,5},{8,6},{9,7},{10,... | collective-permute-start | bytes 393224 | tf_op jit(solution)/shard_map/ppermute | solution.py:286
  96.8 2.8 %collective-permute-start.8 = (bf16[16,4096]{1,0:T(8,128)(2,1)S(1)}, bf16[16,4096]{1,0:T(8,128)(2,1)S(1)}, u32[]{:S(2)}, u32[]{:S(2)}) collective-permute-start(bf16[16,4096]{1,0:T(8,128)(2,1)S(1)} %fusion.22), channel_id=1, source_target_pairs={{0,14},{1,15},{2,0},{3,1},{4,2},{5,3},{6,4},{7,5},{8,6},{9,7},{10,... | collective-permute-start | bytes 393224 | tf_op jit(solution)/shard_map/ppermute | solution.py:286
  100.6 2.8 %collective-permute-start.16 = (bf16[16,4096]{1,0:T(8,128)(2,1)S(1)}, bf16[16,4096]{1,0:T(8,128)(2,1)S(1)}, u32[]{:S(2)}, u32[]{:S(2)}) collective-permute-start(bf16[16,4096]{1,0:T(8,128)(2,1)S(1)} %fusion.16), channel_id=1, source_target_pairs={{0,14},{1,15},{2,0},{3,1},{4,2},{5,3},{6,4},{7,5},{8,6},{9,7},{10,... | collective-permute-start | bytes 393224 | tf_op jit(solution)/shard_map/ppermute | solution.py:286
  104.5 3.4 %copy-done.2 = bf16[512,8192]{1,0:T(8,128)(2,1)S(1)} copy-done((bf16[512,8192]{1,0:T(8,128)(2,1)S(1)}, bf16[512,8192]{1,0:T(8,128)(2,1)}, u32[]{:S(2)}) %copy-start.2) | copy-done | bytes 8388632
  108.9 8.3 %shard_map.75 = (bf16[256,512]{1,0:T(8,128)(2,1)S(1)}, bf16[128,4096]{1,0:T(8,128)(2,1)S(1)}, bf16[128,4096]{1,0:T(8,128)(2,1)S(1)}) custom-call(s32[144]{0:T(256)S(1)} %plan.1.refs_0_, bf16[2,256,512]{2,1,0:T(8,128)(2,1)S(1)} %copy-done.5, bf16[512,8192]{1,0:T(8,128)(2,1)S(1)} %copy-done.2, bf16[16,2,128,128]{3,2,1,0:T(8,128)(2,1)S(1)} %all_to_all.10.refs_3_.refs_1_, ...), custom_call_target="tpu_custom_call" | custom-call | flops 603979776 | bytes 8388608 | tf_op jit(solution)/shard_map/pallas_call | solution.py:182
  118.5 3.4 %copy-done.3 = bf16[512,8192]{1,0:T(8,128)(2,1)S(1)} copy-done((bf16[512,8192]{1,0:T(8,128)(2,1)S(1)}, bf16[512,8192]{1,0:T(8,128)(2,1)}, u32[]{:S(2)}) %copy-start.3) | copy-done | bytes 8388632
  121.9 3.5 %shard_map.76 = (bf16[128,4096]{1,0:T(8,128)(2,1)S(1)}, bf16[128,4096]{1,0:T(8,128)(2,1)S(1)}) custom-call(bf16[256,512]{1,0:T(8,128)(2,1)S(1)} %get-tuple-element.22.attended, bf16[512,8192]{1,0:T(8,128)(2,1)S(1)} %copy-done.3), custom_call_target="tpu_custom_call" | custom-call | flops 1073741824 | bytes 6291456 | tf_op jit(solution)/shard_map/pallas_call | solution.py:227
  126.5 3.0 %collective-permute-start.23 = (bf16[16,4096]{1,0:T(8,128)(2,1)S(1)}, bf16[16,4096]{1,0:T(8,128)(2,1)S(1)}, u32[]{:S(2)}, u32[]{:S(2)}) collective-permute-start(bf16[16,4096]{1,0:T(8,128)(2,1)S(1)} %get-tuple-element.32), channel_id=1, source_target_pairs={{0,14},{1,15},{2,0},{3,1},{4,2},{5,3},{6,4},{7,5},{8,6},{9,7},{10,... | collective-permute-start | bytes 393224 | tf_op jit(solution)/shard_map/ppermute | solution.py:286
  129.6 3.2 %collective-permute-start.30 = (bf16[16,4096]{1,0:T(8,128)(2,1)S(1)}, bf16[16,4096]{1,0:T(8,128)(2,1)S(1)}, u32[]{:S(2)}, u32[]{:S(2)}) collective-permute-start(bf16[16,4096]{1,0:T(8,128)(2,1)S(1)} %get-tuple-element.36), channel_id=1, source_target_pairs={{0,14},{1,15},{2,0},{3,1},{4,2},{5,3},{6,4},{7,5},{8,6},{9,7},{10,... | collective-permute-start | bytes 393224 | tf_op jit(solution)/shard_map/ppermute | solution.py:286
  133.0 2.8 %collective-permute-done.27 = bf16[16,4096]{1,0:T(8,128)(2,1)S(1)} collective-permute-done((bf16[16,4096]{1,0:T(8,128)(2,1)S(1)}, bf16[16,4096]{1,0:T(8,128)(2,1)S(1)}, u32[]{:S(2)}, u32[]{:S(2)}) %collective-permute-start.27) | collective-permute-done | bytes 131104 | tf_op jit(solution)/shard_map/ppermute | solution.py:286
  135.9 4.4 %collective-permute-done.20 = bf16[16,4096]{1,0:T(8,128)(2,1)S(1)} collective-permute-done((bf16[16,4096]{1,0:T(8,128)(2,1)S(1)}, bf16[16,4096]{1,0:T(8,128)(2,1)S(1)}, u32[]{:S(2)}, u32[]{:S(2)}) %collective-permute-start.20) | collective-permute-done | bytes 131104 | tf_op jit(solution)/shard_map/ppermute | solution.py:286
  145.0 2.8 %collective-permute-done.21 = bf16[16,4096]{1,0:T(8,128)(2,1)S(1)} collective-permute-done((bf16[16,4096]{1,0:T(8,128)(2,1)S(1)}, bf16[16,4096]{1,0:T(8,128)(2,1)S(1)}, u32[]{:S(2)}, u32[]{:S(2)}) %collective-permute-start.21) | collective-permute-done | bytes 131104 | tf_op jit(solution)/shard_map/ppermute | solution.py:286
  151.5 2.9 %collective-permute-done.24 = bf16[16,4096]{1,0:T(8,128)(2,1)S(1)} collective-permute-done((bf16[16,4096]{1,0:T(8,128)(2,1)S(1)}, bf16[16,4096]{1,0:T(8,128)(2,1)S(1)}, u32[]{:S(2)}, u32[]{:S(2)}) %collective-permute-start.24) | collective-permute-done | bytes 131104 | tf_op jit(solution)/shard_map/ppermute | solution.py:286
  159.6 2.4 %collective-permute-done.33 = bf16[16,4096]{1,0:T(8,128)(2,1)S(1)} collective-permute-done((bf16[16,4096]{1,0:T(8,128)(2,1)S(1)}, bf16[16,4096]{1,0:T(8,128)(2,1)S(1)}, u32[]{:S(2)}, u32[]{:S(2)}) %collective-permute-start.33) | collective-permute-done | bytes 131104 | tf_op jit(solution)/shard_map/ppermute | solution.py:286
  (110 shorter events, 47.7 us)
Async XLA Ops:
  24.1 10.2 %collective-permute-start = (bf16[16,2,128,128]{3,2,1,0:T(8,128)(2,1)S(1)}, bf16[16,2,128,128]{3,2,1,0:T(8,128)(2,1)S(1)}, u32[]{:S(2)}, u32[]{:S(2)}) collective-permute-start(bf16[16,2,128,128]{3,2,1,0:T(8,128)(2,1)S(1)} %all_to_all.10.refs_3_.refs_1_), channel_id=1, source_target_pairs={{0,1},{1,0},{2,3},{3,2},{4,5},{5,4},{6,7},{7,6},{8,9},{9,8},{10,11... | collective-permute-start | bytes 3145736 | tf_op jit(solution)/shard_map/ppermute | solution.py:297
  47.9 12.2 %collective-permute-start.1 = (bf16[128,4096]{1,0:T(8,128)(2,1)}, bf16[128,4096]{1,0:T(8,128)(2,1)}, u32[]{:S(2)}, u32[]{:S(2)}) collective-permute-start(bf16[128,4096]{1,0:T(8,128)(2,1)} %get-tuple-element.16), channel_id=1, source_target_pairs={{0,1},{1,0},{2,3},{3,2},{4,5},{5,4},{6,7},{7,6},{8,9},{9,8},{10,11... | collective-permute-start | bytes 3145736 | tf_op jit(solution)/shard_map/ppermute | solution.py:302
  53.9 13.3 %collective-permute-start.9 = (bf16[128,4096]{1,0:T(8,128)(2,1)}, bf16[128,4096]{1,0:T(8,128)(2,1)}, u32[]{:S(2)}, u32[]{:S(2)}) collective-permute-start(bf16[128,4096]{1,0:T(8,128)(2,1)} %get-tuple-element.19), channel_id=1, source_target_pairs={{0,1},{1,0},{2,3},{3,2},{4,5},{5,4},{6,7},{7,6},{8,9},{9,8},{10,11... | collective-permute-start | bytes 3145736 | tf_op jit(solution)/shard_map/ppermute | solution.py:302
  55.2 31.1 %all-to-all-start.1 = ((bf16[16,2,128,128]{3,2,1,0:T(8,128)(2,1)}), bf16[16,2,128,128]{3,2,1,0:T(8,128)(2,1)S(1)}, u32[]{:S(2)}, u32[]{:S(2)}) async-start(bf16[16,2,128,128]{3,2,1,0:T(8,128)(2,1)} %after.2), calls=%async_computation.1 | async-start | bytes 2097152 | tf_op jit(solution)/shard_map/all_to_all | solution.py:263
  61.3 10.5 %collective-permute-start.2 = (bf16[16,4096]{1,0:T(8,128)(2,1)S(1)}, bf16[16,4096]{1,0:T(8,128)(2,1)S(1)}, u32[]{:S(2)}, u32[]{:S(2)}) collective-permute-start(bf16[16,4096]{1,0:T(8,128)(2,1)S(1)} %get-tuple-element.40), channel_id=1, source_target_pairs={{0,2},{1,3},{2,4},{3,5},{4,6},{5,7},{6,8},{7,9},{8,10},{9,11},{10,... | collective-permute-start | bytes 393224 | tf_op jit(solution)/shard_map/ppermute | solution.py:286
  63.3 23.9 %collective-permute-start.6 = (bf16[16,4096]{1,0:T(8,128)(2,1)S(1)}, bf16[16,4096]{1,0:T(8,128)(2,1)}, u32[]{:S(2)}, u32[]{:S(2)}) collective-permute-start(bf16[16,4096]{1,0:T(8,128)(2,1)S(1)} %get-tuple-element.39.refs_3_), channel_id=1, source_target_pairs={{0,14},{1,15},{2,0},{3,1},{4,2},{5,3},{6,4},{7,5},{8,6},{9,7},{10,... | collective-permute-start | bytes 393224 | tf_op jit(solution)/shard_map/ppermute | solution.py:286
  68.5 12.2 %collective-permute-start.13 = (bf16[16,4096]{1,0:T(8,128)(2,1)S(1)}, bf16[16,4096]{1,0:T(8,128)(2,1)S(1)}, u32[]{:S(2)}, u32[]{:S(2)}) collective-permute-start(bf16[16,4096]{1,0:T(8,128)(2,1)S(1)} %get-tuple-element.38), channel_id=1, source_target_pairs={{0,14},{1,15},{2,0},{3,1},{4,2},{5,3},{6,4},{7,5},{8,6},{9,7},{10,... | collective-permute-start | bytes 393224 | tf_op jit(solution)/shard_map/ppermute | solution.py:286
  84.2 7.2 %collective-permute-start.14 = (bf16[16,4096]{1,0:T(8,128)(2,1)S(1)}, bf16[16,4096]{1,0:T(8,128)(2,1)}, u32[]{:S(2)}, u32[]{:S(2)}) collective-permute-start(bf16[16,4096]{1,0:T(8,128)(2,1)S(1)} %get-tuple-element.28.refs_2_), channel_id=1, source_target_pairs={{0,14},{1,15},{2,0},{3,1},{4,2},{5,3},{6,4},{7,5},{8,6},{9,7},{10,... | collective-permute-start | bytes 393224 | tf_op jit(solution)/shard_map/ppermute | solution.py:286
  85.9 31.5 %collective-permute-start.12 = (bf16[16,4096]{1,0:T(8,128)(2,1)}, bf16[16,4096]{1,0:T(8,128)(2,1)}, u32[]{:S(2)}, u32[]{:S(2)}) collective-permute-start(bf16[16,4096]{1,0:T(8,128)(2,1)} %get-tuple-element.27), channel_id=1, source_target_pairs={{0,2},{1,3},{2,4},{3,5},{4,6},{5,7},{6,8},{7,9},{8,10},{9,11},{10,... | collective-permute-start | bytes 393224 | tf_op jit(solution)/shard_map/ppermute | solution.py:286
  87.1 17.4 %collective-permute-start.17 = (bf16[16,2,128,128]{3,2,1,0:T(8,128)(2,1)S(1)}, bf16[16,2,128,128]{3,2,1,0:T(8,128)(2,1)S(1)}, u32[]{:S(2)}, u32[]{:S(2)}) collective-permute-start(bf16[16,2,128,128]{3,2,1,0:T(8,128)(2,1)S(1)} %after.3.refs_5_), channel_id=1, source_target_pairs={{0,1},{1,0},{2,3},{3,2},{4,5},{5,4},{6,7},{7,6},{8,9},{9,8},{10,11... | collective-permute-start | bytes 3145736 | tf_op jit(solution)/shard_map/ppermute | solution.py:297
  88.5 7.3 %collective-permute-start.7 = (bf16[16,4096]{1,0:T(8,128)(2,1)S(1)}, bf16[16,4096]{1,0:T(8,128)(2,1)S(1)}, u32[]{:S(2)}, u32[]{:S(2)}) collective-permute-start(bf16[16,4096]{1,0:T(8,128)(2,1)S(1)} %get-tuple-element.26), channel_id=1, source_target_pairs={{0,14},{1,15},{2,0},{3,1},{4,2},{5,3},{6,4},{7,5},{8,6},{9,7},{10,... | collective-permute-start | bytes 393224 | tf_op jit(solution)/shard_map/ppermute | solution.py:286
  91.4 12.1 %collective-permute-start.5 = (bf16[16,4096]{1,0:T(8,128)(2,1)S(1)}, bf16[16,4096]{1,0:T(8,128)(2,1)S(1)}, u32[]{:S(2)}, u32[]{:S(2)}) collective-permute-start(bf16[16,4096]{1,0:T(8,128)(2,1)S(1)} %get-tuple-element.25), channel_id=1, source_target_pairs={{0,2},{1,3},{2,4},{3,5},{4,6},{5,7},{6,8},{7,9},{8,10},{9,11},{10,... | collective-permute-start | bytes 393224 | tf_op jit(solution)/shard_map/ppermute | solution.py:286
  92.5 7.1 %collective-permute-start.15 = (bf16[16,4096]{1,0:T(8,128)(2,1)S(1)}, bf16[16,4096]{1,0:T(8,128)(2,1)S(1)}, u32[]{:S(2)}, u32[]{:S(2)}) collective-permute-start(bf16[16,4096]{1,0:T(8,128)(2,1)S(1)} %fusion.15), channel_id=1, source_target_pairs={{0,14},{1,15},{2,0},{3,1},{4,2},{5,3},{6,4},{7,5},{8,6},{9,7},{10,... | collective-permute-start | bytes 393224 | tf_op jit(solution)/shard_map/ppermute | solution.py:286
  100.6 16.7 %collective-permute-start.16 = (bf16[16,4096]{1,0:T(8,128)(2,1)S(1)}, bf16[16,4096]{1,0:T(8,128)(2,1)S(1)}, u32[]{:S(2)}, u32[]{:S(2)}) collective-permute-start(bf16[16,4096]{1,0:T(8,128)(2,1)S(1)} %fusion.16), channel_id=1, source_target_pairs={{0,14},{1,15},{2,0},{3,1},{4,2},{5,3},{6,4},{7,5},{8,6},{9,7},{10,... | collective-permute-start | bytes 393224 | tf_op jit(solution)/shard_map/ppermute | solution.py:286
  117.3 8.8 %collective-permute-start.18 = (bf16[128,4096]{1,0:T(8,128)(2,1)S(1)}, bf16[128,4096]{1,0:T(8,128)(2,1)S(1)}, u32[]{:S(2)}, u32[]{:S(2)}) collective-permute-start(bf16[128,4096]{1,0:T(8,128)(2,1)S(1)} %get-tuple-element.21), channel_id=1, source_target_pairs={{0,1},{1,0},{2,3},{3,2},{4,5},{5,4},{6,7},{7,6},{8,9},{9,8},{10,11... | collective-permute-start | bytes 3145736 | tf_op jit(solution)/shard_map/ppermute | solution.py:302
  126.5 18.5 %collective-permute-start.23 = (bf16[16,4096]{1,0:T(8,128)(2,1)S(1)}, bf16[16,4096]{1,0:T(8,128)(2,1)S(1)}, u32[]{:S(2)}, u32[]{:S(2)}) collective-permute-start(bf16[16,4096]{1,0:T(8,128)(2,1)S(1)} %get-tuple-element.32), channel_id=1, source_target_pairs={{0,14},{1,15},{2,0},{3,1},{4,2},{5,3},{6,4},{7,5},{8,6},{9,7},{10,... | collective-permute-start | bytes 393224 | tf_op jit(solution)/shard_map/ppermute | solution.py:286
  129.6 11.1 %collective-permute-start.30 = (bf16[16,4096]{1,0:T(8,128)(2,1)S(1)}, bf16[16,4096]{1,0:T(8,128)(2,1)S(1)}, u32[]{:S(2)}, u32[]{:S(2)}) collective-permute-start(bf16[16,4096]{1,0:T(8,128)(2,1)S(1)} %get-tuple-element.36), channel_id=1, source_target_pairs={{0,14},{1,15},{2,0},{3,1},{4,2},{5,3},{6,4},{7,5},{8,6},{9,7},{10,... | collective-permute-start | bytes 393224 | tf_op jit(solution)/shard_map/ppermute | solution.py:286
  132.9 7.4 %collective-permute-start.20 = (bf16[16,4096]{1,0:T(8,128)(2,1)S(1)}, bf16[16,4096]{1,0:T(8,128)(2,1)S(1)}, u32[]{:S(2)}, u32[]{:S(2)}) collective-permute-start(bf16[16,4096]{1,0:T(8,128)(2,1)S(1)} %fusion.9), channel_id=1, source_target_pairs={{0,2},{1,3},{2,4},{3,5},{4,6},{5,7},{6,8},{7,9},{8,10},{9,11},{10,... | collective-permute-start | bytes 393224 | tf_op jit(solution)/shard_map/ppermute | solution.py:286
  135.8 7.0 %collective-permute-start.28 = (bf16[16,4096]{1,0:T(8,128)(2,1)S(1)}, bf16[16,4096]{1,0:T(8,128)(2,1)S(1)}, u32[]{:S(2)}, u32[]{:S(2)}) collective-permute-start(bf16[16,4096]{1,0:T(8,128)(2,1)S(1)} %fusion.3), channel_id=1, source_target_pairs={{0,2},{1,3},{2,4},{3,5},{4,6},{5,7},{6,8},{7,9},{8,10},{9,11},{10,... | collective-permute-start | bytes 393224 | tf_op jit(solution)/shard_map/ppermute | solution.py:286
  140.3 7.5 %collective-permute-start.21 = (bf16[16,4096]{1,0:T(8,128)(2,1)S(1)}, bf16[16,4096]{1,0:T(8,128)(2,1)S(1)}, u32[]{:S(2)}, u32[]{:S(2)}) collective-permute-start(bf16[16,4096]{1,0:T(8,128)(2,1)S(1)} %fusion.10), channel_id=1, source_target_pairs={{0,2},{1,3},{2,4},{3,5},{4,6},{5,7},{6,8},{7,9},{8,10},{9,11},{10,... | collective-permute-start | bytes 393224 | tf_op jit(solution)/shard_map/ppermute | solution.py:286
  142.9 7.1 %collective-permute-start.31 = (bf16[16,4096]{1,0:T(8,128)(2,1)S(1)}, bf16[16,4096]{1,0:T(8,128)(2,1)S(1)}, u32[]{:S(2)}, u32[]{:S(2)}) collective-permute-start(bf16[16,4096]{1,0:T(8,128)(2,1)S(1)} %get-tuple-element.34), channel_id=1, source_target_pairs={{0,14},{1,15},{2,0},{3,1},{4,2},{5,3},{6,4},{7,5},{8,6},{9,7},{10,... | collective-permute-start | bytes 393224 | tf_op jit(solution)/shard_map/ppermute | solution.py:286
  144.1 15.5 %collective-permute-start.29 = (bf16[16,4096]{1,0:T(8,128)(2,1)S(1)}, bf16[16,4096]{1,0:T(8,128)(2,1)S(1)}, u32[]{:S(2)}, u32[]{:S(2)}) collective-permute-start(bf16[16,4096]{1,0:T(8,128)(2,1)S(1)} %get-tuple-element.33), channel_id=1, source_target_pairs={{0,2},{1,3},{2,4},{3,5},{4,6},{5,7},{6,8},{7,9},{8,10},{9,11},{10,... | collective-permute-start | bytes 393224 | tf_op jit(solution)/shard_map/ppermute | solution.py:286
  148.0 11.1 %collective-permute-start.22 = (bf16[16,4096]{1,0:T(8,128)(2,1)S(1)}, bf16[16,4096]{1,0:T(8,128)(2,1)S(1)}, u32[]{:S(2)}, u32[]{:S(2)}) collective-permute-start(bf16[16,4096]{1,0:T(8,128)(2,1)S(1)} %get-tuple-element.29), channel_id=1, source_target_pairs={{0,2},{1,3},{2,4},{3,5},{4,6},{5,7},{6,8},{7,9},{8,10},{9,11},{10,... | collective-permute-start | bytes 393224 | tf_op jit(solution)/shard_map/ppermute | solution.py:286
  150.1 6.8 %collective-permute-start.32 = (bf16[16,4096]{1,0:T(8,128)(2,1)S(1)}, bf16[16,4096]{1,0:T(8,128)(2,1)S(1)}, u32[]{:S(2)}, u32[]{:S(2)}) collective-permute-start(bf16[16,4096]{1,0:T(8,128)(2,1)S(1)} %fusion.1), channel_id=1, source_target_pairs={{0,14},{1,15},{2,0},{3,1},{4,2},{5,3},{6,4},{7,5},{8,6},{9,7},{10,... | collective-permute-start | bytes 393224 | tf_op jit(solution)/shard_map/ppermute | solution.py:286
  (22 other events, 107.7 us)
where the time goes:
time: 165 us; the launch traced here: 163 us
  starting transfers between devices  44.4 us (27%)
  Pallas kernels  33.4 us (20%)
  waiting for transfers between devices  27 us (16%)
  blocking collectives  23.1 us (14%)
  local copies, waits for them, and re-layouts  18.6 us (11%)
  other arithmetic  16.2 us (10%)
    ppermute x28, starting transfers between devices, hop(): moving[key] = lax.ppermute(total, 'head', shift_z(heads, direction))  38.2 us
    ppermute x28, waiting for transfers between devices, hop(): moving[key] = lax.ppermute(total, 'head', shift_z(heads, direction))  26.9 us
    all_to_all x1, blocking collectives, local(): gathered.append(lax.all_to_all(mine, 'ctx', 0, 0, tiled=True))  23.1 us
    pallas_call x2, Pallas kernels, attend(): pl.pallas_call(functools.partial(attend_kernel, step), out_shape=(jax.Sha...  17.4 us
    unnamed x24, local copies, waits for them, and re-layouts  16.3 us
    convert_element_type x20, other arithmetic, hop(): total = total.astype(jnp.bfloat16)  13 us
    pallas_call x2, Pallas kernels, project(): pl.pallas_call(functools.partial(project_kernel, half), out_shape=(shape,...  8.05 us
    pallas_call x1, Pallas kernels, make_plan(): pl.pallas_call(plan_kernel, out_shape=jax.ShapeDtypeStruct((STEPS * PAIRS...  7.92 us
  transfers between devices with their start and end apart: 35, of which 12 were waited for; matrix products, arithmetic and copies ran while one was open for 11% of the time, Pallas kernels for 15%

commit v1 on v0

--- a/solution.py
+++ b/solution.py
@@ -27,6 +27,7 @@
 PAIRS = LOCAL_HEADS * 2
 HIDDEN = -1e30
 MIB = 1 << 20
+GRANT = 56 * MIB
 
 
 ANYWHERE = pl.BlockSpec(memory_space=pl.ANY)
@@ -42,18 +43,6 @@
 def shift_z(heads, amount):
     chips = heads // 2
     return [(h, ((h // 2 + amount) % chips) * 2 + h % 2) for h in range(heads)]
-
-
-def after(x, *earlier):
-    return pl.pallas_call(
-        lambda *refs: None,
-        out_shape=jax.ShapeDtypeStruct(x.shape, x.dtype),
-        in_specs=[ANYWHERE] * (1 + len(earlier)),
-        out_specs=ANYWHERE,
-        input_output_aliases={0: 0},
-        compiler_params=pltpu.CompilerParams(vmem_limit_bytes=MIB),
-        name="after",
-    )(x, *earlier)
 
 
 def plan_kernel(owner, vertical, slash, table):
@@ -193,7 +182,7 @@
         cost_estimate=pl.CostEstimate(
             flops=4 * PAIRS * TILES * BLK * BLK * HD, bytes_accessed=8 * MIB, transcendentals=0
         ),
-        compiler_params=pltpu.CompilerParams(vmem_limit_bytes=16 * MIB),
+        compiler_params=pltpu.CompilerParams(vmem_limit_bytes=GRANT),
     )(table, queries, weight, *stores, *earlier)
 
 
@@ -236,8 +225,28 @@
         cost_estimate=pl.CostEstimate(
             flops=2 * SPAN * depth * WIDTH, bytes_accessed=6 * MIB, transcendentals=0
         ),
-        compiler_params=pltpu.CompilerParams(vmem_limit_bytes=10 * MIB),
+        compiler_params=pltpu.CompilerParams(vmem_limit_bytes=GRANT),
     )(attended, weight)
+
+
+def pair_sums(own, other, chips):
+    def kernel(own_ref, other_ref, *outs):
+        z = lax.axis_index("head") // 2
+        for offset in range(chips):
+            index = lax.rem(z + offset, chips)
+            total = own_ref[index].astype(jnp.float32) + other_ref[index].astype(jnp.float32)
+            outs[offset][...] = total.astype(jnp.bfloat16)
+
+    rows = own.shape[0] // chips
+    shape = (chips, rows, own.shape[1])
+    return pl.pallas_call(
+        kernel,
+        out_shape=[jax.ShapeDtypeStruct(shape[1:], own.dtype)] * chips,
+        in_specs=[IN_VMEM] * 2,
+        out_specs=[IN_VMEM] * chips,
+        cost_estimate=pl.CostEstimate(flops=0, bytes_accessed=3 * MIB, transcendentals=0),
+        compiler_params=pltpu.CompilerParams(vmem_limit_bytes=8 * MIB),
+    )(own.reshape(shape), other.reshape(shape))
 
 
 def local(queries, key_rows, value_rows, out_weight, span_owner, vertical_blocks, slash_offsets):
@@ -245,7 +254,6 @@
     chips = heads // 2
     head_group = lax.axis_index("head")
     core = lax.rem(head_group, 2)
-    z = head_group // 2
     kv_head = head_group * LOCAL_HEADS // (QH // KVH)
     swap = core_swap(heads)
 
@@ -258,19 +266,9 @@
     for step in range(STEPS):
         mine = jnp.concatenate([own_block(key_rows, step), own_block(value_rows, step)])
         mine = jnp.broadcast_to(mine[None], (SPANS, 2, BLK, HD))
-        if gathered:
-            mine = after(mine, gathered[0])
         gathered.append(lax.all_to_all(mine, "ctx", 0, 0, tiled=True))
 
-    def chunk(stream, offset):
-        index = lax.rem(z + offset + chips, chips)
-        own, other = stream
-        return lax.dynamic_index_in_dim(own, index, 0, False).astype(
-            jnp.float32
-        ) + lax.dynamic_index_in_dim(other, index, 0, False).astype(jnp.float32)
-
     moving = {}
-    sent = {}
 
     def hop(step, half, distance):
         for direction in (1, -1):
@@ -278,15 +276,11 @@
             if distance > far:
                 continue
             key = (step, half, direction)
-            total = chunk(streams[step, half], direction * distance)
+            total = streams[step, half][(direction * distance) % chips]
             if key in moving:
-                total = total + moving[key].astype(jnp.float32)
+                total = total.astype(jnp.float32) + moving[key].astype(jnp.float32)
             total = total.astype(jnp.bfloat16)
-            sent[key] = total
             moving[key] = lax.ppermute(total, "head", shift_z(heads, direction))
-
-    def sent_by(step):
-        return [value for key, value in sent.items() if key[0] == step]
 
     stores = []
     streams = {}
@@ -300,10 +294,7 @@
             if half > 0:
                 send, own = project(half, attended, out_weight)
             other = lax.ppermute(send, "head", swap)
-            streams[step, half] = (
-                own.reshape(chips, 16, WIDTH),
-                other.reshape(chips, 16, WIDTH),
-            )
+            streams[step, half] = pair_sums(own, other, chips)
 
     def hops(step, distance):
         for half in range(HALVES):
@@ -312,7 +303,6 @@
     compute(0, [])
     hops(0, far)
     hops(0, far - 1)
-    gathered[1] = after(gathered[1], *sent_by(0))
     compute(1, [])
     hops(1, far)
     hops(0, far - 2)
@@ -324,7 +314,7 @@
     for step in range(STEPS):
         columns = []
         for half in range(HALVES):
-            total = chunk(streams[step, half], 0)
+            total = streams[step, half][0].astype(jnp.float32)
             for direction in (1, -1):
                 total = total + moving[step, half, direction].astype(jnp.float32)
             columns.append(total.astype(jnp.bfloat16))
@@ -345,6 +335,4 @@
     out_specs = P(None, ("ctx", "head"), None)
 
 
-    return jax.shard_map(
-        local, mesh=mesh, in_specs=in_specs, out_specs=out_specs, check_vma=False
-    )
+    return jax.shard_map(local, mesh=mesh, in_specs=in_specs, out_specs=out_specs, check_vma=False)

time: 165 us -> 162 us (0.982)
  blocking collectives: 23.1 us -> 0 us
  starting transfers between devices: 44.4 us -> 63.9 us
  waiting for transfers between devices: 27 us -> 44.5 us
  other arithmetic: 16.2 us -> 1.79 us
  local copies, waits for them, and re-layouts: 18.6 us -> 8.35 us
  Pallas kernels: 33.4 us -> 41.5 us
    all_to_all x1 -> x2, waiting for transfers between devices: 0.01 us -> 30.5 us  [local(): gathered.append(lax.all_to_all(mine, 'ctx', 0, 0, tiled=True))]
    all_to_all x1 -> x0, blocking collectives: 23.1 us -> none  [local(): gathered.append(lax.all_to_all(mine, 'ctx', 0, 0, tiled=True))]
    ppermute x28, waiting for transfers between devices: 26.9 us -> 13.9 us  [hop(): moving[key] = lax.ppermute(total, 'head', shift_z(heads, direction))]
    convert_element_type x20, other arithmetic: 13 us -> 0.68 us  [hop(): total = total.astype(jnp.bfloat16)]
    unnamed x24 -> x18, local copies, waits for them, and re-layouts: 16.3 us -> 5 us
    ppermute x28, starting transfers between devices: 38.2 us -> 48.9 us  [hop(): moving[key] = lax.ppermute(total, 'head', shift_z(heads, direction))]
    all_to_all x1 -> x2, starting transfers between devices: 4.9 us -> 13.5 us  [local(): gathered.append(lax.all_to_all(mine, 'ctx', 0, 0, tiled=True))]
    pallas_call x2, Pallas kernels: 8.05 us -> 11.9 us  [project(): pl.pallas_call(functools.partial(project_kernel, half), out_shape=(shape,...]
  transfers between devices with their start and end apart: 35 -> 36, of which waited for: 12 -> 9; matrix products, arithmetic and copies ran while one was open for 11% -> 1% of each run, Pallas kernels for 15% -> 26%
where the time goes in v1:
time: 162 us; the launch traced here: 161 us
  starting transfers between devices  63.9 us (39%)
  waiting for transfers between devices  44.5 us (27%)
  Pallas kernels  41.5 us (26%)
  local copies, waits for them, and re-layouts  8.35 us (5%)
  other arithmetic  1.79 us (1%)
    ppermute x28, starting transfers between devices, hop(): moving[key] = lax.ppermute(total, 'head', shift_z(heads, direction))  48.9 us
    all_to_all x2, waiting for transfers between devices, local(): gathered.append(lax.all_to_all(mine, 'ctx', 0, 0, tiled=True))  30.5 us
    pallas_call x2, Pallas kernels, attend(): pl.pallas_call(functools.partial(attend_kernel, step), out_shape=(jax.Sha...  20.7 us
    ppermute x28, waiting for transfers between devices, hop(): moving[key] = lax.ppermute(total, 'head', shift_z(heads, direction))  13.9 us
    all_to_all x2, starting transfers between devices, local(): gathered.append(lax.all_to_all(mine, 'ctx', 0, 0, tiled=True))  13.5 us
    pallas_call x2, Pallas kernels, project(): pl.pallas_call(functools.partial(project_kernel, half), out_shape=(shape,...  11.9 us
    pallas_call x1, Pallas kernels, make_plan(): pl.pallas_call(plan_kernel, out_shape=jax.ShapeDtypeStruct((STEPS * PAIRS...  7.92 us
    unnamed x18, local copies, waits for them, and re-layouts  5 us
  transfers between devices with their start and end apart: 36, of which 9 were waited for; matrix products, arithmetic and copies ran while one was open for 1% of the time, Pallas kernels for 26%

profile of v1, /device:TPU:2, one launch (start us, length us, event | category | flops | bytes accessed | tf_op | source)
XLA Modules:
  0.0 160.5 jit_solution(8492962382076414110)
XLA Ops:
  2.1 7.5 %all-to-all-start = ((bf16[16,2,128,128]{3,2,1,0:T(8,128)(2,1)}), bf16[16,2,128,128]{3,2,1,0:T(8,128)(2,1)S(1)}, u32[]{:S(2)}, u32[]{:S(2)}) async-start(bf16[16,2,128,128]{3,2,1,0:T(8,128)(2,1)} %broadcast_in_dim.8), calls=%async_computation | async-start | bytes 2097152 | tf_op jit(solution)/shard_map/all_to_all | solution.py:269
  9.6 15.8 %all-to-all-done.refs_3_ = bf16[16,2,128,128]{3,2,1,0:T(8,128)(2,1)S(1)} async-done(((bf16[16,2,128,128]{3,2,1,0:T(8,128)(2,1)}), bf16[16,2,128,128]{3,2,1,0:T(8,128)(2,1)S(1)}, u32[]{:S(2)}, u32[]{:S(2)}) %all-to-all-start) | async-done | bytes 1048608 | tf_op jit(solution)/shard_map/all_to_all | solution.py:269
  26.6 6.0 %all-to-all-start.1 = ((bf16[16,2,128,128]{3,2,1,0:T(8,128)(2,1)}), bf16[16,2,128,128]{3,2,1,0:T(8,128)(2,1)}, u32[]{:S(2)}, u32[]{:S(2)}) async-start(bf16[16,2,128,128]{3,2,1,0:T(8,128)(2,1)} %broadcast_in_dim.20), calls=%async_computation.1 | async-start | bytes 2097152 | tf_op jit(solution)/shard_map/all_to_all | solution.py:269
  32.7 14.7 %all-to-all-done.1.refs_5_ = bf16[16,2,128,128]{3,2,1,0:T(8,128)(2,1)} async-done(((bf16[16,2,128,128]{3,2,1,0:T(8,128)(2,1)}), bf16[16,2,128,128]{3,2,1,0:T(8,128)(2,1)}, u32[]{:S(2)}, u32[]{:S(2)}) %all-to-all-start.1) | async-done | bytes 1048608 | tf_op jit(solution)/shard_map/all_to_all | solution.py:269
  49.7 7.9 %plan.1.refs_0_ = s32[144]{0:T(256)S(1)} custom-call(s32[2,16]{1,0:T(2,128)S(1)} %copy-done.5, s32[64,4]{1,0:T(8,128)S(1)} %copy.8.vertical, s32[64,4]{1,0:T(8,128)S(1)} %copy.9.slash), custom_call_target="tpu_custom_call" | custom-call | tf_op jit(solution)/shard_map/plan/pallas_call | solution.py:87
  59.1 10.1 %shard_map.73 = (bf16[256,512]{1,0:T(8,128)(2,1)}, bf16[128,4096]{1,0:T(8,128)(2,1)}, bf16[128,4096]{1,0:T(8,128)(2,1)}) custom-call(s32[144]{0:T(256)} %copy-done.4, bf16[2,256,512]{2,1,0:T(8,128)(2,1)} %refs_1_.3, bf16[512,8192]{1,0:T(8,128)(2,1)} %w_hbm.3, bf16[16,2,128,128]{3,2,1,0:T(8,128)(2,1)} %copy-done.6, bf16[16,2,128,128]{3,2,1,0:T(8,128)(2,1)} %copy-done.7), custom_call_target="tpu_custom_call" | custom-call | flops 603979776 | bytes 8388608 | tf_op jit(solution)/shard_map/pallas_call | solution.py:171
  69.8 10.7 %shard_map.77 = (bf16[256,512]{1,0:T(8,128)(2,1)}, bf16[128,4096]{1,0:T(8,128)(2,1)}, bf16[128,4096]{1,0:T(8,128)(2,1)}) custom-call(s32[144]{0:T(256)} %copy-done.4, bf16[2,256,512]{2,1,0:T(8,128)(2,1)} %refs_1_.3, bf16[512,8192]{1,0:T(8,128)(2,1)} %w_hbm.3, bf16[16,2,128,128]{3,2,1,0:T(8,128)(2,1)} %copy-done.6, bf16[16,2,128,128]{3,2,1,0:T(8,128)(2,1)} %copy-done.7, ...), custom_call_target="tpu_custom_call" | custom-call | flops 603979776 | bytes 8388608 | tf_op jit(solution)/shard_map/pallas_call | solution.py:171
  80.6 6.0 %shard_map.75 = (bf16[128,4096]{1,0:T(8,128)(2,1)}, bf16[128,4096]{1,0:T(8,128)(2,1)}) custom-call(bf16[256,512]{1,0:T(8,128)(2,1)} %get-tuple-element.57.attended, bf16[512,8192]{1,0:T(8,128)(2,1)} %w_hbm.3), custom_call_target="tpu_custom_call" | custom-call | flops 1073741824 | bytes 6291456 | tf_op jit(solution)/shard_map/pallas_call | solution.py:216
  87.2 5.9 %shard_map.79 = (bf16[128,4096]{1,0:T(8,128)(2,1)}, bf16[128,4096]{1,0:T(8,128)(2,1)}) custom-call(bf16[256,512]{1,0:T(8,128)(2,1)} %get-tuple-element.78.attended, bf16[512,8192]{1,0:T(8,128)(2,1)} %w_hbm.3), custom_call_target="tpu_custom_call" | custom-call | flops 1073741824 | bytes 6291456 | tf_op jit(solution)/shard_map/pallas_call | solution.py:216
  95.5 4.0 %collective-permute-start.6 = (bf16[16,4096]{1,0:T(8,128)(2,1)S(1)}, bf16[16,4096]{1,0:T(8,128)(2,1)S(1)}, u32[]{:S(2)}, u32[]{:S(2)}) collective-permute-start(bf16[16,4096]{1,0:T(8,128)(2,1)S(1)} %get-tuple-element.56), channel_id=1, source_target_pairs={{0,14},{1,15},{2,0},{3,1},{4,2},{5,3},{6,4},{7,5},{8,6},{9,7},{10,... | collective-permute-start | bytes 393224 | tf_op jit(solution)/shard_map/ppermute | solution.py:283
  99.9 3.2 %collective-permute-start.23 = (bf16[16,4096]{1,0:T(8,128)(2,1)S(1)}, bf16[16,4096]{1,0:T(8,128)(2,1)S(1)}, u32[]{:S(2)}, u32[]{:S(2)}) collective-permute-start(bf16[16,4096]{1,0:T(8,128)(2,1)S(1)} %get-tuple-element.77), channel_id=1, source_target_pairs={{0,14},{1,15},{2,0},{3,1},{4,2},{5,3},{6,4},{7,5},{8,6},{9,7},{10,... | collective-permute-start | bytes 393224 | tf_op jit(solution)/shard_map/ppermute | solution.py:283
  104.9 3.5 %collective-permute-start.13 = (bf16[16,4096]{1,0:T(8,128)(2,1)S(1)}, bf16[16,4096]{1,0:T(8,128)(2,1)S(1)}, u32[]{:S(2)}, u32[]{:S(2)}) collective-permute-start(bf16[16,4096]{1,0:T(8,128)(2,1)S(1)} %get-tuple-element.67), channel_id=1, source_target_pairs={{0,14},{1,15},{2,0},{3,1},{4,2},{5,3},{6,4},{7,5},{8,6},{9,7},{10,... | collective-permute-start | bytes 393224 | tf_op jit(solution)/shard_map/ppermute | solution.py:283
  108.6 3.3 %collective-permute-start.30 = (bf16[16,4096]{1,0:T(8,128)(2,1)S(1)}, bf16[16,4096]{1,0:T(8,128)(2,1)S(1)}, u32[]{:S(2)}, u32[]{:S(2)}) collective-permute-start(bf16[16,4096]{1,0:T(8,128)(2,1)S(1)} %get-tuple-element.88), channel_id=1, source_target_pairs={{0,14},{1,15},{2,0},{3,1},{4,2},{5,3},{6,4},{7,5},{8,6},{9,7},{10,... | collective-permute-start | bytes 393224 | tf_op jit(solution)/shard_map/ppermute | solution.py:283
  112.1 3.3 %collective-permute-start.7 = (bf16[16,4096]{1,0:T(8,128)(2,1)S(1)}, bf16[16,4096]{1,0:T(8,128)(2,1)S(1)}, u32[]{:S(2)}, u32[]{:S(2)}) collective-permute-start(bf16[16,4096]{1,0:T(8,128)(2,1)S(1)} %add_convert_fusion.20), channel_id=1, source_target_pairs={{0,14},{1,15},{2,0},{3,1},{4,2},{5,3},{6,4},{7,5},{8,6},{9,7},{10,... | collective-permute-start | bytes 393224 | tf_op jit(solution)/shard_map/ppermute | solution.py:283
  115.6 3.3 %collective-permute-start.24 = (bf16[16,4096]{1,0:T(8,128)(2,1)S(1)}, bf16[16,4096]{1,0:T(8,128)(2,1)S(1)}, u32[]{:S(2)}, u32[]{:S(2)}) collective-permute-start(bf16[16,4096]{1,0:T(8,128)(2,1)S(1)} %add_convert_fusion.8), channel_id=1, source_target_pairs={{0,14},{1,15},{2,0},{3,1},{4,2},{5,3},{6,4},{7,5},{8,6},{9,7},{10,... | collective-permute-start | bytes 393224 | tf_op jit(solution)/shard_map/ppermute | solution.py:283
  119.2 3.2 %collective-permute-start.14 = (bf16[16,4096]{1,0:T(8,128)(2,1)S(1)}, bf16[16,4096]{1,0:T(8,128)(2,1)S(1)}, u32[]{:S(2)}, u32[]{:S(2)}) collective-permute-start(bf16[16,4096]{1,0:T(8,128)(2,1)S(1)} %add_convert_fusion.15), channel_id=1, source_target_pairs={{0,14},{1,15},{2,0},{3,1},{4,2},{5,3},{6,4},{7,5},{8,6},{9,7},{10,... | collective-permute-start | bytes 393224 | tf_op jit(solution)/shard_map/ppermute | solution.py:283
  122.9 2.9 %collective-permute-start.31 = (bf16[16,4096]{1,0:T(8,128)(2,1)S(1)}, bf16[16,4096]{1,0:T(8,128)(2,1)S(1)}, u32[]{:S(2)}, u32[]{:S(2)}) collective-permute-start(bf16[16,4096]{1,0:T(8,128)(2,1)S(1)} %add_convert_fusion.3), channel_id=1, source_target_pairs={{0,14},{1,15},{2,0},{3,1},{4,2},{5,3},{6,4},{7,5},{8,6},{9,7},{10,... | collective-permute-start | bytes 393224 | tf_op jit(solution)/shard_map/ppermute | solution.py:283
  126.0 3.3 %collective-permute-start.8 = (bf16[16,4096]{1,0:T(8,128)(2,1)S(1)}, bf16[16,4096]{1,0:T(8,128)(2,1)S(1)}, u32[]{:S(2)}, u32[]{:S(2)}) collective-permute-start(bf16[16,4096]{1,0:T(8,128)(2,1)S(1)} %add_convert_fusion.19), channel_id=1, source_target_pairs={{0,14},{1,15},{2,0},{3,1},{4,2},{5,3},{6,4},{7,5},{8,6},{9,7},{10,... | collective-permute-start | bytes 393224 | tf_op jit(solution)/shard_map/ppermute | solution.py:283
  129.5 3.3 %collective-permute-start.25 = (bf16[16,4096]{1,0:T(8,128)(2,1)S(1)}, bf16[16,4096]{1,0:T(8,128)(2,1)S(1)}, u32[]{:S(2)}, u32[]{:S(2)}) collective-permute-start(bf16[16,4096]{1,0:T(8,128)(2,1)S(1)} %add_convert_fusion.7), channel_id=1, source_target_pairs={{0,14},{1,15},{2,0},{3,1},{4,2},{5,3},{6,4},{7,5},{8,6},{9,7},{10,... | collective-permute-start | bytes 393224 | tf_op jit(solution)/shard_map/ppermute | solution.py:283
  133.0 3.5 %collective-permute-start.15 = (bf16[16,4096]{1,0:T(8,128)(2,1)S(1)}, bf16[16,4096]{1,0:T(8,128)(2,1)S(1)}, u32[]{:S(2)}, u32[]{:S(2)}) collective-permute-start(bf16[16,4096]{1,0:T(8,128)(2,1)S(1)} %add_convert_fusion.14), channel_id=1, source_target_pairs={{0,14},{1,15},{2,0},{3,1},{4,2},{5,3},{6,4},{7,5},{8,6},{9,7},{10,... | collective-permute-start | bytes 393224 | tf_op jit(solution)/shard_map/ppermute | solution.py:283
  136.7 3.0 %collective-permute-done.15 = bf16[16,4096]{1,0:T(8,128)(2,1)S(1)} collective-permute-done((bf16[16,4096]{1,0:T(8,128)(2,1)S(1)}, bf16[16,4096]{1,0:T(8,128)(2,1)S(1)}, u32[]{:S(2)}, u32[]{:S(2)}) %collective-permute-start.15) | collective-permute-done | bytes 131104 | tf_op jit(solution)/shard_map/ppermute | solution.py:283
  139.6 3.7 %collective-permute-start.32 = (bf16[16,4096]{1,0:T(8,128)(2,1)S(1)}, bf16[16,4096]{1,0:T(8,128)(2,1)S(1)}, u32[]{:S(2)}, u32[]{:S(2)}) collective-permute-start(bf16[16,4096]{1,0:T(8,128)(2,1)S(1)} %add_convert_fusion.2), channel_id=1, source_target_pairs={{0,14},{1,15},{2,0},{3,1},{4,2},{5,3},{6,4},{7,5},{8,6},{9,7},{10,... | collective-permute-start | bytes 393224 | tf_op jit(solution)/shard_map/ppermute | solution.py:283
  146.3 3.0 %collective-permute-start.22 = (bf16[16,4096]{1,0:T(8,128)(2,1)S(1)}, bf16[16,4096]{1,0:T(8,128)(2,1)S(1)}, u32[]{:S(2)}, u32[]{:S(2)}) collective-permute-start(bf16[16,4096]{1,0:T(8,128)(2,1)S(1)} %add_convert_fusion.9), channel_id=1, source_target_pairs={{0,2},{1,3},{2,4},{3,5},{4,6},{5,7},{6,8},{7,9},{8,10},{9,11},{10,... | collective-permute-start | bytes 393224 | tf_op jit(solution)/shard_map/ppermute | solution.py:283
  149.3 3.1 %collective-permute-done.5 = bf16[16,4096]{1,0:T(8,128)(2,1)S(1)} collective-permute-done((bf16[16,4096]{1,0:T(8,128)(2,1)S(1)}, bf16[16,4096]{1,0:T(8,128)(2,1)S(1)}, u32[]{:S(2)}, u32[]{:S(2)}) %collective-permute-start.5) | collective-permute-done | bytes 131104 | tf_op jit(solution)/shard_map/ppermute | solution.py:283
  (107 shorter events, 25.9 us)
Async XLA Ops:
  2.1 23.3 %all-to-all-start = ((bf16[16,2,128,128]{3,2,1,0:T(8,128)(2,1)}), bf16[16,2,128,128]{3,2,1,0:T(8,128)(2,1)S(1)}, u32[]{:S(2)}, u32[]{:S(2)}) async-start(bf16[16,2,128,128]{3,2,1,0:T(8,128)(2,1)} %broadcast_in_dim.8), calls=%async_computation | async-start | bytes 2097152 | tf_op jit(solution)/shard_map/all_to_all | solution.py:269
  26.6 20.8 %all-to-all-start.1 = ((bf16[16,2,128,128]{3,2,1,0:T(8,128)(2,1)}), bf16[16,2,128,128]{3,2,1,0:T(8,128)(2,1)}, u32[]{:S(2)}, u32[]{:S(2)}) async-start(bf16[16,2,128,128]{3,2,1,0:T(8,128)(2,1)} %broadcast_in_dim.20), calls=%async_computation.1 | async-start | bytes 2097152 | tf_op jit(solution)/shard_map/all_to_all | solution.py:269
  32.7 25.5 %collective-permute-start = (bf16[16,2,128,128]{3,2,1,0:T(8,128)(2,1)S(1)}, bf16[16,2,128,128]{3,2,1,0:T(8,128)(2,1)S(1)}, u32[]{:S(2)}, u32[]{:S(2)}) collective-permute-start(bf16[16,2,128,128]{3,2,1,0:T(8,128)(2,1)S(1)} %all-to-all-done.refs_3_), channel_id=1, source_target_pairs={{0,1},{1,0},{2,3},{3,2},{4,5},{5,4},{6,7},{7,6},{8,9},{9,8},{10,11... | collective-permute-start | bytes 3145736 | tf_op jit(solution)/shard_map/ppermute | solution.py:291
  47.4 22.4 %collective-permute-start.17 = (bf16[16,2,128,128]{3,2,1,0:T(8,128)(2,1)}, bf16[16,2,128,128]{3,2,1,0:T(8,128)(2,1)}, u32[]{:S(2)}, u32[]{:S(2)}) collective-permute-start(bf16[16,2,128,128]{3,2,1,0:T(8,128)(2,1)} %all-to-all-done.1.refs_5_), channel_id=1, source_target_pairs={{0,1},{1,0},{2,3},{3,2},{4,5},{5,4},{6,7},{7,6},{8,9},{9,8},{10,11... | collective-permute-start | bytes 3145736 | tf_op jit(solution)/shard_map/ppermute | solution.py:291
  69.2 24.0 %collective-permute-start.1 = (bf16[128,4096]{1,0:T(8,128)(2,1)}, bf16[128,4096]{1,0:T(8,128)(2,1)S(1)}, u32[]{:S(2)}, u32[]{:S(2)}) collective-permute-start(bf16[128,4096]{1,0:T(8,128)(2,1)} %get-tuple-element.48), channel_id=1, source_target_pairs={{0,1},{1,0},{2,3},{3,2},{4,5},{5,4},{6,7},{7,6},{8,9},{9,8},{10,11... | collective-permute-start | bytes 3145736 | tf_op jit(solution)/shard_map/ppermute | solution.py:296
  80.5 19.0 %collective-permute-start.18 = (bf16[128,4096]{1,0:T(8,128)(2,1)}, bf16[128,4096]{1,0:T(8,128)(2,1)S(1)}, u32[]{:S(2)}, u32[]{:S(2)}) collective-permute-start(bf16[128,4096]{1,0:T(8,128)(2,1)} %get-tuple-element.69), channel_id=1, source_target_pairs={{0,1},{1,0},{2,3},{3,2},{4,5},{5,4},{6,7},{7,6},{8,9},{9,8},{10,11... | collective-permute-start | bytes 3145736 | tf_op jit(solution)/shard_map/ppermute | solution.py:296
  86.6 13.2 %collective-permute-start.9 = (bf16[128,4096]{1,0:T(8,128)(2,1)}, bf16[128,4096]{1,0:T(8,128)(2,1)S(1)}, u32[]{:S(2)}, u32[]{:S(2)}) collective-permute-start(bf16[128,4096]{1,0:T(8,128)(2,1)} %get-tuple-element.59), channel_id=1, source_target_pairs={{0,1},{1,0},{2,3},{3,2},{4,5},{5,4},{6,7},{7,6},{8,9},{9,8},{10,11... | collective-permute-start | bytes 3145736 | tf_op jit(solution)/shard_map/ppermute | solution.py:296
  93.1 10.3 %collective-permute-start.26 = (bf16[128,4096]{1,0:T(8,128)(2,1)}, bf16[128,4096]{1,0:T(8,128)(2,1)S(1)}, u32[]{:S(2)}, u32[]{:S(2)}) collective-permute-start(bf16[128,4096]{1,0:T(8,128)(2,1)} %get-tuple-element.80), channel_id=1, source_target_pairs={{0,1},{1,0},{2,3},{3,2},{4,5},{5,4},{6,7},{7,6},{8,9},{9,8},{10,11... | collective-permute-start | bytes 3145736 | tf_op jit(solution)/shard_map/ppermute | solution.py:296
  93.5 11.4 %collective-permute-start.2 = (bf16[16,4096]{1,0:T(8,128)(2,1)S(1)}, bf16[16,4096]{1,0:T(8,128)(2,1)S(1)}, u32[]{:S(2)}, u32[]{:S(2)}) collective-permute-start(bf16[16,4096]{1,0:T(8,128)(2,1)S(1)} %get-tuple-element.53), channel_id=1, source_target_pairs={{0,2},{1,3},{2,4},{3,5},{4,6},{5,7},{6,8},{7,9},{8,10},{9,11},{10,... | collective-permute-start | bytes 393224 | tf_op jit(solution)/shard_map/ppermute | solution.py:283
  95.5 12.9 %collective-permute-start.6 = (bf16[16,4096]{1,0:T(8,128)(2,1)S(1)}, bf16[16,4096]{1,0:T(8,128)(2,1)S(1)}, u32[]{:S(2)}, u32[]{:S(2)}) collective-permute-start(bf16[16,4096]{1,0:T(8,128)(2,1)S(1)} %get-tuple-element.56), channel_id=1, source_target_pairs={{0,14},{1,15},{2,0},{3,1},{4,2},{5,3},{6,4},{7,5},{8,6},{9,7},{10,... | collective-permute-start | bytes 393224 | tf_op jit(solution)/shard_map/ppermute | solution.py:283
  99.8 8.8 %collective-permute-start.19 = (bf16[16,4096]{1,0:T(8,128)(2,1)S(1)}, bf16[16,4096]{1,0:T(8,128)(2,1)S(1)}, u32[]{:S(2)}, u32[]{:S(2)}) collective-permute-start(bf16[16,4096]{1,0:T(8,128)(2,1)S(1)} %get-tuple-element.74), channel_id=1, source_target_pairs={{0,2},{1,3},{2,4},{3,5},{4,6},{5,7},{6,8},{7,9},{8,10},{9,11},{10,... | collective-permute-start | bytes 393224 | tf_op jit(solution)/shard_map/ppermute | solution.py:283
  99.9 12.0 %collective-permute-start.23 = (bf16[16,4096]{1,0:T(8,128)(2,1)S(1)}, bf16[16,4096]{1,0:T(8,128)(2,1)S(1)}, u32[]{:S(2)}, u32[]{:S(2)}) collective-permute-start(bf16[16,4096]{1,0:T(8,128)(2,1)S(1)} %get-tuple-element.77), channel_id=1, source_target_pairs={{0,14},{1,15},{2,0},{3,1},{4,2},{5,3},{6,4},{7,5},{8,6},{9,7},{10,... | collective-permute-start | bytes 393224 | tf_op jit(solution)/shard_map/ppermute | solution.py:283
  103.3 8.7 %collective-permute-start.10 = (bf16[16,4096]{1,0:T(8,128)(2,1)S(1)}, bf16[16,4096]{1,0:T(8,128)(2,1)S(1)}, u32[]{:S(2)}, u32[]{:S(2)}) collective-permute-start(bf16[16,4096]{1,0:T(8,128)(2,1)S(1)} %get-tuple-element.63), channel_id=1, source_target_pairs={{0,2},{1,3},{2,4},{3,5},{4,6},{5,7},{6,8},{7,9},{8,10},{9,11},{10,... | collective-permute-start | bytes 393224 | tf_op jit(solution)/shard_map/ppermute | solution.py:283
  104.9 10.5 %collective-permute-start.13 = (bf16[16,4096]{1,0:T(8,128)(2,1)S(1)}, bf16[16,4096]{1,0:T(8,128)(2,1)S(1)}, u32[]{:S(2)}, u32[]{:S(2)}) collective-permute-start(bf16[16,4096]{1,0:T(8,128)(2,1)S(1)} %get-tuple-element.67), channel_id=1, source_target_pairs={{0,14},{1,15},{2,0},{3,1},{4,2},{5,3},{6,4},{7,5},{8,6},{9,7},{10,... | collective-permute-start | bytes 393224 | tf_op jit(solution)/shard_map/ppermute | solution.py:283
  108.6 10.3 %collective-permute-start.30 = (bf16[16,4096]{1,0:T(8,128)(2,1)S(1)}, bf16[16,4096]{1,0:T(8,128)(2,1)S(1)}, u32[]{:S(2)}, u32[]{:S(2)}) collective-permute-start(bf16[16,4096]{1,0:T(8,128)(2,1)S(1)} %get-tuple-element.88), channel_id=1, source_target_pairs={{0,14},{1,15},{2,0},{3,1},{4,2},{5,3},{6,4},{7,5},{8,6},{9,7},{10,... | collective-permute-start | bytes 393224 | tf_op jit(solution)/shard_map/ppermute | solution.py:283
  112.1 10.3 %collective-permute-start.7 = (bf16[16,4096]{1,0:T(8,128)(2,1)S(1)}, bf16[16,4096]{1,0:T(8,128)(2,1)S(1)}, u32[]{:S(2)}, u32[]{:S(2)}) collective-permute-start(bf16[16,4096]{1,0:T(8,128)(2,1)S(1)} %add_convert_fusion.20), channel_id=1, source_target_pairs={{0,14},{1,15},{2,0},{3,1},{4,2},{5,3},{6,4},{7,5},{8,6},{9,7},{10,... | collective-permute-start | bytes 393224 | tf_op jit(solution)/shard_map/ppermute | solution.py:283
  115.6 10.3 %collective-permute-start.24 = (bf16[16,4096]{1,0:T(8,128)(2,1)S(1)}, bf16[16,4096]{1,0:T(8,128)(2,1)S(1)}, u32[]{:S(2)}, u32[]{:S(2)}) collective-permute-start(bf16[16,4096]{1,0:T(8,128)(2,1)S(1)} %add_convert_fusion.8), channel_id=1, source_target_pairs={{0,14},{1,15},{2,0},{3,1},{4,2},{5,3},{6,4},{7,5},{8,6},{9,7},{10,... | collective-permute-start | bytes 393224 | tf_op jit(solution)/shard_map/ppermute | solution.py:283
  119.2 10.2 %collective-permute-start.14 = (bf16[16,4096]{1,0:T(8,128)(2,1)S(1)}, bf16[16,4096]{1,0:T(8,128)(2,1)S(1)}, u32[]{:S(2)}, u32[]{:S(2)}) collective-permute-start(bf16[16,4096]{1,0:T(8,128)(2,1)S(1)} %add_convert_fusion.15), channel_id=1, source_target_pairs={{0,14},{1,15},{2,0},{3,1},{4,2},{5,3},{6,4},{7,5},{8,6},{9,7},{10,... | collective-permute-start | bytes 393224 | tf_op jit(solution)/shard_map/ppermute | solution.py:283
  122.9 9.9 %collective-permute-start.31 = (bf16[16,4096]{1,0:T(8,128)(2,1)S(1)}, bf16[16,4096]{1,0:T(8,128)(2,1)S(1)}, u32[]{:S(2)}, u32[]{:S(2)}) collective-permute-start(bf16[16,4096]{1,0:T(8,128)(2,1)S(1)} %add_convert_fusion.3), channel_id=1, source_target_pairs={{0,14},{1,15},{2,0},{3,1},{4,2},{5,3},{6,4},{7,5},{8,6},{9,7},{10,... | collective-permute-start | bytes 393224 | tf_op jit(solution)/shard_map/ppermute | solution.py:283
  126.0 20.3 %collective-permute-start.8 = (bf16[16,4096]{1,0:T(8,128)(2,1)S(1)}, bf16[16,4096]{1,0:T(8,128)(2,1)S(1)}, u32[]{:S(2)}, u32[]{:S(2)}) collective-permute-start(bf16[16,4096]{1,0:T(8,128)(2,1)S(1)} %add_convert_fusion.19), channel_id=1, source_target_pairs={{0,14},{1,15},{2,0},{3,1},{4,2},{5,3},{6,4},{7,5},{8,6},{9,7},{10,... | collective-permute-start | bytes 393224 | tf_op jit(solution)/shard_map/ppermute | solution.py:283
  129.5 25.0 %collective-permute-start.25 = (bf16[16,4096]{1,0:T(8,128)(2,1)S(1)}, bf16[16,4096]{1,0:T(8,128)(2,1)S(1)}, u32[]{:S(2)}, u32[]{:S(2)}) collective-permute-start(bf16[16,4096]{1,0:T(8,128)(2,1)S(1)} %add_convert_fusion.7), channel_id=1, source_target_pairs={{0,14},{1,15},{2,0},{3,1},{4,2},{5,3},{6,4},{7,5},{8,6},{9,7},{10,... | collective-permute-start | bytes 393224 | tf_op jit(solution)/shard_map/ppermute | solution.py:283
  132.8 21.9 %collective-permute-start.12 = (bf16[16,4096]{1,0:T(8,128)(2,1)S(1)}, bf16[16,4096]{1,0:T(8,128)(2,1)S(1)}, u32[]{:S(2)}, u32[]{:S(2)}) collective-permute-start(bf16[16,4096]{1,0:T(8,128)(2,1)S(1)} %add_convert_fusion.16), channel_id=1, source_target_pairs={{0,2},{1,3},{2,4},{3,5},{4,6},{5,7},{6,8},{7,9},{8,10},{9,11},{10,... | collective-permute-start | bytes 393224 | tf_op jit(solution)/shard_map/ppermute | solution.py:283
  136.5 21.0 %collective-permute-start.29 = (bf16[16,4096]{1,0:T(8,128)(2,1)S(1)}, bf16[16,4096]{1,0:T(8,128)(2,1)S(1)}, u32[]{:S(2)}, u32[]{:S(2)}) collective-permute-start(bf16[16,4096]{1,0:T(8,128)(2,1)S(1)} %add_convert_fusion.4), channel_id=1, source_target_pairs={{0,2},{1,3},{2,4},{3,5},{4,6},{5,7},{6,8},{7,9},{8,10},{9,11},{10,... | collective-permute-start | bytes 393224 | tf_op jit(solution)/shard_map/ppermute | solution.py:283
  146.3 8.3 %collective-permute-start.22 = (bf16[16,4096]{1,0:T(8,128)(2,1)S(1)}, bf16[16,4096]{1,0:T(8,128)(2,1)S(1)}, u32[]{:S(2)}, u32[]{:S(2)}) collective-permute-start(bf16[16,4096]{1,0:T(8,128)(2,1)S(1)} %add_convert_fusion.9), channel_id=1, source_target_pairs={{0,2},{1,3},{2,4},{3,5},{4,6},{5,7},{6,8},{7,9},{8,10},{9,11},{10,... | collective-permute-start | bytes 393224 | tf_op jit(solution)/shard_map/ppermute | solution.py:283
  (20 other events, 164.2 us)

commit v2 on v1

v2 whole, which is shorter than its diff:
```python
import functools
import math

import jax
import jax.numpy as jnp
from jax import lax
from jax.experimental import pallas as pl
from jax.experimental.pallas import tpu as pltpu
from jax.sharding import PartitionSpec as P


QH = 64
KVH = 4
HD = 128
BLK = 128
STEPS = 2
SPANS = 16
LOCAL_HEADS = 4
SPAN = 256
NV = 4
NS = 4
DW = 8192
TILE = 512
HALVES = 2
WIDTH = DW // HALVES
TILES = 1 + NV + NS
PAIRS = LOCAL_HEADS * 2
ROWS = STEPS * SPAN
HIDDEN = -1e30
MIB = 1 << 20
GRANT = 56 * MIB


ANYWHERE = pl.BlockSpec(memory_space=pl.ANY)
SCALARS = pl.BlockSpec(memory_space=pltpu.SMEM)
IN_HBM = pl.BlockSpec(memory_space=pltpu.HBM)
IN_VMEM = pl.BlockSpec(memory_space=pltpu.VMEM)


def core_swap(heads):
    return [(h, h ^ 1) for h in range(heads)]


def shift_z(heads, amount):
    chips = heads // 2
    return [(h, ((h // 2 + amount) % chips) * 2 + h % 2) for h in range(heads)]


def plan_kernel(owner, vertical, slash, table):
    device = lax.axis_index("ctx")
    head_group = lax.axis_index("head")

    def one_pair(index, carry):
        step = index // PAIRS
        pair = lax.rem(index, PAIRS)
        head = head_group * LOCAL_HEADS + pair // 2

        def look(p, place):
            return place + jnp.where(owner[step, p] == device, p, 0)

        place = lax.fori_loop(0, SPANS, look, jnp.int32(0))
        block = (step * SPANS + place) * 2 + lax.rem(pair, 2)

        def put(slot, k, good):
            k = jnp.where(good, k, block)
            span = k // 2
            which = span // SPANS
            holder = owner[which, lax.rem(span, SPANS)]
            stored = (which * 2 + lax.rem(k, 2)) * SPANS + holder
            table[index * TILES + slot] = stored * 2 + jnp.where(good, 1, 0)

        put(0, block, block >= 0)
        picked = [vertical[head, n] for n in range(NV)]
        for n, k in enumerate(picked):
            put(1 + n, k, k < block)
        for n in range(NS):
            k = block - slash[head, n]
            good = k >= 0
            for other in picked:
                good = good & (k != other)
            put(1 + NV + n, k, good)
        return carry

    lax.fori_loop(0, STEPS * PAIRS, one_pair, 0)


def make_plan(owner, vertical, slash):
    return pl.pallas_call(
        plan_kernel,
        out_shape=jax.ShapeDtypeStruct((STEPS * PAIRS * TILES,), jnp.int32),
        in_specs=[SCALARS] * 3,
        out_specs=SCALARS,
        compiler_params=pltpu.CompilerParams(vmem_limit_bytes=MIB),
        name="plan",
    )(owner, vertical, slash)


def attend_kernel(table, q_hbm, mine, other, out, q_v, kv_v, s_0, s_1, m_0, m_1, p_0, p_1, sems):
    core = lax.rem(lax.axis_index("head"), 2)

    copies = [pltpu.make_async_copy(q_hbm, q_v, sems.at[0])]
    for step in range(STEPS):
        for side, store in enumerate((mine, other)):
            half = core if side == 0 else 1 - core
            start = pl.multiple_of((2 * step + half) * SPANS, SPANS)
            copies.append(
                pltpu.make_async_copy(
                    store.at[:, step], kv_v.at[pl.ds(start, SPANS)], sems.at[1 + 2 * step + side]
                )
            )
    for copy in copies:
        copy.start()
    for copy in copies[:3]:
        copy.wait()

    rows_at = lax.broadcasted_iota(jnp.int32, (BLK, BLK), 0)
    cols_at = lax.broadcasted_iota(jnp.int32, (BLK, BLK), 1)
    causal = cols_at <= rows_at
    factor = math.log2(math.e) / math.sqrt(HD)

    def parts(pair):
        step = pair // PAIRS
        head = lax.rem(pair // 2, LOCAL_HEADS)
        return step, pl.ds(pl.multiple_of(head * HD, HD), HD)

    def score(pair, inner, s_v, m_v):
        step, cols = parts(pair)
        q = q_v[step, inner * BLK : (inner + 1) * BLK, cols]
        codes = [table[pair * TILES + n] for n in range(TILES)]
        keys = jnp.concatenate(
            [kv_v[lax.shift_right_logical(code, 1), 0] for code in codes], axis=0
        )
        found = lax.dot_general(
            q, keys, (((1,), (1,)), ((), ())), preferred_element_type=jnp.float32
        )
        largest = None
        for n in range(TILES):
            s = found[:, n * BLK : (n + 1) * BLK]
            s = jnp.where(causal if n == 0 else (codes[n] & 1) == 1, s, HIDDEN)
            s_v[:, n * BLK : (n + 1) * BLK] = s
            largest = s if largest is None else jnp.maximum(largest, s)
        m_v[...] = largest

    def finish(pair, inner, s_v, m_v, p_v):
        step, cols = parts(pair)
        chunk = 32
        totals = []
        for row in range(0, BLK, chunk):
            rows = slice(row, row + chunk)
            shift = jnp.max(m_v[rows], axis=1, keepdims=True) * factor
            total = None
            for n in range(TILES):
                at = slice(n * BLK, (n + 1) * BLK)
                w = jnp.exp2(s_v[rows, at] * factor - shift)
                p_v[rows, at] = w.astype(jnp.bfloat16)
                total = w if total is None else total + w
            totals.append(jnp.sum(total, axis=1, keepdims=True))
        values = jnp.concatenate(
            [kv_v[lax.shift_right_logical(table[pair * TILES + n], 1), 1] for n in range(TILES)],
            axis=0,
        )
        mixed = jnp.dot(p_v[...], values, preferred_element_type=jnp.float32)
        result = (mixed / jnp.concatenate(totals, axis=0)).astype(jnp.bfloat16)
        for group in range(BLK // 16):
            z = inner * 4 + group // 2
            start = jnp.where(core == group % 2, ROWS // 2, 0) + step * (SPAN // 2) + z * 16
            out[pl.ds(pl.multiple_of(start, 16), 16), cols] = result[group * 16 : group * 16 + 16]

    last = STEPS * PAIRS - 2
    score(0, 0, s_0, m_0)

    def two_pairs(index, carry):
        pair = index * 2

        @pl.when(index == PAIRS // 2 - 1)
        def _():
            for copy in copies[3:]:
                copy.wait()

        score(pair + 1, 1, s_1, m_1)
        finish(pair, 0, s_0, m_0, p_0)
        score(jnp.minimum(pair + 2, last), 0, s_0, m_0)
        finish(pair + 1, 1, s_1, m_1, p_1)
        return carry

    lax.fori_loop(0, STEPS * PAIRS // 2, two_pairs, 0)


def attend(table, queries, mine, other):
    keys = TILES * BLK
    return pl.pallas_call(
        attend_kernel,
        out_shape=jax.ShapeDtypeStruct((ROWS, LOCAL_HEADS * HD), jnp.bfloat16),
        in_specs=[SCALARS] + [ANYWHERE] * 3,
        out_specs=IN_VMEM,
        scratch_shapes=[
            pltpu.VMEM((STEPS, SPAN, LOCAL_HEADS * HD), jnp.bfloat16),
            pltpu.VMEM((STEPS * 2 * SPANS, 2, BLK, HD), jnp.bfloat16),
            pltpu.VMEM((BLK, keys), jnp.float32),
            pltpu.VMEM((BLK, keys), jnp.float32),
            pltpu.VMEM((BLK, BLK), jnp.float32),
            pltpu.VMEM((BLK, BLK), jnp.float32),
            pltpu.VMEM((BLK, keys), jnp.bfloat16),
            pltpu.VMEM((BLK, keys), jnp.bfloat16),
            pltpu.SemaphoreType.DMA((1 + 2 * STEPS,)),
        ],
        cost_estimate=pl.CostEstimate(
            flops=8 * PAIRS * TILES * BLK * BLK * HD, bytes_accessed=8 * MIB, transcendentals=0
        ),
        compiler_params=pltpu.CompilerParams(vmem_limit_bytes=12 * MIB),
        name="attend",
    )(table, queries, mine, other)


def project_kernel(half, attended, w_hbm, send, own, w_v, out_v, in_sems, out_sems):
    tiles = WIDTH // TILE

    def columns(n):
        return pl.ds(pl.multiple_of(n * TILE, TILE), TILE)

    def copy_in(n):
        source = pl.ds(pl.multiple_of(half * WIDTH + n * TILE, TILE), TILE)
        return pltpu.make_async_copy(w_hbm.at[:, source], w_v.at[:, columns(n)], in_sems.at[n])

    def copies_out(n):
        return [
            pltpu.make_async_copy(
                out_v.at[pl.ds(side * (ROWS // 2), ROWS // 2), columns(n)],
                target.at[:, columns(n)],
                out_sems.at[n, side],
            )
            for side, target in enumerate((send, own))
        ]

    for n in range(tiles):
        copy_in(n).start()

    def one_tile(n, carry):
        copy_in(n).wait()
        for rows in (slice(0, ROWS // 2), slice(ROWS // 2, ROWS)):
            out_v[rows, columns(n)] = jnp.dot(
                attended[rows], w_v[:, columns(n)], preferred_element_type=jnp.float32
            ).astype(jnp.bfloat16)
        for copy in copies_out(n):
            copy.start()
        return carry

    lax.fori_loop(0, tiles, one_tile, 0)

    def end(n, carry):
        for copy in copies_out(n):
            copy.wait()
        return carry

    lax.fori_loop(0, tiles, end, 0)


def project(half, attended, weight):
    depth = LOCAL_HEADS * HD
    shape = jax.ShapeDtypeStruct((ROWS // 2, WIDTH), jnp.bfloat16)
    return pl.pallas_call(
        functools.partial(project_kernel, half),
        out_shape=(shape, shape),
        in_specs=[IN_VMEM, IN_HBM],
        out_specs=(ANYWHERE, ANYWHERE),
        scratch_shapes=[
            pltpu.VMEM((depth, WIDTH), jnp.bfloat16),
            pltpu.VMEM((ROWS, WIDTH), jnp.bfloat16),
            pltpu.SemaphoreType.DMA((WIDTH // TILE,)),
            pltpu.SemaphoreType.DMA((WIDTH // TILE, 2)),
        ],
        cost_estimate=pl.CostEstimate(
            flops=2 * ROWS * depth * WIDTH, bytes_accessed=8 * MIB, transcendentals=0
        ),
        compiler_params=pltpu.CompilerParams(vmem_limit_bytes=GRANT),
    )(attended, weight)


def pair_sums(own, other, chips):
    def kernel(own_ref, other_ref, *outs):
        z = lax.axis_index("head") // 2
        for step in range(STEPS):
            for offset in range(chips):
                index = step * chips + lax.rem(z + offset, chips)
                total = own_ref[index].astype(jnp.float32) + other_ref[index].astype(jnp.float32)
                outs[step * chips + offset][...] = total.astype(jnp.bfloat16)

    shape = (STEPS * chips, own.shape[0] // (STEPS * chips), own.shape[1])
    sums = pl.pallas_call(
        kernel,
        out_shape=[jax.ShapeDtypeStruct(shape[1:], own.dtype)] * (STEPS * chips),
        in_specs=[IN_VMEM] * 2,
        out_specs=[IN_VMEM] * (STEPS * chips),
        cost_estimate=pl.CostEstimate(flops=0, bytes_accessed=6 * MIB, transcendentals=0),
        compiler_params=pltpu.CompilerParams(vmem_limit_bytes=8 * MIB),
    )(own.reshape(shape), other.reshape(shape))
    return [sums[step * chips : (step + 1) * chips] for step in range(STEPS)]


def local(queries, key_rows, value_rows, out_weight, span_owner, vertical_blocks, slash_offsets):
    heads = lax.axis_size("head")
    chips = heads // 2
    head_group = lax.axis_index("head")
    core = lax.rem(head_group, 2)
    kv_head = head_group * LOCAL_HEADS // (QH // KVH)
    swap = core_swap(heads)

    table = make_plan(span_owner, vertical_blocks, slash_offsets)

    def own_block(rows):
        return lax.dynamic_slice(rows, (0, core * BLK, kv_head * HD), (STEPS, BLK, HD))

    block = jnp.stack([own_block(key_rows), own_block(value_rows)], axis=1)
    block = jnp.broadcast_to(block[None], (SPANS, STEPS, 2, BLK, HD))
    mine = lax.all_to_all(block, "ctx", 0, 0, tiled=True)
    other = lax.ppermute(mine, "head", swap)
    attended = attend(table, queries, mine, other)

    streams = {}
    for half in range(HALVES):
        send, own = project(half, attended, out_weight)
        got = lax.ppermute(send, "head", swap)
        for step, sums in enumerate(pair_sums(own, got, chips)):
            streams[step, half] = sums

    moving = {}
    far = chips // 2

    def hop(step, half, direction, number):
        longest = far if (direction == 1) == (half == 0) else far - 1
        distance = longest - number
        if distance < 1:
            return
        key = (step, half, direction)
        total = streams[step, half][(direction * distance) % chips]
        if key in moving:
            total = total.astype(jnp.float32) + moving[key].astype(jnp.float32)
        total = total.astype(jnp.bfloat16)
        moving[key] = lax.ppermute(total, "head", shift_z(heads, direction))

    for number in range(far):
        for side in (1, -1):
            for half in range(HALVES):
                for step in range(STEPS):
                    hop(step, half, side, number)

    outputs = []
    for step in range(STEPS):
        columns = []
        for half in range(HALVES):
            total = streams[step, half][0].astype(jnp.float32)
            for direction in (1, -1):
                total = total + moving[step, half, direction].astype(jnp.float32)
            columns.append(total.astype(jnp.bfloat16))
        outputs.append(jnp.concatenate(columns, axis=1)[None])
    return jnp.concatenate(outputs)


def solution(mesh):
    in_specs = (
        P(None, "ctx", "head"),
        P(None, "ctx", None),
        P(None, "ctx", None),
        P("head", None),
        P(),
        P(),
        P(),
    )
    out_specs = P(None, ("ctx", "head"), None)

    return jax.shard_map(local, mesh=mesh, in_specs=in_specs, out_specs=out_specs, check_vma=False)
```

time: 162 us -> 130 us (0.80)
  blocking collectives: 0 us -> 34.4 us
  waiting for transfers between devices: 44.5 us -> 13.3 us
  starting transfers between devices: 63.9 us -> 46.3 us
  Pallas kernels: 41.5 us -> 30.4 us
  local copies, waits for them, and re-layouts: 8.35 us -> 2.39 us
    all_to_all x0 -> x1, blocking collectives: none -> 34.4 us  [local(): mine = lax.all_to_all(block, 'ctx', 0, 0, tiled=True)]
    all_to_all x2 -> x0, waiting for transfers between devices: 30.5 us -> none  [local(): gathered.append(lax.all_to_all(mine, 'ctx', 0, 0, tiled=True))]
    all_to_all x2 -> x0, starting transfers between devices: 13.5 us -> none  [local(): gathered.append(lax.all_to_all(mine, 'ctx', 0, 0, tiled=True))]
    pallas_call x2 -> x1, Pallas kernels: 20.7 us -> 8.17 us  [attend(): pl.pallas_call(attend_kernel, out_shape=jax.ShapeDtypeStruct((ROWS, LOCAL...]
    unnamed x18 -> x16, local copies, waits for them, and re-layouts: 5 us -> 1.01 us
    ppermute x28, starting transfers between devices: 48.9 us -> 45.5 us  [hop(): moving[key] = lax.ppermute(total, 'head', shift_z(heads, direction))]
    broadcast_in_dim x2 -> x1, local copies, waits for them, and re-layouts: 2.53 us -> 0.49 us  [local(): block = jnp.broadcast_to(block[None], (SPANS, STEPS, 2, BLK, HD))]
  transfers between devices with their start and end apart: 36 -> 31, of which waited for: 9 -> 9; matrix products, arithmetic and copies ran while one was open for 1% -> 1% of each run, Pallas kernels for 26% -> 12%
where the time goes in v2:
time: 130 us; the launch traced here: 129 us
  starting transfers between devices  46.3 us (36%)
  blocking collectives  34.4 us (26%)
  Pallas kernels  30.4 us (23%)
  waiting for transfers between devices  13.3 us (10%)
  local copies, waits for them, and re-layouts  2.39 us (2%)
  other arithmetic  1.79 us (1%)
    ppermute x28, starting transfers between devices, hop(): moving[key] = lax.ppermute(total, 'head', shift_z(heads, direction))  45.5 us
    all_to_all x1, blocking collectives, local(): mine = lax.all_to_all(block, 'ctx', 0, 0, tiled=True)  34.4 us
    pallas_call x2, Pallas kernels, project(): pl.pallas_call(functools.partial(project_kernel, half), out_shape=(shape,...  13.3 us
    ppermute x28, waiting for transfers between devices, hop(): moving[key] = lax.ppermute(total, 'head', shift_z(heads, direction))  13.2 us
    pallas_call x1, Pallas kernels, attend(): pl.pallas_call(attend_kernel, out_shape=jax.ShapeDtypeStruct((ROWS, LOCAL...  8.17 us
    pallas_call x1, Pallas kernels, make_plan(): pl.pallas_call(plan_kernel, out_shape=jax.ShapeDtypeStruct((STEPS * PAIRS...  7.92 us
  transfers between devices with their start and end apart: 31, of which 9 were waited for; matrix products, arithmetic and copies ran while one was open for 1% of the time, Pallas kernels for 12%

profile of v2, /device:TPU:2, one launch (start us, length us, event | category | flops | bytes accessed | tf_op | source)
XLA Modules:
  0.0 129.1 jit_solution(17565149345335251509)
XLA Ops:
  1.5 34.4 %all_to_all.5.mine = bf16[16,2,2,128,128]{4,3,2,1,0:T(8,128)(2,1)S(1)} all-to-all(bf16[16,2,2,128,128]{4,3,2,1,0:T(8,128)(2,1)S(1)} %broadcast_in_dim.12), channel_id=1, replica_groups=mesh['ctx'=16,'head'=16] {'ctx'}, dimensions={0} | all-to-all | bytes 4194304 | tf_op jit(solution)/shard_map/all_to_all | solution.py:315
  36.1 7.9 %plan.1.table = s32[144]{0:T(256)S(1)} custom-call(s32[2,16]{1,0:T(2,128)S(1)} %copy-done.4, s32[64,4]{1,0:T(8,128)S(1)} %copy.8.vertical, s32[64,4]{1,0:T(8,128)S(1)} %copy.9.slash), custom_call_target="tpu_custom_call" | custom-call | tf_op jit(solution)/shard_map/plan/pallas_call | solution.py:88
  44.0 8.2 %attend.1.attended = bf16[512,512]{1,0:T(8,128)(2,1)S(1)} custom-call(s32[144]{0:T(256)S(1)} %plan.1.table, bf16[2,256,512]{2,1,0:T(8,128)(2,1)S(1)} %copy-done.3, bf16[16,2,2,128,128]{4,3,2,1,0:T(8,128)(2,1)S(1)} %all_to_all.5.mine, bf16[16,2,2,128,128]{4,3,2,1,0:T(8,128)(2,1)} %collective-permute-done.other), custom_call_target="tpu_custom_call" | custom-call | flops 1207959552 | bytes 8388608 | tf_op jit(solution)/shard_map/attend/pallas_call | solution.py:191
  53.0 6.7 %shard_map.75 = (bf16[256,4096]{1,0:T(8,128)(2,1)}, bf16[256,4096]{1,0:T(8,128)(2,1)}) custom-call(bf16[512,512]{1,0:T(8,128)(2,1)} %copy-done, bf16[512,8192]{1,0:T(8,128)(2,1)} %w_hbm.3), custom_call_target="tpu_custom_call" | custom-call | flops 2147483648 | bytes 8388608 | tf_op jit(solution)/shard_map/pallas_call | solution.py:261
  60.3 6.7 %shard_map.73 = (bf16[256,4096]{1,0:T(8,128)(2,1)}, bf16[256,4096]{1,0:T(8,128)(2,1)}) custom-call(bf16[512,512]{1,0:T(8,128)(2,1)} %copy-done, bf16[512,8192]{1,0:T(8,128)(2,1)} %w_hbm.3), custom_call_target="tpu_custom_call" | custom-call | flops 2147483648 | bytes 8388608 | tf_op jit(solution)/shard_map/pallas_call | solution.py:261
  67.7 2.0 %collective-permute-start.10 = (bf16[16,4096]{1,0:T(8,128)(2,1)S(1)}, bf16[16,4096]{1,0:T(8,128)(2,1)S(1)}, u32[]{:S(2)}, u32[]{:S(2)}) collective-permute-start(bf16[16,4096]{1,0:T(8,128)(2,1)S(1)} %get-tuple-element.56), channel_id=1, source_target_pairs={{0,2},{1,3},{2,4},{3,5},{4,6},{5,7},{6,8},{7,9},{8,10},{9,11},{10,... | collective-permute-start | bytes 393224 | tf_op jit(solution)/shard_map/ppermute | solution.py:339
  69.7 4.0 %collective-permute-start.13 = (bf16[16,4096]{1,0:T(8,128)(2,1)S(1)}, bf16[16,4096]{1,0:T(8,128)(2,1)S(1)}, u32[]{:S(2)}, u32[]{:S(2)}) collective-permute-start(bf16[16,4096]{1,0:T(8,128)(2,1)S(1)} %get-tuple-element.60), channel_id=1, source_target_pairs={{0,14},{1,15},{2,0},{3,1},{4,2},{5,3},{6,4},{7,5},{8,6},{9,7},{10,... | collective-permute-start | bytes 393224 | tf_op jit(solution)/shard_map/ppermute | solution.py:339
  73.7 3.2 %collective-permute-start.27 = (bf16[16,4096]{1,0:T(8,128)(2,1)S(1)}, bf16[16,4096]{1,0:T(8,128)(2,1)S(1)}, u32[]{:S(2)}, u32[]{:S(2)}) collective-permute-start(bf16[16,4096]{1,0:T(8,128)(2,1)S(1)} %get-tuple-element.76), channel_id=1, source_target_pairs={{0,14},{1,15},{2,0},{3,1},{4,2},{5,3},{6,4},{7,5},{8,6},{9,7},{10,... | collective-permute-start | bytes 393224 | tf_op jit(solution)/shard_map/ppermute | solution.py:339
  77.7 3.0 %collective-permute-start.6 = (bf16[16,4096]{1,0:T(8,128)(2,1)S(1)}, bf16[16,4096]{1,0:T(8,128)(2,1)S(1)}, u32[]{:S(2)}, u32[]{:S(2)}) collective-permute-start(bf16[16,4096]{1,0:T(8,128)(2,1)S(1)} %get-tuple-element.50), channel_id=1, source_target_pairs={{0,14},{1,15},{2,0},{3,1},{4,2},{5,3},{6,4},{7,5},{8,6},{9,7},{10,... | collective-permute-start | bytes 393224 | tf_op jit(solution)/shard_map/ppermute | solution.py:339
  80.9 3.3 %collective-permute-start.21 = (bf16[16,4096]{1,0:T(8,128)(2,1)S(1)}, bf16[16,4096]{1,0:T(8,128)(2,1)S(1)}, u32[]{:S(2)}, u32[]{:S(2)}) collective-permute-start(bf16[16,4096]{1,0:T(8,128)(2,1)S(1)} %get-tuple-element.68), channel_id=1, source_target_pairs={{0,14},{1,15},{2,0},{3,1},{4,2},{5,3},{6,4},{7,5},{8,6},{9,7},{10,... | collective-permute-start | bytes 393224 | tf_op jit(solution)/shard_map/ppermute | solution.py:339
  84.6 3.3 %collective-permute-start.14 = (bf16[16,4096]{1,0:T(8,128)(2,1)S(1)}, bf16[16,4096]{1,0:T(8,128)(2,1)S(1)}, u32[]{:S(2)}, u32[]{:S(2)}) collective-permute-start(bf16[16,4096]{1,0:T(8,128)(2,1)S(1)} %add_convert_fusion.15), channel_id=1, source_target_pairs={{0,14},{1,15},{2,0},{3,1},{4,2},{5,3},{6,4},{7,5},{8,6},{9,7},{10,... | collective-permute-start | bytes 393224 | tf_op jit(solution)/shard_map/ppermute | solution.py:339
  88.1 3.3 %collective-permute-start.28 = (bf16[16,4096]{1,0:T(8,128)(2,1)S(1)}, bf16[16,4096]{1,0:T(8,128)(2,1)S(1)}, u32[]{:S(2)}, u32[]{:S(2)}) collective-permute-start(bf16[16,4096]{1,0:T(8,128)(2,1)S(1)} %add_convert_fusion.3), channel_id=1, source_target_pairs={{0,14},{1,15},{2,0},{3,1},{4,2},{5,3},{6,4},{7,5},{8,6},{9,7},{10,... | collective-permute-start | bytes 393224 | tf_op jit(solution)/shard_map/ppermute | solution.py:339
  91.7 3.1 %collective-permute-start.7 = (bf16[16,4096]{1,0:T(8,128)(2,1)S(1)}, bf16[16,4096]{1,0:T(8,128)(2,1)S(1)}, u32[]{:S(2)}, u32[]{:S(2)}) collective-permute-start(bf16[16,4096]{1,0:T(8,128)(2,1)S(1)} %add_convert_fusion.20), channel_id=1, source_target_pairs={{0,14},{1,15},{2,0},{3,1},{4,2},{5,3},{6,4},{7,5},{8,6},{9,7},{10,... | collective-permute-start | bytes 393224 | tf_op jit(solution)/shard_map/ppermute | solution.py:339
  95.4 2.9 %collective-permute-start.22 = (bf16[16,4096]{1,0:T(8,128)(2,1)S(1)}, bf16[16,4096]{1,0:T(8,128)(2,1)S(1)}, u32[]{:S(2)}, u32[]{:S(2)}) collective-permute-start(bf16[16,4096]{1,0:T(8,128)(2,1)S(1)} %add_convert_fusion.8), channel_id=1, source_target_pairs={{0,14},{1,15},{2,0},{3,1},{4,2},{5,3},{6,4},{7,5},{8,6},{9,7},{10,... | collective-permute-start | bytes 393224 | tf_op jit(solution)/shard_map/ppermute | solution.py:339
  98.5 3.3 %collective-permute-start.15 = (bf16[16,4096]{1,0:T(8,128)(2,1)S(1)}, bf16[16,4096]{1,0:T(8,128)(2,1)S(1)}, u32[]{:S(2)}, u32[]{:S(2)}) collective-permute-start(bf16[16,4096]{1,0:T(8,128)(2,1)S(1)} %add_convert_fusion.14), channel_id=1, source_target_pairs={{0,14},{1,15},{2,0},{3,1},{4,2},{5,3},{6,4},{7,5},{8,6},{9,7},{10,... | collective-permute-start | bytes 393224 | tf_op jit(solution)/shard_map/ppermute | solution.py:339
  102.0 3.3 %collective-permute-start.29 = (bf16[16,4096]{1,0:T(8,128)(2,1)S(1)}, bf16[16,4096]{1,0:T(8,128)(2,1)S(1)}, u32[]{:S(2)}, u32[]{:S(2)}) collective-permute-start(bf16[16,4096]{1,0:T(8,128)(2,1)S(1)} %add_convert_fusion.2), channel_id=1, source_target_pairs={{0,14},{1,15},{2,0},{3,1},{4,2},{5,3},{6,4},{7,5},{8,6},{9,7},{10,... | collective-permute-start | bytes 393224 | tf_op jit(solution)/shard_map/ppermute | solution.py:339
  105.5 3.3 %collective-permute-start.8 = (bf16[16,4096]{1,0:T(8,128)(2,1)S(1)}, bf16[16,4096]{1,0:T(8,128)(2,1)S(1)}, u32[]{:S(2)}, u32[]{:S(2)}) collective-permute-start(bf16[16,4096]{1,0:T(8,128)(2,1)S(1)} %add_convert_fusion.19), channel_id=1, source_target_pairs={{0,14},{1,15},{2,0},{3,1},{4,2},{5,3},{6,4},{7,5},{8,6},{9,7},{10,... | collective-permute-start | bytes 393224 | tf_op jit(solution)/shard_map/ppermute | solution.py:339
  109.0 2.6 %collective-permute-done.4 = bf16[16,4096]{1,0:T(8,128)(2,1)S(1)} collective-permute-done((bf16[16,4096]{1,0:T(8,128)(2,1)S(1)}, bf16[16,4096]{1,0:T(8,128)(2,1)S(1)}, u32[]{:S(2)}, u32[]{:S(2)}) %collective-permute-start.4) | collective-permute-done | bytes 131104 | tf_op jit(solution)/shard_map/ppermute | solution.py:339
  112.8 2.8 %collective-permute-done.19 = bf16[16,4096]{1,0:T(8,128)(2,1)S(1)} collective-permute-done((bf16[16,4096]{1,0:T(8,128)(2,1)S(1)}, bf16[16,4096]{1,0:T(8,128)(2,1)S(1)}, u32[]{:S(2)}, u32[]{:S(2)}) %collective-permute-start.19) | collective-permute-done | bytes 131104 | tf_op jit(solution)/shard_map/ppermute | solution.py:339
  115.6 2.0 %collective-permute-start.16 = (bf16[16,4096]{1,0:T(8,128)(2,1)S(1)}, bf16[16,4096]{1,0:T(8,128)(2,1)S(1)}, u32[]{:S(2)}, u32[]{:S(2)}) collective-permute-start(bf16[16,4096]{1,0:T(8,128)(2,1)S(1)} %add_convert_fusion.13), channel_id=1, source_target_pairs={{0,14},{1,15},{2,0},{3,1},{4,2},{5,3},{6,4},{7,5},{8,6},{9,7},{10,... | collective-permute-start | bytes 393224 | tf_op jit(solution)/shard_map/ppermute | solution.py:339
  117.8 2.8 %collective-permute-done.16 = bf16[16,4096]{1,0:T(8,128)(2,1)S(1)} collective-permute-done((bf16[16,4096]{1,0:T(8,128)(2,1)S(1)}, bf16[16,4096]{1,0:T(8,128)(2,1)S(1)}, u32[]{:S(2)}, u32[]{:S(2)}) %collective-permute-start.16) | collective-permute-done | bytes 131104 | tf_op jit(solution)/shard_map/ppermute | solution.py:339
  121.3 2.5 %collective-permute-start.20 = (bf16[16,4096]{1,0:T(8,128)(2,1)S(1)}, bf16[16,4096]{1,0:T(8,128)(2,1)S(1)}, u32[]{:S(2)}, u32[]{:S(2)}) collective-permute-start(bf16[16,4096]{1,0:T(8,128)(2,1)S(1)} %add_convert_fusion.9), channel_id=1, source_target_pairs={{0,2},{1,3},{2,4},{3,5},{4,6},{5,7},{6,8},{7,9},{8,10},{9,11},{10,... | collective-permute-start | bytes 393224 | tf_op jit(solution)/shard_map/ppermute | solution.py:339
  123.9 2.8 %collective-permute-done.5 = bf16[16,4096]{1,0:T(8,128)(2,1)S(1)} collective-permute-done((bf16[16,4096]{1,0:T(8,128)(2,1)S(1)}, bf16[16,4096]{1,0:T(8,128)(2,1)S(1)}, u32[]{:S(2)}, u32[]{:S(2)}) %collective-permute-start.5) | collective-permute-done | bytes 131104 | tf_op jit(solution)/shard_map/ppermute | solution.py:339
  126.8 1.3 %collective-permute-done.20 = bf16[16,4096]{1,0:T(8,128)(2,1)S(1)} collective-permute-done((bf16[16,4096]{1,0:T(8,128)(2,1)S(1)}, bf16[16,4096]{1,0:T(8,128)(2,1)S(1)}, u32[]{:S(2)}, u32[]{:S(2)}) %collective-permute-start.20) | collective-permute-done | bytes 131104 | tf_op jit(solution)/shard_map/ppermute | solution.py:339
  (91 shorter events, 9.8 us)
Async XLA Ops:
  35.9 8.1 %collective-permute-start = (bf16[16,2,2,128,128]{4,3,2,1,0:T(8,128)(2,1)S(1)}, bf16[16,2,2,128,128]{4,3,2,1,0:T(8,128)(2,1)}, u32[]{:S(2)}, u32[]{:S(2)}) collective-permute-start(bf16[16,2,2,128,128]{4,3,2,1,0:T(8,128)(2,1)S(1)} %all_to_all.5.mine), channel_id=1, source_target_pairs={{0,1},{1,0},{2,3},{3,2},{4,5},{5,4},{6,7},{7,6},{8,9},{9,8},{10,11... | collective-permute-start | bytes 6291464 | tf_op jit(solution)/shard_map/ppermute | solution.py:316
  59.7 7.5 %collective-permute-start.9 = (bf16[256,4096]{1,0:T(8,128)(2,1)}, bf16[256,4096]{1,0:T(8,128)(2,1)S(1)}, u32[]{:S(2)}, u32[]{:S(2)}) collective-permute-start(bf16[256,4096]{1,0:T(8,128)(2,1)} %get-tuple-element.52), channel_id=1, source_target_pairs={{0,1},{1,0},{2,3},{3,2},{4,5},{5,4},{6,7},{7,6},{8,9},{9,8},{10,11... | collective-permute-start | bytes 6291464 | tf_op jit(solution)/shard_map/ppermute | solution.py:322
  67.0 10.0 %collective-permute-start.1 = (bf16[256,4096]{1,0:T(8,128)(2,1)}, bf16[256,4096]{1,0:T(8,128)(2,1)S(1)}, u32[]{:S(2)}, u32[]{:S(2)}) collective-permute-start(bf16[256,4096]{1,0:T(8,128)(2,1)} %get-tuple-element.42), channel_id=1, source_target_pairs={{0,1},{1,0},{2,3},{3,2},{4,5},{5,4},{6,7},{7,6},{8,9},{9,8},{10,11... | collective-permute-start | bytes 6291464 | tf_op jit(solution)/shard_map/ppermute | solution.py:322
  67.7 10.0 %collective-permute-start.10 = (bf16[16,4096]{1,0:T(8,128)(2,1)S(1)}, bf16[16,4096]{1,0:T(8,128)(2,1)S(1)}, u32[]{:S(2)}, u32[]{:S(2)}) collective-permute-start(bf16[16,4096]{1,0:T(8,128)(2,1)S(1)} %get-tuple-element.56), channel_id=1, source_target_pairs={{0,2},{1,3},{2,4},{3,5},{4,6},{5,7},{6,8},{7,9},{8,10},{9,11},{10,... | collective-permute-start | bytes 393224 | tf_op jit(solution)/shard_map/ppermute | solution.py:339
  69.7 11.1 %collective-permute-start.13 = (bf16[16,4096]{1,0:T(8,128)(2,1)S(1)}, bf16[16,4096]{1,0:T(8,128)(2,1)S(1)}, u32[]{:S(2)}, u32[]{:S(2)}) collective-permute-start(bf16[16,4096]{1,0:T(8,128)(2,1)S(1)} %get-tuple-element.60), channel_id=1, source_target_pairs={{0,14},{1,15},{2,0},{3,1},{4,2},{5,3},{6,4},{7,5},{8,6},{9,7},{10,... | collective-permute-start | bytes 393224 | tf_op jit(solution)/shard_map/ppermute | solution.py:339
  73.7 7.2 %collective-permute-start.24 = (bf16[16,4096]{1,0:T(8,128)(2,1)S(1)}, bf16[16,4096]{1,0:T(8,128)(2,1)S(1)}, u32[]{:S(2)}, u32[]{:S(2)}) collective-permute-start(bf16[16,4096]{1,0:T(8,128)(2,1)S(1)} %get-tuple-element.72), channel_id=1, source_target_pairs={{0,2},{1,3},{2,4},{3,5},{4,6},{5,7},{6,8},{7,9},{8,10},{9,11},{10,... | collective-permute-start | bytes 393224 | tf_op jit(solution)/shard_map/ppermute | solution.py:339
  73.7 10.6 %collective-permute-start.27 = (bf16[16,4096]{1,0:T(8,128)(2,1)S(1)}, bf16[16,4096]{1,0:T(8,128)(2,1)S(1)}, u32[]{:S(2)}, u32[]{:S(2)}) collective-permute-start(bf16[16,4096]{1,0:T(8,128)(2,1)S(1)} %get-tuple-element.76), channel_id=1, source_target_pairs={{0,14},{1,15},{2,0},{3,1},{4,2},{5,3},{6,4},{7,5},{8,6},{9,7},{10,... | collective-permute-start | bytes 393224 | tf_op jit(solution)/shard_map/ppermute | solution.py:339
  77.4 7.2 %collective-permute-start.2 = (bf16[16,4096]{1,0:T(8,128)(2,1)S(1)}, bf16[16,4096]{1,0:T(8,128)(2,1)S(1)}, u32[]{:S(2)}, u32[]{:S(2)}) collective-permute-start(bf16[16,4096]{1,0:T(8,128)(2,1)S(1)} %get-tuple-element.47), channel_id=1, source_target_pairs={{0,2},{1,3},{2,4},{3,5},{4,6},{5,7},{6,8},{7,9},{8,10},{9,11},{10,... | collective-permute-start | bytes 393224 | tf_op jit(solution)/shard_map/ppermute | solution.py:339
  77.7 10.2 %collective-permute-start.6 = (bf16[16,4096]{1,0:T(8,128)(2,1)S(1)}, bf16[16,4096]{1,0:T(8,128)(2,1)S(1)}, u32[]{:S(2)}, u32[]{:S(2)}) collective-permute-start(bf16[16,4096]{1,0:T(8,128)(2,1)S(1)} %get-tuple-element.50), channel_id=1, source_target_pairs={{0,14},{1,15},{2,0},{3,1},{4,2},{5,3},{6,4},{7,5},{8,6},{9,7},{10,... | collective-permute-start | bytes 393224 | tf_op jit(solution)/shard_map/ppermute | solution.py:339
  80.8 7.3 %collective-permute-start.17 = (bf16[16,4096]{1,0:T(8,128)(2,1)S(1)}, bf16[16,4096]{1,0:T(8,128)(2,1)S(1)}, u32[]{:S(2)}, u32[]{:S(2)}) collective-permute-start(bf16[16,4096]{1,0:T(8,128)(2,1)S(1)} %get-tuple-element.65), channel_id=1, source_target_pairs={{0,2},{1,3},{2,4},{3,5},{4,6},{5,7},{6,8},{7,9},{8,10},{9,11},{10,... | collective-permute-start | bytes 393224 | tf_op jit(solution)/shard_map/ppermute | solution.py:339
  80.9 10.5 %collective-permute-start.21 = (bf16[16,4096]{1,0:T(8,128)(2,1)S(1)}, bf16[16,4096]{1,0:T(8,128)(2,1)S(1)}, u32[]{:S(2)}, u32[]{:S(2)}) collective-permute-start(bf16[16,4096]{1,0:T(8,128)(2,1)S(1)} %get-tuple-element.68), channel_id=1, source_target_pairs={{0,14},{1,15},{2,0},{3,1},{4,2},{5,3},{6,4},{7,5},{8,6},{9,7},{10,... | collective-permute-start | bytes 393224 | tf_op jit(solution)/shard_map/ppermute | solution.py:339
  84.3 7.4 %collective-permute-start.11 = (bf16[16,4096]{1,0:T(8,128)(2,1)S(1)}, bf16[16,4096]{1,0:T(8,128)(2,1)S(1)}, u32[]{:S(2)}, u32[]{:S(2)}) collective-permute-start(bf16[16,4096]{1,0:T(8,128)(2,1)S(1)} %add_convert_fusion.17), channel_id=1, source_target_pairs={{0,2},{1,3},{2,4},{3,5},{4,6},{5,7},{6,8},{7,9},{8,10},{9,11},{10,... | collective-permute-start | bytes 393224 | tf_op jit(solution)/shard_map/ppermute | solution.py:339
  84.6 10.3 %collective-permute-start.14 = (bf16[16,4096]{1,0:T(8,128)(2,1)S(1)}, bf16[16,4096]{1,0:T(8,128)(2,1)S(1)}, u32[]{:S(2)}, u32[]{:S(2)}) collective-permute-start(bf16[16,4096]{1,0:T(8,128)(2,1)S(1)} %add_convert_fusion.15), channel_id=1, source_target_pairs={{0,14},{1,15},{2,0},{3,1},{4,2},{5,3},{6,4},{7,5},{8,6},{9,7},{10,... | collective-permute-start | bytes 393224 | tf_op jit(solution)/shard_map/ppermute | solution.py:339
  87.9 7.5 %collective-permute-start.25 = (bf16[16,4096]{1,0:T(8,128)(2,1)S(1)}, bf16[16,4096]{1,0:T(8,128)(2,1)S(1)}, u32[]{:S(2)}, u32[]{:S(2)}) collective-permute-start(bf16[16,4096]{1,0:T(8,128)(2,1)S(1)} %add_convert_fusion.5), channel_id=1, source_target_pairs={{0,2},{1,3},{2,4},{3,5},{4,6},{5,7},{6,8},{7,9},{8,10},{9,11},{10,... | collective-permute-start | bytes 393224 | tf_op jit(solution)/shard_map/ppermute | solution.py:339
  88.1 10.3 %collective-permute-start.28 = (bf16[16,4096]{1,0:T(8,128)(2,1)S(1)}, bf16[16,4096]{1,0:T(8,128)(2,1)S(1)}, u32[]{:S(2)}, u32[]{:S(2)}) collective-permute-start(bf16[16,4096]{1,0:T(8,128)(2,1)S(1)} %add_convert_fusion.3), channel_id=1, source_target_pairs={{0,14},{1,15},{2,0},{3,1},{4,2},{5,3},{6,4},{7,5},{8,6},{9,7},{10,... | collective-permute-start | bytes 393224 | tf_op jit(solution)/shard_map/ppermute | solution.py:339
  91.4 7.1 %collective-permute-start.3 = (bf16[16,4096]{1,0:T(8,128)(2,1)S(1)}, bf16[16,4096]{1,0:T(8,128)(2,1)S(1)}, u32[]{:S(2)}, u32[]{:S(2)}) collective-permute-start(bf16[16,4096]{1,0:T(8,128)(2,1)S(1)} %add_convert_fusion.23), channel_id=1, source_target_pairs={{0,2},{1,3},{2,4},{3,5},{4,6},{5,7},{6,8},{7,9},{8,10},{9,11},{10,... | collective-permute-start | bytes 393224 | tf_op jit(solution)/shard_map/ppermute | solution.py:339
  91.7 10.2 %collective-permute-start.7 = (bf16[16,4096]{1,0:T(8,128)(2,1)S(1)}, bf16[16,4096]{1,0:T(8,128)(2,1)S(1)}, u32[]{:S(2)}, u32[]{:S(2)}) collective-permute-start(bf16[16,4096]{1,0:T(8,128)(2,1)S(1)} %add_convert_fusion.20), channel_id=1, source_target_pairs={{0,14},{1,15},{2,0},{3,1},{4,2},{5,3},{6,4},{7,5},{8,6},{9,7},{10,... | collective-permute-start | bytes 393224 | tf_op jit(solution)/shard_map/ppermute | solution.py:339
  94.9 7.1 %collective-permute-start.18 = (bf16[16,4096]{1,0:T(8,128)(2,1)S(1)}, bf16[16,4096]{1,0:T(8,128)(2,1)S(1)}, u32[]{:S(2)}, u32[]{:S(2)}) collective-permute-start(bf16[16,4096]{1,0:T(8,128)(2,1)S(1)} %add_convert_fusion.11), channel_id=1, source_target_pairs={{0,2},{1,3},{2,4},{3,5},{4,6},{5,7},{6,8},{7,9},{8,10},{9,11},{10,... | collective-permute-start | bytes 393224 | tf_op jit(solution)/shard_map/ppermute | solution.py:339
  95.4 9.9 %collective-permute-start.22 = (bf16[16,4096]{1,0:T(8,128)(2,1)S(1)}, bf16[16,4096]{1,0:T(8,128)(2,1)S(1)}, u32[]{:S(2)}, u32[]{:S(2)}) collective-permute-start(bf16[16,4096]{1,0:T(8,128)(2,1)S(1)} %add_convert_fusion.8), channel_id=1, source_target_pairs={{0,14},{1,15},{2,0},{3,1},{4,2},{5,3},{6,4},{7,5},{8,6},{9,7},{10,... | collective-permute-start | bytes 393224 | tf_op jit(solution)/shard_map/ppermute | solution.py:339
  98.4 19.3 %collective-permute-start.12 = (bf16[16,4096]{1,0:T(8,128)(2,1)S(1)}, bf16[16,4096]{1,0:T(8,128)(2,1)S(1)}, u32[]{:S(2)}, u32[]{:S(2)}) collective-permute-start(bf16[16,4096]{1,0:T(8,128)(2,1)S(1)} %add_convert_fusion.16), channel_id=1, source_target_pairs={{0,2},{1,3},{2,4},{3,5},{4,6},{5,7},{6,8},{7,9},{8,10},{9,11},{10,... | collective-permute-start | bytes 393224 | tf_op jit(solution)/shard_map/ppermute | solution.py:339
  98.5 7.0 %collective-permute-start.15 = (bf16[16,4096]{1,0:T(8,128)(2,1)S(1)}, bf16[16,4096]{1,0:T(8,128)(2,1)S(1)}, u32[]{:S(2)}, u32[]{:S(2)}) collective-permute-start(bf16[16,4096]{1,0:T(8,128)(2,1)S(1)} %add_convert_fusion.14), channel_id=1, source_target_pairs={{0,14},{1,15},{2,0},{3,1},{4,2},{5,3},{6,4},{7,5},{8,6},{9,7},{10,... | collective-permute-start | bytes 393224 | tf_op jit(solution)/shard_map/ppermute | solution.py:339
  101.9 19.5 %collective-permute-start.26 = (bf16[16,4096]{1,0:T(8,128)(2,1)S(1)}, bf16[16,4096]{1,0:T(8,128)(2,1)S(1)}, u32[]{:S(2)}, u32[]{:S(2)}) collective-permute-start(bf16[16,4096]{1,0:T(8,128)(2,1)S(1)} %add_convert_fusion.4), channel_id=1, source_target_pairs={{0,2},{1,3},{2,4},{3,5},{4,6},{5,7},{6,8},{7,9},{8,10},{9,11},{10,... | collective-permute-start | bytes 393224 | tf_op jit(solution)/shard_map/ppermute | solution.py:339
  105.5 18.4 %collective-permute-start.8 = (bf16[16,4096]{1,0:T(8,128)(2,1)S(1)}, bf16[16,4096]{1,0:T(8,128)(2,1)S(1)}, u32[]{:S(2)}, u32[]{:S(2)}) collective-permute-start(bf16[16,4096]{1,0:T(8,128)(2,1)S(1)} %add_convert_fusion.19), channel_id=1, source_target_pairs={{0,14},{1,15},{2,0},{3,1},{4,2},{5,3},{6,4},{7,5},{8,6},{9,7},{10,... | collective-permute-start | bytes 393224 | tf_op jit(solution)/shard_map/ppermute | solution.py:339
  111.6 15.2 %collective-permute-start.23 = (bf16[16,4096]{1,0:T(8,128)(2,1)S(1)}, bf16[16,4096]{1,0:T(8,128)(2,1)S(1)}, u32[]{:S(2)}, u32[]{:S(2)}) collective-permute-start(bf16[16,4096]{1,0:T(8,128)(2,1)S(1)} %add_convert_fusion.7), channel_id=1, source_target_pairs={{0,14},{1,15},{2,0},{3,1},{4,2},{5,3},{6,4},{7,5},{8,6},{9,7},{10,... | collective-permute-start | bytes 393224 | tf_op jit(solution)/shard_map/ppermute | solution.py:339
  (14 other events, 208.3 us)

commit v3 on v2

v3 whole, which is shorter than its diff:
```python
import functools
import math

import jax
import jax.numpy as jnp
from jax import lax
from jax.experimental import pallas as pl
from jax.experimental.pallas import tpu as pltpu
from jax.sharding import PartitionSpec as P


QH = 64
KVH = 4
HD = 128
BLK = 128
STEPS = 2
SPANS = 16
LOCAL_HEADS = 4
SPAN = 256
NV = 4
NS = 4
DW = 8192
TILE = 512
HALVES = 2
WIDTH = DW // HALVES
TILES = 1 + NV + NS
PAIRS = LOCAL_HEADS * 2
HIDDEN = -1e30
MIB = 1 << 20
GRANT = 24 * MIB


ANYWHERE = pl.BlockSpec(memory_space=pl.ANY)
SCALARS = pl.BlockSpec(memory_space=pltpu.SMEM)
IN_HBM = pl.BlockSpec(memory_space=pltpu.HBM)
IN_VMEM = pl.BlockSpec(memory_space=pltpu.VMEM)


def core_swap(heads):
    return [(h, h ^ 1) for h in range(heads)]


def shift_z(heads, amount):
    chips = heads // 2
    return [(h, ((h // 2 + amount) % chips) * 2 + h % 2) for h in range(heads)]


def plan_kernel(owner, vertical, slash, table):
    device = lax.axis_index("ctx")
    head_group = lax.axis_index("head")

    def one_pair(index, carry):
        step = index // PAIRS
        pair = lax.rem(index, PAIRS)
        head = head_group * LOCAL_HEADS + pair // 2

        def look(p, place):
            return place + jnp.where(owner[step, p] == device, p, 0)

        place = lax.fori_loop(0, SPANS, look, jnp.int32(0))
        block = (step * SPANS + place) * 2 + lax.rem(pair, 2)

        def put(slot, k, good):
            k = jnp.where(good, k, block)
            span = k // 2
            which = span // SPANS
            holder = owner[which, lax.rem(span, SPANS)]
            stored = (which * 2 + lax.rem(k, 2)) * SPANS + holder
            table[index * TILES + slot] = stored * 2 + jnp.where(good, 1, 0)

        put(0, block, block >= 0)
        picked = [vertical[head, n] for n in range(NV)]
        for n, k in enumerate(picked):
            put(1 + n, k, k < block)
        for n in range(NS):
            k = block - slash[head, n]
            good = k >= 0
            for other in picked:
                good = good & (k != other)
            put(1 + NV + n, k, good)
        return carry

    lax.fori_loop(0, STEPS * PAIRS, one_pair, 0)


def make_plan(owner, vertical, slash):
    return pl.pallas_call(
        plan_kernel,
        out_shape=jax.ShapeDtypeStruct((STEPS * PAIRS * TILES,), jnp.int32),
        in_specs=[SCALARS] * 3,
        out_specs=SCALARS,
        compiler_params=pltpu.CompilerParams(vmem_limit_bytes=MIB),
        name="plan",
    )(owner, vertical, slash)


def attend_kernel(step, table, q_hbm, *refs):
    stores = refs[: 2 * (step + 1)]
    w_hbm = refs[2 * (step + 1)]
    targets, scratch = refs[-16:-12], refs[-12:]
    q_v, kv_v, s_0, s_1, m_0, m_1, p_0, p_1, out, w_v, out_v, all_sems = scratch
    sems, w_sems, out_sems = all_sems.at[0], all_sems.at[1], all_sems.at[2:]
    core = lax.rem(lax.axis_index("head"), 2)

    copies = [pltpu.make_async_copy(q_hbm.at[step], q_v, sems.at[0])]
    for index, store in enumerate(stores):
        half = core if index % 2 == 0 else 1 - core
        start = pl.multiple_of((index // 2 * 2 + half) * SPANS, SPANS)
        copies.append(
            pltpu.make_async_copy(store, kv_v.at[pl.ds(start, SPANS)], sems.at[1 + index])
        )
    w_copies = []
    for half in range(HALVES):
        cols = pl.ds(half * WIDTH, WIDTH)
        w_copies.append(
            pltpu.make_async_copy(w_hbm.at[:, cols], w_v.at[:, cols], w_sems.at[half])
        )
    for copy in copies + w_copies:
        copy.start()
    for copy in copies:
        copy.wait()

    rows_at = lax.broadcasted_iota(jnp.int32, (BLK, BLK), 0)
    cols_at = lax.broadcasted_iota(jnp.int32, (BLK, BLK), 1)
    causal = cols_at <= rows_at
    factor = math.log2(math.e) / math.sqrt(HD)

    def columns(pair):
        return pl.ds(pl.multiple_of(pair // 2 * HD, HD), HD)

    def code_of(pair, n):
        return table[(step * PAIRS + pair) * TILES + n]

    def score(pair, inner, s_v, m_v):
        q = q_v[inner * BLK : (inner + 1) * BLK, columns(pair)]
        codes = [code_of(pair, n) for n in range(TILES)]
        keys = jnp.concatenate(
            [kv_v[lax.shift_right_logical(code, 1), 0] for code in codes], axis=0
        )
        found = lax.dot_general(
            q, keys, (((1,), (1,)), ((), ())), preferred_element_type=jnp.float32
        )
        largest = None
        for n in range(TILES):
            s = found[:, n * BLK : (n + 1) * BLK]
            s = jnp.where(causal if n == 0 else (codes[n] & 1) == 1, s, HIDDEN)
            s_v[:, n * BLK : (n + 1) * BLK] = s
            largest = s if largest is None else jnp.maximum(largest, s)
        m_v[...] = largest

    def finish(pair, inner, s_v, m_v, p_v):
        cols = columns(pair)
        chunk = 32
        totals = []
        for row in range(0, BLK, chunk):
            rows = slice(row, row + chunk)
            shift = jnp.max(m_v[rows], axis=1, keepdims=True) * factor
            total = None
            for n in range(TILES):
                at = slice(n * BLK, (n + 1) * BLK)
                w = jnp.exp2(s_v[rows, at] * factor - shift)
                p_v[rows, at] = w.astype(jnp.bfloat16)
                total = w if total is None else total + w
            totals.append(jnp.sum(total, axis=1, keepdims=True))
        values = jnp.concatenate(
            [kv_v[lax.shift_right_logical(code_of(pair, n), 1), 1] for n in range(TILES)],
            axis=0,
        )
        mixed = jnp.dot(p_v[...], values, preferred_element_type=jnp.float32)
        result = (mixed / jnp.concatenate(totals, axis=0)).astype(jnp.bfloat16)
        for group in range(BLK // 16):
            z = inner * 4 + group // 2
            start = jnp.where(core == group % 2, SPAN // 2, 0) + z * 16
            out[pl.ds(pl.multiple_of(start, 16), 16), cols] = result[group * 16 : group * 16 + 16]

    score(0, 0, s_0, m_0)

    def two_pairs(index, carry):
        pair = index * 2
        score(pair + 1, 1, s_1, m_1)
        finish(pair, 0, s_0, m_0, p_0)
        score(jnp.minimum(pair + 2, PAIRS - 2), 0, s_0, m_0)
        finish(pair + 1, 1, s_1, m_1, p_1)
        return carry

    lax.fori_loop(0, PAIRS // 2, two_pairs, 0)

    def copies_out(half, n):
        source = pl.ds(pl.multiple_of(half * WIDTH + n * TILE, TILE), TILE)
        cols = pl.ds(pl.multiple_of(n * TILE, TILE), TILE)
        return [
            pltpu.make_async_copy(
                out_v.at[pl.ds(side * (SPAN // 2), SPAN // 2), source],
                targets[half * 2 + side].at[:, cols],
                out_sems.at[half * 2 + side, n],
            )
            for side in range(2)
        ]

    tiles = WIDTH // TILE
    for half in range(HALVES):
        w_copies[half].wait()

        def one_tile(n, carry):
            cols = pl.ds(pl.multiple_of(half * WIDTH + n * TILE, TILE), TILE)
            out_v[:, cols] = jnp.dot(
                out[...], w_v[:, cols], preferred_element_type=jnp.float32
            ).astype(jnp.bfloat16)
            for copy in copies_out(half, n):
                copy.start()
            return carry

        lax.fori_loop(0, tiles, one_tile, 0)
    for half in range(HALVES):

        def end(n, carry):
            for copy in copies_out(half, n):
                copy.wait()
            return carry

        lax.fori_loop(0, tiles, end, 0)


def attend(step, table, queries, stores, weight):
    keys = TILES * BLK
    depth = LOCAL_HEADS * HD
    shape = jax.ShapeDtypeStruct((SPAN // 2, WIDTH), jnp.bfloat16)
    return pl.pallas_call(
        functools.partial(attend_kernel, step),
        out_shape=[shape] * (2 * HALVES),
        in_specs=[SCALARS] + [ANYWHERE] * (1 + len(stores)) + [IN_HBM],
        out_specs=[ANYWHERE] * (2 * HALVES),
        scratch_shapes=[
            pltpu.VMEM((SPAN, LOCAL_HEADS * HD), jnp.bfloat16),
            pltpu.VMEM(((step + 1) * 2 * SPANS, 2, BLK, HD), jnp.bfloat16),
            pltpu.VMEM((BLK, keys), jnp.float32),
            pltpu.VMEM((BLK, keys), jnp.float32),
            pltpu.VMEM((BLK, BLK), jnp.float32),
            pltpu.VMEM((BLK, BLK), jnp.float32),
            pltpu.VMEM((BLK, keys), jnp.bfloat16),
            pltpu.VMEM((BLK, keys), jnp.bfloat16),
            pltpu.VMEM((SPAN, depth), jnp.bfloat16),
            pltpu.VMEM((depth, DW), jnp.bfloat16),
            pltpu.VMEM((SPAN, DW), jnp.bfloat16),
            pltpu.SemaphoreType.DMA((6, WIDTH // TILE)),
        ],
        cost_estimate=pl.CostEstimate(
            flops=2 * SPAN * depth * DW + 4 * PAIRS * TILES * BLK * BLK * HD,
            bytes_accessed=16 * MIB,
            transcendentals=0,
        ),
        compiler_params=pltpu.CompilerParams(vmem_limit_bytes=GRANT),
    )(table, queries, *stores, weight)


def pair_sums(own, other, chips):
    def kernel(own_ref, other_ref, *outs):
        z = lax.axis_index("head") // 2
        for offset in range(chips):
            index = lax.rem(z + offset, chips)
            total = own_ref[index].astype(jnp.float32) + other_ref[index].astype(jnp.float32)
            outs[offset][...] = total.astype(jnp.bfloat16)

    shape = (chips, own.shape[0] // chips, own.shape[1])
    return pl.pallas_call(
        kernel,
        out_shape=[jax.ShapeDtypeStruct(shape[1:], own.dtype)] * chips,
        in_specs=[IN_VMEM] * 2,
        out_specs=[IN_VMEM] * chips,
        cost_estimate=pl.CostEstimate(flops=0, bytes_accessed=3 * MIB, transcendentals=0),
        compiler_params=pltpu.CompilerParams(vmem_limit_bytes=8 * MIB),
    )(own.reshape(shape), other.reshape(shape))


def local(queries, key_rows, value_rows, out_weight, span_owner, vertical_blocks, slash_offsets):
    heads = lax.axis_size("head")
    chips = heads // 2
    head_group = lax.axis_index("head")
    core = lax.rem(head_group, 2)
    kv_head = head_group * LOCAL_HEADS // (QH // KVH)
    swap = core_swap(heads)

    table = make_plan(span_owner, vertical_blocks, slash_offsets)

    weight = pltpu.with_memory_space_constraint(out_weight, pltpu.HBM)
    queries = pltpu.with_memory_space_constraint(queries, pltpu.HBM)

    def own_block(rows):
        return lax.dynamic_slice(rows, (0, core * BLK, kv_head * HD), (STEPS, BLK, HD))

    blocks = jnp.stack([own_block(key_rows), own_block(value_rows)], axis=1)
    stores = []
    streams = {}
    for step in range(STEPS):
        block = jnp.broadcast_to(blocks[step][None], (SPANS, 2, BLK, HD))
        mine = lax.all_to_all(block, "ctx", 0, 0, tiled=True)
        stores += [mine, lax.ppermute(mine, "head", swap)]
        partials = attend(step, table, queries, stores, weight)
        for half in range(HALVES):
            send, own = partials[2 * half : 2 * half + 2]
            got = lax.ppermute(send, "head", swap)
            streams[step, half] = pair_sums(own, got, chips)

    moving = {}
    far = chips // 2

    def hop(step, half, direction, number):
        longest = far if (direction == 1) == (half == 0) else far - 1
        distance = longest - number
        if distance < 1:
            return
        key = (step, half, direction)
        total = streams[step, half][(direction * distance) % chips]
        if key in moving:
            total = total.astype(jnp.float32) + moving[key].astype(jnp.float32)
        total = total.astype(jnp.bfloat16)
        moving[key] = lax.ppermute(total, "head", shift_z(heads, direction))

    for number in range(far):
        for side in (1, -1):
            for half in range(HALVES):
                for step in range(STEPS):
                    hop(step, half, side, number)

    outputs = []
    for step in range(STEPS):
        columns = []
        for half in range(HALVES):
            total = streams[step, half][0].astype(jnp.float32)
            for direction in (1, -1):
                total = total + moving[step, half, direction].astype(jnp.float32)
            columns.append(total.astype(jnp.bfloat16))
        outputs.append(jnp.concatenate(columns, axis=1)[None])
    return jnp.concatenate(outputs)


def solution(mesh):
    in_specs = (
        P(None, "ctx", "head"),
        P(None, "ctx", None),
        P(None, "ctx", None),
        P("head", None),
        P(),
        P(),
        P(),
    )
    out_specs = P(None, ("ctx", "head"), None)

    return jax.shard_map(
        local, mesh=mesh, in_specs=in_specs, out_specs=out_specs, check_vma=False
    )
```

time: 130 us -> 145 us (1.12); the launches traced: 129 us -> 143 us
  waiting for transfers between devices: 13.3 us -> 28.3 us
  blocking collectives: 34.4 us -> 23.1 us
  starting transfers between devices: 46.3 us -> 53.2 us
  local copies, waits for them, and re-layouts: 2.39 us -> 4.56 us
    all_to_all x0 -> x1, waiting for transfers between devices: none -> 15.1 us  [local(): mine = lax.all_to_all(block, 'ctx', 0, 0, tiled=True)]
    all_to_all x1, blocking collectives: 34.4 us -> 23.1 us  [local(): mine = lax.all_to_all(block, 'ctx', 0, 0, tiled=True)]
    all_to_all x0 -> x1, starting transfers between devices: none -> 4.9 us  [local(): mine = lax.all_to_all(block, 'ctx', 0, 0, tiled=True)]
    ppermute x28, starting transfers between devices: 45.5 us -> 47 us  [hop(): moving[key] = lax.ppermute(total, 'head', shift_z(heads, direction))]
    pallas_call x3 -> x2, Pallas kernels: 21.5 us -> 22.2 us  [attend(): pl.pallas_call(functools.partial(attend_kernel, step), out_shape=[shape]...]
  transfers between devices with their start and end apart: 31 -> 35, of which waited for: 9 -> 7; matrix products, arithmetic and copies ran while one was open for 1% -> 2% of each run, Pallas kernels for 12% -> 14%
where the time goes in v3:
time: 145 us; the launch traced here: 143 us
  starting transfers between devices  53.2 us (37%)
  Pallas kernels  31.1 us (21%)
  waiting for transfers between devices  28.3 us (20%)
  blocking collectives  23.1 us (16%)
  local copies, waits for them, and re-layouts  4.56 us (3%)
  other arithmetic  1.8 us (1%)
    ppermute x28, starting transfers between devices, hop(): moving[key] = lax.ppermute(total, 'head', shift_z(heads, direction))  47 us
    all_to_all x1, blocking collectives, local(): mine = lax.all_to_all(block, 'ctx', 0, 0, tiled=True)  23.1 us
    pallas_call x2, Pallas kernels, attend(): pl.pallas_call(functools.partial(attend_kernel, step), out_shape=[shape]...  22.2 us
    all_to_all x1, waiting for transfers between devices, local(): mine = lax.all_to_all(block, 'ctx', 0, 0, tiled=True)  15.1 us
    ppermute x28, waiting for transfers between devices, hop(): moving[key] = lax.ppermute(total, 'head', shift_z(heads, direction))  13.2 us
    pallas_call x1, Pallas kernels, make_plan(): pl.pallas_call(plan_kernel, out_shape=jax.ShapeDtypeStruct((STEPS * PAIRS...  7.92 us
    all_to_all x1, starting transfers between devices, local(): mine = lax.all_to_all(block, 'ctx', 0, 0, tiled=True)  4.9 us
  transfers between devices with their start and end apart: 35, of which 7 were waited for; matrix products, arithmetic and copies ran while one was open for 2% of the time, Pallas kernels for 14%

profile of v3, /device:TPU:2, one launch (start us, length us, event | category | flops | bytes accessed | tf_op | source)
XLA Modules:
  0.0 142.5 jit_solution(2375001396799220784)
XLA Ops:
  1.1 23.1 %all_to_all.10.refs_0_ = bf16[16,2,128,128]{3,2,1,0:T(8,128)(2,1)S(1)} all-to-all(bf16[16,2,128,128]{3,2,1,0:T(8,128)(2,1)S(1)} %broadcast_in_dim.21), channel_id=1, replica_groups=mesh['ctx'=16,'head'=16] {'ctx'}, dimensions={0} | all-to-all | bytes 2097152 | tf_op jit(solution)/shard_map/all_to_all | solution.py:296
  25.4 4.9 %all-to-all-start.1 = ((bf16[16,2,128,128]{3,2,1,0:T(8,128)(2,1)}), bf16[16,2,128,128]{3,2,1,0:T(8,128)(2,1)S(1)}, u32[]{:S(2)}, u32[]{:S(2)}) async-start(bf16[16,2,128,128]{3,2,1,0:T(8,128)(2,1)} %broadcast_in_dim.24), calls=%async_computation.1 | async-start | bytes 2097152 | tf_op jit(solution)/shard_map/all_to_all | solution.py:296
  30.3 15.1 %all-to-all-done.1.refs_2_ = bf16[16,2,128,128]{3,2,1,0:T(8,128)(2,1)S(1)} async-done(((bf16[16,2,128,128]{3,2,1,0:T(8,128)(2,1)}), bf16[16,2,128,128]{3,2,1,0:T(8,128)(2,1)S(1)}, u32[]{:S(2)}, u32[]{:S(2)}) %all-to-all-start.1) | async-done | bytes 1048608 | tf_op jit(solution)/shard_map/all_to_all | solution.py:296
  47.7 7.9 %plan.1.table = s32[144]{0:T(256)S(1)} custom-call(s32[2,16]{1,0:T(2,128)S(1)} %copy-done, s32[64,4]{1,0:T(8,128)S(1)} %copy.8.vertical, s32[64,4]{1,0:T(8,128)S(1)} %copy.9.slash), custom_call_target="tpu_custom_call" | custom-call | tf_op jit(solution)/shard_map/plan/pallas_call | solution.py:87
  55.7 11.3 %shard_map.76 = (bf16[128,4096]{1,0:T(8,128)(2,1)S(1)}, bf16[128,4096]{1,0:T(8,128)(2,1)S(1)}, bf16[128,4096]{1,0:T(8,128)(2,1)S(1)}, bf16[128,4096]{1,0:T(8,128)(2,1)S(1)}) custom-call(s32[144]{0:T(256)S(1)} %plan.1.table, bf16[2,256,512]{2,1,0:T(8,128)(2,1)} %q_hbm.3, bf16[16,2,128,128]{3,2,1,0:T(8,128)(2,1)S(1)} %all_to_all.10.refs_0_, ...), custom_call_target="tpu_custom_call" | custom-call | flops 2751463424 | bytes 16777216 | tf_op jit(solution)/shard_map/pallas_call | solution.py:228
  67.7 10.8 %shard_map.73 = (bf16[128,4096]{1,0:T(8,128)(2,1)S(1)}, bf16[128,4096]{1,0:T(8,128)(2,1)S(1)}, bf16[128,4096]{1,0:T(8,128)(2,1)S(1)}, bf16[128,4096]{1,0:T(8,128)(2,1)S(1)}) custom-call(s32[144]{0:T(256)S(1)} %plan.1.table, bf16[2,256,512]{2,1,0:T(8,128)(2,1)} %q_hbm.3, bf16[16,2,128,128]{3,2,1,0:T(8,128)(2,1)S(1)} %all_to_all.10.refs_0_, ...), custom_call_target="tpu_custom_call" | custom-call | flops 2751463424 | bytes 16777216 | tf_op jit(solution)/shard_map/pallas_call | solution.py:228
  79.4 2.0 %collective-permute-start.19 = (bf16[16,4096]{1,0:T(8,128)(2,1)S(1)}, bf16[16,4096]{1,0:T(8,128)(2,1)S(1)}, u32[]{:S(2)}, u32[]{:S(2)}) collective-permute-start(bf16[16,4096]{1,0:T(8,128)(2,1)S(1)} %get-tuple-element.71), channel_id=1, source_target_pairs={{0,2},{1,3},{2,4},{3,5},{4,6},{5,7},{6,8},{7,9},{8,10},{9,11},{10,... | collective-permute-start | bytes 393224 | tf_op jit(solution)/shard_map/ppermute | solution.py:317
  81.4 4.0 %collective-permute-start.23 = (bf16[16,4096]{1,0:T(8,128)(2,1)S(1)}, bf16[16,4096]{1,0:T(8,128)(2,1)S(1)}, u32[]{:S(2)}, u32[]{:S(2)}) collective-permute-start(bf16[16,4096]{1,0:T(8,128)(2,1)S(1)} %get-tuple-element.74), channel_id=1, source_target_pairs={{0,14},{1,15},{2,0},{3,1},{4,2},{5,3},{6,4},{7,5},{8,6},{9,7},{10,... | collective-permute-start | bytes 393224 | tf_op jit(solution)/shard_map/ppermute | solution.py:317
  85.7 3.2 %collective-permute-start.30 = (bf16[16,4096]{1,0:T(8,128)(2,1)S(1)}, bf16[16,4096]{1,0:T(8,128)(2,1)S(1)}, u32[]{:S(2)}, u32[]{:S(2)}) collective-permute-start(bf16[16,4096]{1,0:T(8,128)(2,1)S(1)} %get-tuple-element.84), channel_id=1, source_target_pairs={{0,14},{1,15},{2,0},{3,1},{4,2},{5,3},{6,4},{7,5},{8,6},{9,7},{10,... | collective-permute-start | bytes 393224 | tf_op jit(solution)/shard_map/ppermute | solution.py:317
  89.8 3.3 %collective-permute-start.6 = (bf16[16,4096]{1,0:T(8,128)(2,1)S(1)}, bf16[16,4096]{1,0:T(8,128)(2,1)S(1)}, u32[]{:S(2)}, u32[]{:S(2)}) collective-permute-start(bf16[16,4096]{1,0:T(8,128)(2,1)S(1)} %get-tuple-element.54), channel_id=1, source_target_pairs={{0,14},{1,15},{2,0},{3,1},{4,2},{5,3},{6,4},{7,5},{8,6},{9,7},{10,... | collective-permute-start | bytes 393224 | tf_op jit(solution)/shard_map/ppermute | solution.py:317
  93.2 3.3 %collective-permute-start.13 = (bf16[16,4096]{1,0:T(8,128)(2,1)S(1)}, bf16[16,4096]{1,0:T(8,128)(2,1)S(1)}, u32[]{:S(2)}, u32[]{:S(2)}) collective-permute-start(bf16[16,4096]{1,0:T(8,128)(2,1)S(1)} %get-tuple-element.64), channel_id=1, source_target_pairs={{0,14},{1,15},{2,0},{3,1},{4,2},{5,3},{6,4},{7,5},{8,6},{9,7},{10,... | collective-permute-start | bytes 393224 | tf_op jit(solution)/shard_map/ppermute | solution.py:317
  96.7 3.3 %collective-permute-start.24 = (bf16[16,4096]{1,0:T(8,128)(2,1)S(1)}, bf16[16,4096]{1,0:T(8,128)(2,1)S(1)}, u32[]{:S(2)}, u32[]{:S(2)}) collective-permute-start(bf16[16,4096]{1,0:T(8,128)(2,1)S(1)} %add_convert_fusion.8), channel_id=1, source_target_pairs={{0,14},{1,15},{2,0},{3,1},{4,2},{5,3},{6,4},{7,5},{8,6},{9,7},{10,... | collective-permute-start | bytes 393224 | tf_op jit(solution)/shard_map/ppermute | solution.py:317
  100.2 3.3 %collective-permute-start.31 = (bf16[16,4096]{1,0:T(8,128)(2,1)S(1)}, bf16[16,4096]{1,0:T(8,128)(2,1)S(1)}, u32[]{:S(2)}, u32[]{:S(2)}) collective-permute-start(bf16[16,4096]{1,0:T(8,128)(2,1)S(1)} %add_convert_fusion.3), channel_id=1, source_target_pairs={{0,14},{1,15},{2,0},{3,1},{4,2},{5,3},{6,4},{7,5},{8,6},{9,7},{10,... | collective-permute-start | bytes 393224 | tf_op jit(solution)/shard_map/ppermute | solution.py:317
  103.8 3.2 %collective-permute-start.7 = (bf16[16,4096]{1,0:T(8,128)(2,1)S(1)}, bf16[16,4096]{1,0:T(8,128)(2,1)S(1)}, u32[]{:S(2)}, u32[]{:S(2)}) collective-permute-start(bf16[16,4096]{1,0:T(8,128)(2,1)S(1)} %add_convert_fusion.20), channel_id=1, source_target_pairs={{0,14},{1,15},{2,0},{3,1},{4,2},{5,3},{6,4},{7,5},{8,6},{9,7},{10,... | collective-permute-start | bytes 393224 | tf_op jit(solution)/shard_map/ppermute | solution.py:317
  107.6 2.9 %collective-permute-start.14 = (bf16[16,4096]{1,0:T(8,128)(2,1)S(1)}, bf16[16,4096]{1,0:T(8,128)(2,1)S(1)}, u32[]{:S(2)}, u32[]{:S(2)}) collective-permute-start(bf16[16,4096]{1,0:T(8,128)(2,1)S(1)} %add_convert_fusion.15), channel_id=1, source_target_pairs={{0,14},{1,15},{2,0},{3,1},{4,2},{5,3},{6,4},{7,5},{8,6},{9,7},{10,... | collective-permute-start | bytes 393224 | tf_op jit(solution)/shard_map/ppermute | solution.py:317
  110.7 3.3 %collective-permute-start.25 = (bf16[16,4096]{1,0:T(8,128)(2,1)S(1)}, bf16[16,4096]{1,0:T(8,128)(2,1)S(1)}, u32[]{:S(2)}, u32[]{:S(2)}) collective-permute-start(bf16[16,4096]{1,0:T(8,128)(2,1)S(1)} %add_convert_fusion.7), channel_id=1, source_target_pairs={{0,14},{1,15},{2,0},{3,1},{4,2},{5,3},{6,4},{7,5},{8,6},{9,7},{10,... | collective-permute-start | bytes 393224 | tf_op jit(solution)/shard_map/ppermute | solution.py:317
  114.1 3.3 %collective-permute-start.32 = (bf16[16,4096]{1,0:T(8,128)(2,1)S(1)}, bf16[16,4096]{1,0:T(8,128)(2,1)S(1)}, u32[]{:S(2)}, u32[]{:S(2)}) collective-permute-start(bf16[16,4096]{1,0:T(8,128)(2,1)S(1)} %add_convert_fusion.2), channel_id=1, source_target_pairs={{0,14},{1,15},{2,0},{3,1},{4,2},{5,3},{6,4},{7,5},{8,6},{9,7},{10,... | collective-permute-start | bytes 393224 | tf_op jit(solution)/shard_map/ppermute | solution.py:317
  117.9 3.3 %collective-permute-start.8 = (bf16[16,4096]{1,0:T(8,128)(2,1)S(1)}, bf16[16,4096]{1,0:T(8,128)(2,1)S(1)}, u32[]{:S(2)}, u32[]{:S(2)}) collective-permute-start(bf16[16,4096]{1,0:T(8,128)(2,1)S(1)} %add_convert_fusion.19), channel_id=1, source_target_pairs={{0,14},{1,15},{2,0},{3,1},{4,2},{5,3},{6,4},{7,5},{8,6},{9,7},{10,... | collective-permute-start | bytes 393224 | tf_op jit(solution)/shard_map/ppermute | solution.py:317
  121.3 2.6 %collective-permute-done.4 = bf16[16,4096]{1,0:T(8,128)(2,1)S(1)} collective-permute-done((bf16[16,4096]{1,0:T(8,128)(2,1)S(1)}, bf16[16,4096]{1,0:T(8,128)(2,1)S(1)}, u32[]{:S(2)}, u32[]{:S(2)}) %collective-permute-start.4) | collective-permute-done | bytes 131104 | tf_op jit(solution)/shard_map/ppermute | solution.py:317
  124.7 4.2 %collective-permute-done.15 = bf16[16,4096]{1,0:T(8,128)(2,1)S(1)} collective-permute-done((bf16[16,4096]{1,0:T(8,128)(2,1)S(1)}, bf16[16,4096]{1,0:T(8,128)(2,1)S(1)}, u32[]{:S(2)}, u32[]{:S(2)}) %collective-permute-start.15) | collective-permute-done | bytes 131104 | tf_op jit(solution)/shard_map/ppermute | solution.py:317
  128.9 2.4 %collective-permute-start.22 = (bf16[16,4096]{1,0:T(8,128)(2,1)S(1)}, bf16[16,4096]{1,0:T(8,128)(2,1)S(1)}, u32[]{:S(2)}, u32[]{:S(2)}) collective-permute-start(bf16[16,4096]{1,0:T(8,128)(2,1)S(1)} %add_convert_fusion.9), channel_id=1, source_target_pairs={{0,2},{1,3},{2,4},{3,5},{4,6},{5,7},{6,8},{7,9},{8,10},{9,11},{10,... | collective-permute-start | bytes 393224 | tf_op jit(solution)/shard_map/ppermute | solution.py:317
  132.3 3.0 %collective-permute-done.22 = bf16[16,4096]{1,0:T(8,128)(2,1)S(1)} collective-permute-done((bf16[16,4096]{1,0:T(8,128)(2,1)S(1)}, bf16[16,4096]{1,0:T(8,128)(2,1)S(1)}, u32[]{:S(2)}, u32[]{:S(2)}) %collective-permute-start.22) | collective-permute-done | bytes 131104 | tf_op jit(solution)/shard_map/ppermute | solution.py:317
  136.4 2.3 %collective-permute-start.16 = (bf16[16,4096]{1,0:T(8,128)(2,1)S(1)}, bf16[16,4096]{1,0:T(8,128)(2,1)S(1)}, u32[]{:S(2)}, u32[]{:S(2)}) collective-permute-start(bf16[16,4096]{1,0:T(8,128)(2,1)S(1)} %add_convert_fusion.13), channel_id=1, source_target_pairs={{0,14},{1,15},{2,0},{3,1},{4,2},{5,3},{6,4},{7,5},{8,6},{9,7},{10,... | collective-permute-start | bytes 393224 | tf_op jit(solution)/shard_map/ppermute | solution.py:317
  138.8 2.7 %collective-permute-done.5 = bf16[16,4096]{1,0:T(8,128)(2,1)S(1)} collective-permute-done((bf16[16,4096]{1,0:T(8,128)(2,1)S(1)}, bf16[16,4096]{1,0:T(8,128)(2,1)S(1)}, u32[]{:S(2)}, u32[]{:S(2)}) %collective-permute-start.5) | collective-permute-done | bytes 131104 | tf_op jit(solution)/shard_map/ppermute | solution.py:317
  (89 shorter events, 13.2 us)
Async XLA Ops:
  25.4 20.0 %all-to-all-start.1 = ((bf16[16,2,128,128]{3,2,1,0:T(8,128)(2,1)}), bf16[16,2,128,128]{3,2,1,0:T(8,128)(2,1)S(1)}, u32[]{:S(2)}, u32[]{:S(2)}) async-start(bf16[16,2,128,128]{3,2,1,0:T(8,128)(2,1)} %broadcast_in_dim.24), calls=%async_computation.1 | async-start | bytes 2097152 | tf_op jit(solution)/shard_map/all_to_all | solution.py:296
  30.3 25.3 %collective-permute-start = (bf16[16,2,128,128]{3,2,1,0:T(8,128)(2,1)S(1)}, bf16[16,2,128,128]{3,2,1,0:T(8,128)(2,1)S(1)}, u32[]{:S(2)}, u32[]{:S(2)}) collective-permute-start(bf16[16,2,128,128]{3,2,1,0:T(8,128)(2,1)S(1)} %all_to_all.10.refs_0_), channel_id=1, source_target_pairs={{0,1},{1,0},{2,3},{3,2},{4,5},{5,4},{6,7},{7,6},{8,9},{9,8},{10,11... | collective-permute-start | bytes 3145736 | tf_op jit(solution)/shard_map/ppermute | solution.py:297
  45.5 10.2 %collective-permute-start.17 = (bf16[16,2,128,128]{3,2,1,0:T(8,128)(2,1)S(1)}, bf16[16,2,128,128]{3,2,1,0:T(8,128)(2,1)}, u32[]{:S(2)}, u32[]{:S(2)}) collective-permute-start(bf16[16,2,128,128]{3,2,1,0:T(8,128)(2,1)S(1)} %all-to-all-done.1.refs_2_), channel_id=1, source_target_pairs={{0,1},{1,0},{2,3},{3,2},{4,5},{5,4},{6,7},{7,6},{8,9},{9,8},{10,11... | collective-permute-start | bytes 3145736 | tf_op jit(solution)/shard_map/ppermute | solution.py:297
  67.0 12.1 %collective-permute-start.18 = (bf16[128,4096]{1,0:T(8,128)(2,1)S(1)}, bf16[128,4096]{1,0:T(8,128)(2,1)S(1)}, u32[]{:S(2)}, u32[]{:S(2)}) collective-permute-start(bf16[128,4096]{1,0:T(8,128)(2,1)S(1)} %get-tuple-element.66), channel_id=1, source_target_pairs={{0,1},{1,0},{2,3},{3,2},{4,5},{5,4},{6,7},{7,6},{8,9},{9,8},{10,11... | collective-permute-start | bytes 3145736 | tf_op jit(solution)/shard_map/ppermute | solution.py:301
  67.6 17.8 %collective-permute-start.26 = (bf16[128,4096]{1,0:T(8,128)(2,1)S(1)}, bf16[128,4096]{1,0:T(8,128)(2,1)S(1)}, u32[]{:S(2)}, u32[]{:S(2)}) collective-permute-start(bf16[128,4096]{1,0:T(8,128)(2,1)S(1)} %get-tuple-element.76), channel_id=1, source_target_pairs={{0,1},{1,0},{2,3},{3,2},{4,5},{5,4},{6,7},{7,6},{8,9},{9,8},{10,11... | collective-permute-start | bytes 3145736 | tf_op jit(solution)/shard_map/ppermute | solution.py:301
  79.0 10.2 %collective-permute-start.9 = (bf16[128,4096]{1,0:T(8,128)(2,1)S(1)}, bf16[128,4096]{1,0:T(8,128)(2,1)S(1)}, u32[]{:S(2)}, u32[]{:S(2)}) collective-permute-start(bf16[128,4096]{1,0:T(8,128)(2,1)S(1)} %get-tuple-element.56), channel_id=1, source_target_pairs={{0,1},{1,0},{2,3},{3,2},{4,5},{5,4},{6,7},{7,6},{8,9},{9,8},{10,11... | collective-permute-start | bytes 3145736 | tf_op jit(solution)/shard_map/ppermute | solution.py:301
  79.4 10.4 %collective-permute-start.19 = (bf16[16,4096]{1,0:T(8,128)(2,1)S(1)}, bf16[16,4096]{1,0:T(8,128)(2,1)S(1)}, u32[]{:S(2)}, u32[]{:S(2)}) collective-permute-start(bf16[16,4096]{1,0:T(8,128)(2,1)S(1)} %get-tuple-element.71), channel_id=1, source_target_pairs={{0,2},{1,3},{2,4},{3,5},{4,6},{5,7},{6,8},{7,9},{8,10},{9,11},{10,... | collective-permute-start | bytes 393224 | tf_op jit(solution)/shard_map/ppermute | solution.py:317
  81.4 11.7 %collective-permute-start.23 = (bf16[16,4096]{1,0:T(8,128)(2,1)S(1)}, bf16[16,4096]{1,0:T(8,128)(2,1)S(1)}, u32[]{:S(2)}, u32[]{:S(2)}) collective-permute-start(bf16[16,4096]{1,0:T(8,128)(2,1)S(1)} %get-tuple-element.74), channel_id=1, source_target_pairs={{0,14},{1,15},{2,0},{3,1},{4,2},{5,3},{6,4},{7,5},{8,6},{9,7},{10,... | collective-permute-start | bytes 393224 | tf_op jit(solution)/shard_map/ppermute | solution.py:317
  85.6 7.6 %collective-permute-start.27 = (bf16[16,4096]{1,0:T(8,128)(2,1)S(1)}, bf16[16,4096]{1,0:T(8,128)(2,1)S(1)}, u32[]{:S(2)}, u32[]{:S(2)}) collective-permute-start(bf16[16,4096]{1,0:T(8,128)(2,1)S(1)} %get-tuple-element.80), channel_id=1, source_target_pairs={{0,2},{1,3},{2,4},{3,5},{4,6},{5,7},{6,8},{7,9},{8,10},{9,11},{10,... | collective-permute-start | bytes 393224 | tf_op jit(solution)/shard_map/ppermute | solution.py:317
  85.7 10.8 %collective-permute-start.30 = (bf16[16,4096]{1,0:T(8,128)(2,1)S(1)}, bf16[16,4096]{1,0:T(8,128)(2,1)S(1)}, u32[]{:S(2)}, u32[]{:S(2)}) collective-permute-start(bf16[16,4096]{1,0:T(8,128)(2,1)S(1)} %get-tuple-element.84), channel_id=1, source_target_pairs={{0,14},{1,15},{2,0},{3,1},{4,2},{5,3},{6,4},{7,5},{8,6},{9,7},{10,... | collective-permute-start | bytes 393224 | tf_op jit(solution)/shard_map/ppermute | solution.py:317
  89.2 7.5 %collective-permute-start.2 = (bf16[16,4096]{1,0:T(8,128)(2,1)S(1)}, bf16[16,4096]{1,0:T(8,128)(2,1)S(1)}, u32[]{:S(2)}, u32[]{:S(2)}) collective-permute-start(bf16[16,4096]{1,0:T(8,128)(2,1)S(1)} %get-tuple-element.51), channel_id=1, source_target_pairs={{0,2},{1,3},{2,4},{3,5},{4,6},{5,7},{6,8},{7,9},{8,10},{9,11},{10,... | collective-permute-start | bytes 393224 | tf_op jit(solution)/shard_map/ppermute | solution.py:317
  89.8 10.3 %collective-permute-start.6 = (bf16[16,4096]{1,0:T(8,128)(2,1)S(1)}, bf16[16,4096]{1,0:T(8,128)(2,1)S(1)}, u32[]{:S(2)}, u32[]{:S(2)}) collective-permute-start(bf16[16,4096]{1,0:T(8,128)(2,1)S(1)} %get-tuple-element.54), channel_id=1, source_target_pairs={{0,14},{1,15},{2,0},{3,1},{4,2},{5,3},{6,4},{7,5},{8,6},{9,7},{10,... | collective-permute-start | bytes 393224 | tf_op jit(solution)/shard_map/ppermute | solution.py:317
  93.2 10.3 %collective-permute-start.13 = (bf16[16,4096]{1,0:T(8,128)(2,1)S(1)}, bf16[16,4096]{1,0:T(8,128)(2,1)S(1)}, u32[]{:S(2)}, u32[]{:S(2)}) collective-permute-start(bf16[16,4096]{1,0:T(8,128)(2,1)S(1)} %get-tuple-element.64), channel_id=1, source_target_pairs={{0,14},{1,15},{2,0},{3,1},{4,2},{5,3},{6,4},{7,5},{8,6},{9,7},{10,... | collective-permute-start | bytes 393224 | tf_op jit(solution)/shard_map/ppermute | solution.py:317
  96.7 10.3 %collective-permute-start.24 = (bf16[16,4096]{1,0:T(8,128)(2,1)S(1)}, bf16[16,4096]{1,0:T(8,128)(2,1)S(1)}, u32[]{:S(2)}, u32[]{:S(2)}) collective-permute-start(bf16[16,4096]{1,0:T(8,128)(2,1)S(1)} %add_convert_fusion.8), channel_id=1, source_target_pairs={{0,14},{1,15},{2,0},{3,1},{4,2},{5,3},{6,4},{7,5},{8,6},{9,7},{10,... | collective-permute-start | bytes 393224 | tf_op jit(solution)/shard_map/ppermute | solution.py:317
  100.1 7.5 %collective-permute-start.28 = (bf16[16,4096]{1,0:T(8,128)(2,1)S(1)}, bf16[16,4096]{1,0:T(8,128)(2,1)S(1)}, u32[]{:S(2)}, u32[]{:S(2)}) collective-permute-start(bf16[16,4096]{1,0:T(8,128)(2,1)S(1)} %add_convert_fusion.5), channel_id=1, source_target_pairs={{0,2},{1,3},{2,4},{3,5},{4,6},{5,7},{6,8},{7,9},{8,10},{9,11},{10,... | collective-permute-start | bytes 393224 | tf_op jit(solution)/shard_map/ppermute | solution.py:317
  100.2 10.3 %collective-permute-start.31 = (bf16[16,4096]{1,0:T(8,128)(2,1)S(1)}, bf16[16,4096]{1,0:T(8,128)(2,1)S(1)}, u32[]{:S(2)}, u32[]{:S(2)}) collective-permute-start(bf16[16,4096]{1,0:T(8,128)(2,1)S(1)} %add_convert_fusion.3), channel_id=1, source_target_pairs={{0,14},{1,15},{2,0},{3,1},{4,2},{5,3},{6,4},{7,5},{8,6},{9,7},{10,... | collective-permute-start | bytes 393224 | tf_op jit(solution)/shard_map/ppermute | solution.py:317
  103.8 10.2 %collective-permute-start.7 = (bf16[16,4096]{1,0:T(8,128)(2,1)S(1)}, bf16[16,4096]{1,0:T(8,128)(2,1)S(1)}, u32[]{:S(2)}, u32[]{:S(2)}) collective-permute-start(bf16[16,4096]{1,0:T(8,128)(2,1)S(1)} %add_convert_fusion.20), channel_id=1, source_target_pairs={{0,14},{1,15},{2,0},{3,1},{4,2},{5,3},{6,4},{7,5},{8,6},{9,7},{10,... | collective-permute-start | bytes 393224 | tf_op jit(solution)/shard_map/ppermute | solution.py:317
  107.6 9.9 %collective-permute-start.14 = (bf16[16,4096]{1,0:T(8,128)(2,1)S(1)}, bf16[16,4096]{1,0:T(8,128)(2,1)S(1)}, u32[]{:S(2)}, u32[]{:S(2)}) collective-permute-start(bf16[16,4096]{1,0:T(8,128)(2,1)S(1)} %add_convert_fusion.15), channel_id=1, source_target_pairs={{0,14},{1,15},{2,0},{3,1},{4,2},{5,3},{6,4},{7,5},{8,6},{9,7},{10,... | collective-permute-start | bytes 393224 | tf_op jit(solution)/shard_map/ppermute | solution.py:317
  110.5 7.3 %collective-permute-start.21 = (bf16[16,4096]{1,0:T(8,128)(2,1)S(1)}, bf16[16,4096]{1,0:T(8,128)(2,1)S(1)}, u32[]{:S(2)}, u32[]{:S(2)}) collective-permute-start(bf16[16,4096]{1,0:T(8,128)(2,1)S(1)} %add_convert_fusion.10), channel_id=1, source_target_pairs={{0,2},{1,3},{2,4},{3,5},{4,6},{5,7},{6,8},{7,9},{8,10},{9,11},{10,... | collective-permute-start | bytes 393224 | tf_op jit(solution)/shard_map/ppermute | solution.py:317
  110.7 20.8 %collective-permute-start.25 = (bf16[16,4096]{1,0:T(8,128)(2,1)S(1)}, bf16[16,4096]{1,0:T(8,128)(2,1)S(1)}, u32[]{:S(2)}, u32[]{:S(2)}) collective-permute-start(bf16[16,4096]{1,0:T(8,128)(2,1)S(1)} %add_convert_fusion.7), channel_id=1, source_target_pairs={{0,14},{1,15},{2,0},{3,1},{4,2},{5,3},{6,4},{7,5},{8,6},{9,7},{10,... | collective-permute-start | bytes 393224 | tf_op jit(solution)/shard_map/ppermute | solution.py:317
  114.0 22.4 %collective-permute-start.29 = (bf16[16,4096]{1,0:T(8,128)(2,1)S(1)}, bf16[16,4096]{1,0:T(8,128)(2,1)S(1)}, u32[]{:S(2)}, u32[]{:S(2)}) collective-permute-start(bf16[16,4096]{1,0:T(8,128)(2,1)S(1)} %add_convert_fusion.4), channel_id=1, source_target_pairs={{0,2},{1,3},{2,4},{3,5},{4,6},{5,7},{6,8},{7,9},{8,10},{9,11},{10,... | collective-permute-start | bytes 393224 | tf_op jit(solution)/shard_map/ppermute | solution.py:317
  117.9 20.9 %collective-permute-start.8 = (bf16[16,4096]{1,0:T(8,128)(2,1)S(1)}, bf16[16,4096]{1,0:T(8,128)(2,1)S(1)}, u32[]{:S(2)}, u32[]{:S(2)}) collective-permute-start(bf16[16,4096]{1,0:T(8,128)(2,1)S(1)} %add_convert_fusion.19), channel_id=1, source_target_pairs={{0,14},{1,15},{2,0},{3,1},{4,2},{5,3},{6,4},{7,5},{8,6},{9,7},{10,... | collective-permute-start | bytes 393224 | tf_op jit(solution)/shard_map/ppermute | solution.py:317
  121.2 20.4 %collective-permute-start.12 = (bf16[16,4096]{1,0:T(8,128)(2,1)S(1)}, bf16[16,4096]{1,0:T(8,128)(2,1)S(1)}, u32[]{:S(2)}, u32[]{:S(2)}) collective-permute-start(bf16[16,4096]{1,0:T(8,128)(2,1)S(1)} %add_convert_fusion.16), channel_id=1, source_target_pairs={{0,2},{1,3},{2,4},{3,5},{4,6},{5,7},{6,8},{7,9},{8,10},{9,11},{10,... | collective-permute-start | bytes 393224 | tf_op jit(solution)/shard_map/ppermute | solution.py:317
  131.4 7.3 %collective-permute-start.33 = (bf16[16,4096]{1,0:T(8,128)(2,1)S(1)}, bf16[16,4096]{1,0:T(8,128)(2,1)S(1)}, u32[]{:S(2)}, u32[]{:S(2)}) collective-permute-start(bf16[16,4096]{1,0:T(8,128)(2,1)S(1)} %add_convert_fusion.1), channel_id=1, source_target_pairs={{0,14},{1,15},{2,0},{3,1},{4,2},{5,3},{6,4},{7,5},{8,6},{9,7},{10,... | collective-permute-start | bytes 393224 | tf_op jit(solution)/shard_map/ppermute | solution.py:317
  (12 other events, 72.7 us)

commit v4 on v3

--- a/solution.py
+++ b/solution.py
@@ -97,9 +97,11 @@
 def attend_kernel(step, table, q_hbm, *refs):
     stores = refs[: 2 * (step + 1)]
     w_hbm = refs[2 * (step + 1)]
-    targets, scratch = refs[-16:-12], refs[-12:]
+    targets, scratch = refs[-14:-12], refs[-12:]
     q_v, kv_v, s_0, s_1, m_0, m_1, p_0, p_1, out, w_v, out_v, all_sems = scratch
     sems, w_sems, out_sems = all_sems.at[0], all_sems.at[1], all_sems.at[2:]
+    depth = LOCAL_HEADS * HD
+    w_parts = 8
     core = lax.rem(lax.axis_index("head"), 2)
 
     copies = [pltpu.make_async_copy(q_hbm.at[step], q_v, sems.at[0])]
@@ -110,11 +112,9 @@
             pltpu.make_async_copy(store, kv_v.at[pl.ds(start, SPANS)], sems.at[1 + index])
         )
     w_copies = []
-    for half in range(HALVES):
-        cols = pl.ds(half * WIDTH, WIDTH)
-        w_copies.append(
-            pltpu.make_async_copy(w_hbm.at[:, cols], w_v.at[:, cols], w_sems.at[half])
-        )
+    for part in range(w_parts):
+        rows = pl.ds(part * (depth // w_parts), depth // w_parts)
+        w_copies.append(pltpu.make_async_copy(w_hbm.at[rows], w_v.at[rows], w_sems.at[part]))
     for copy in copies + w_copies:
         copy.start()
     for copy in copies:
@@ -185,51 +185,49 @@
 
     lax.fori_loop(0, PAIRS // 2, two_pairs, 0)
 
-    def copies_out(half, n):
-        source = pl.ds(pl.multiple_of(half * WIDTH + n * TILE, TILE), TILE)
+    def copies_out(n):
         cols = pl.ds(pl.multiple_of(n * TILE, TILE), TILE)
         return [
             pltpu.make_async_copy(
-                out_v.at[pl.ds(side * (SPAN // 2), SPAN // 2), source],
-                targets[half * 2 + side].at[:, cols],
-                out_sems.at[half * 2 + side, n],
+                out_v.at[pl.ds(side * (SPAN // 2), SPAN // 2), cols],
+                targets[side].at[:, cols],
+                out_sems.at[side, n],
             )
             for side in range(2)
         ]
 
-    tiles = WIDTH // TILE
-    for half in range(HALVES):
-        w_copies[half].wait()
-
-        def one_tile(n, carry):
-            cols = pl.ds(pl.multiple_of(half * WIDTH + n * TILE, TILE), TILE)
-            out_v[:, cols] = jnp.dot(
-                out[...], w_v[:, cols], preferred_element_type=jnp.float32
-            ).astype(jnp.bfloat16)
-            for copy in copies_out(half, n):
-                copy.start()
-            return carry
-
-        lax.fori_loop(0, tiles, one_tile, 0)
-    for half in range(HALVES):
-
-        def end(n, carry):
-            for copy in copies_out(half, n):
-                copy.wait()
-            return carry
-
-        lax.fori_loop(0, tiles, end, 0)
+    tiles = DW // TILE
+    for copy in w_copies:
+        copy.wait()
+
+    def one_tile(n, carry):
+        cols = pl.ds(pl.multiple_of(n * TILE, TILE), TILE)
+        out_v[:, cols] = jnp.dot(
+            out[...], w_v[:, cols], preferred_element_type=jnp.float32
+        ).astype(jnp.bfloat16)
+        for copy in copies_out(n):
+            copy.start()
+        return carry
+
+    lax.fori_loop(0, tiles, one_tile, 0)
+
+    def end(n, carry):
+        for copy in copies_out(n):
+            copy.wait()
+        return carry
+
+    lax.fori_loop(0, tiles, end, 0)
 
 
 def attend(step, table, queries, stores, weight):
     keys = TILES * BLK
     depth = LOCAL_HEADS * HD
-    shape = jax.ShapeDtypeStruct((SPAN // 2, WIDTH), jnp.bfloat16)
+    shape = pltpu.HBM((SPAN // 2, DW), jnp.bfloat16)
     return pl.pallas_call(
         functools.partial(attend_kernel, step),
-        out_shape=[shape] * (2 * HALVES),
+        out_shape=[shape] * 2,
         in_specs=[SCALARS] + [ANYWHERE] * (1 + len(stores)) + [IN_HBM],
-        out_specs=[ANYWHERE] * (2 * HALVES),
+        out_specs=[IN_HBM] * 2,
         scratch_shapes=[
             pltpu.VMEM((SPAN, LOCAL_HEADS * HD), jnp.bfloat16),
             pltpu.VMEM(((step + 1) * 2 * SPANS, 2, BLK, HD), jnp.bfloat16),
@@ -242,7 +240,7 @@
             pltpu.VMEM((SPAN, depth), jnp.bfloat16),
             pltpu.VMEM((depth, DW), jnp.bfloat16),
             pltpu.VMEM((SPAN, DW), jnp.bfloat16),
-            pltpu.SemaphoreType.DMA((6, WIDTH // TILE)),
+            pltpu.SemaphoreType.DMA((4, DW // TILE)),
         ],
         cost_estimate=pl.CostEstimate(
             flops=2 * SPAN * depth * DW + 4 * PAIRS * TILES * BLK * BLK * HD,
@@ -253,23 +251,75 @@
     )(table, queries, *stores, weight)
 
 
+def waves(chips):
+    far = chips // 2
+    plan = []
+    for number in range(far):
+        for direction in (1, -1):
+            distances = []
+            for half in range(HALVES):
+                longest = far if (direction == 1) == (half == 0) else far - 1
+                if number < longest:
+                    distances.append((half, direction * (longest - number)))
+            plan.append((number, direction, distances))
+    plan.append((far, 0, [(half, 0) for half in range(HALVES)]))
+    return plan
+
+
 def pair_sums(own, other, chips):
-    def kernel(own_ref, other_ref, *outs):
+    plan = waves(chips)
+    near = 2
+
+    def kernel(own_ref, other_ref, *refs):
+        outs = refs[: len(plan)]
+        rest, sems = refs[len(plan) :]
         z = lax.axis_index("head") // 2
-        for offset in range(chips):
-            index = lax.rem(z + offset, chips)
-            total = own_ref[index].astype(jnp.float32) + other_ref[index].astype(jnp.float32)
-            outs[offset][...] = total.astype(jnp.bfloat16)
+        copies = []
+        row = 0
+        for entry, (number, direction, distances) in enumerate(plan):
+            for slot, (half, distance) in enumerate(distances):
+                index = lax.rem(z + distance + chips, chips)
+                cols = slice(half * WIDTH, (half + 1) * WIDTH)
+                total = own_ref[index, :, cols].astype(jnp.float32)
+                total = total + other_ref[index, :, cols].astype(jnp.float32)
+                total = total.astype(jnp.bfloat16)
+                if entry < near:
+                    outs[entry][slot] = total
+                else:
+                    rest[row + slot] = total
+            if entry >= near:
+                copies.append(
+                    pltpu.make_async_copy(
+                        rest.at[pl.ds(row, len(distances))], outs[entry], sems.at[entry]
+                    )
+                )
+                copies[-1].start()
+                row += len(distances)
+        for copy in copies:
+            copy.wait()
 
     shape = (chips, own.shape[0] // chips, own.shape[1])
-    return pl.pallas_call(
+    out_shape = []
+    for entry, (number, direction, distances) in enumerate(plan):
+        piece = (len(distances), shape[1], WIDTH)
+        if entry < near:
+            out_shape.append(jax.ShapeDtypeStruct(piece, own.dtype))
+        else:
+            out_shape.append(pltpu.HBM(piece, own.dtype))
+    later = sum(len(distances) for _, _, distances in plan[near:])
+    sums = pl.pallas_call(
         kernel,
-        out_shape=[jax.ShapeDtypeStruct(shape[1:], own.dtype)] * chips,
+        out_shape=out_shape,
         in_specs=[IN_VMEM] * 2,
-        out_specs=[IN_VMEM] * chips,
-        cost_estimate=pl.CostEstimate(flops=0, bytes_accessed=3 * MIB, transcendentals=0),
-        compiler_params=pltpu.CompilerParams(vmem_limit_bytes=8 * MIB),
+        out_specs=[IN_VMEM] * near + [IN_HBM] * (len(plan) - near),
+        scratch_shapes=[
+            pltpu.VMEM((later, shape[1], WIDTH), own.dtype),
+            pltpu.SemaphoreType.DMA((len(plan),)),
+        ],
+        cost_estimate=pl.CostEstimate(flops=0, bytes_accessed=6 * MIB, transcendentals=0),
+        compiler_params=pltpu.CompilerParams(vmem_limit_bytes=12 * MIB),
     )(own.reshape(shape), other.reshape(shape))
+    return {(number, direction): value for (number, direction, _), value in zip(plan, sums)}
 
 
 def local(queries, key_rows, value_rows, out_weight, span_owner, vertical_blocks, slash_offsets):
@@ -295,40 +345,40 @@
         block = jnp.broadcast_to(blocks[step][None], (SPANS, 2, BLK, HD))
         mine = lax.all_to_all(block, "ctx", 0, 0, tiled=True)
         stores += [mine, lax.ppermute(mine, "head", swap)]
-        partials = attend(step, table, queries, stores, weight)
-        for half in range(HALVES):
-            send, own = partials[2 * half : 2 * half + 2]
-            got = lax.ppermute(send, "head", swap)
-            streams[step, half] = pair_sums(own, got, chips)
-
+        send, own = attend(step, table, queries, stores, weight)
+        got = lax.ppermute(send, "head", swap)
+        streams[step] = pair_sums(own, got, chips)
+
+    far = chips // 2
     moving = {}
-    far = chips // 2
-
-    def hop(step, half, direction, number):
-        longest = far if (direction == 1) == (half == 0) else far - 1
-        distance = longest - number
-        if distance < 1:
-            return
-        key = (step, half, direction)
-        total = streams[step, half][(direction * distance) % chips]
-        if key in moving:
-            total = total.astype(jnp.float32) + moving[key].astype(jnp.float32)
-        total = total.astype(jnp.bfloat16)
-        moving[key] = lax.ppermute(total, "head", shift_z(heads, direction))
-
     for number in range(far):
-        for side in (1, -1):
-            for half in range(HALVES):
-                for step in range(STEPS):
-                    hop(step, half, side, number)
+        for step in range(STEPS):
+            for direction in (1, -1):
+                total = streams[step][number, direction]
+                if number > 0:
+                    before = moving[step, number - 1, direction]
+                    if total.shape[0] < before.shape[0]:
+                        keep = 0 if direction == 1 else 1
+                        moving[step, "ended", direction] = before[1 - keep]
+                        before = before[keep : keep + 1]
+                    total = total.astype(jnp.float32) + before.astype(jnp.float32)
+                    total = total.astype(jnp.bfloat16)
+                moving[step, number, direction] = lax.ppermute(
+                    total, "head", shift_z(heads, direction)
+                )
 
     outputs = []
     for step in range(STEPS):
+        last = far - 1
+        arrived = (
+            (moving[step, last, 1][0], moving[step, "ended", -1]),
+            (moving[step, "ended", 1], moving[step, last, -1][0]),
+        )
         columns = []
         for half in range(HALVES):
-            total = streams[step, half][0].astype(jnp.float32)
-            for direction in (1, -1):
-                total = total + moving[step, half, direction].astype(jnp.float32)
+            total = streams[step][far, 0][half].astype(jnp.float32)
+            for value in arrived[half]:
+                total = total + value.astype(jnp.float32)
             columns.append(total.astype(jnp.bfloat16))
         outputs.append(jnp.concatenate(columns, axis=1)[None])
     return jnp.concatenate(outputs)

time: 145 us -> 129 us (0.89)
  starting transfers between devices: 53.2 us -> 35.3 us
  local copies, waits for them, and re-layouts: 4.56 us -> 2.62 us
  Pallas kernels: 31.1 us -> 32.9 us
  waiting for transfers between devices: 28.3 us -> 29.9 us
    ppermute x28 -> x16, starting transfers between devices: 47 us -> 29.7 us  [local(): lax.ppermute(total, 'head', shift_z(heads, direction))]
    unnamed x4 -> x38, local copies, waits for them, and re-layouts: 2.22 us -> 0.26 us
    pallas_call x4 -> x2, Pallas kernels: 0.98 us -> 2.64 us  [pair_sums(): pl.pallas_call(kernel, out_shape=out_shape, in_specs=[IN_VMEM] * 2, out_s...]
    ppermute x28 -> x16, waiting for transfers between devices: 13.2 us -> 14.7 us  [local(): lax.ppermute(total, 'head', shift_z(heads, direction))]
  transfers between devices with their start and end apart: 35 -> 21, of which waited for: 7 -> 8; matrix products, arithmetic and copies ran while one was open for 2% -> 1% of each run, Pallas kernels for 14% -> 17%
where the time goes in v4:
time: 129 us; the launch traced here: 127 us
  starting transfers between devices  35.3 us (27%)
  Pallas kernels  32.9 us (26%)
  waiting for transfers between devices  29.9 us (23%)
  blocking collectives  23.1 us (18%)
  other arithmetic  2.69 us (2%)
  local copies, waits for them, and re-layouts  2.62 us (2%)
    ppermute x16, starting transfers between devices, local(): lax.ppermute(total, 'head', shift_z(heads, direction))  29.7 us
    all_to_all x1, blocking collectives, local(): mine = lax.all_to_all(block, 'ctx', 0, 0, tiled=True)  23.1 us
    pallas_call x2, Pallas kernels, attend(): pl.pallas_call(functools.partial(attend_kernel, step), out_shape=[shape]...  22.3 us
    all_to_all x1, waiting for transfers between devices, local(): mine = lax.all_to_all(block, 'ctx', 0, 0, tiled=True)  15.1 us
    ppermute x16, waiting for transfers between devices, local(): lax.ppermute(total, 'head', shift_z(heads, direction))  14.7 us
    pallas_call x1, Pallas kernels, make_plan(): pl.pallas_call(plan_kernel, out_shape=jax.ShapeDtypeStruct((STEPS * PAIRS...  7.92 us
    all_to_all x1, starting transfers between devices, local(): mine = lax.all_to_all(block, 'ctx', 0, 0, tiled=True)  4.9 us
    pallas_call x2, Pallas kernels, pair_sums(): pl.pallas_call(kernel, out_shape=out_shape, in_specs=[IN_VMEM] * 2, out_s...  2.64 us
  transfers between devices with their start and end apart: 21, of which 8 were waited for; matrix products, arithmetic and copies ran while one was open for 1% of the time, Pallas kernels for 17%

profile of v4, /device:TPU:2, one launch (start us, length us, event | category | flops | bytes accessed | tf_op | source)
XLA Modules:
  0.0 127.0 jit_solution(4317055330462632866)
XLA Ops:
  1.1 23.1 %all_to_all.10.refs_0_ = bf16[16,2,128,128]{3,2,1,0:T(8,128)(2,1)S(1)} all-to-all(bf16[16,2,128,128]{3,2,1,0:T(8,128)(2,1)S(1)} %broadcast_in_dim.21), channel_id=1, replica_groups=mesh['ctx'=16,'head'=16] {'ctx'}, dimensions={0} | all-to-all | bytes 2097152 | tf_op jit(solution)/shard_map/all_to_all | solution.py:346
  24.2 1.2 broadcast_in_dim.24
  25.5 4.9 %all-to-all-start.1 = ((bf16[16,2,128,128]{3,2,1,0:T(8,128)(2,1)}), bf16[16,2,128,128]{3,2,1,0:T(8,128)(2,1)S(1)}, u32[]{:S(2)}, u32[]{:S(2)}) async-start(bf16[16,2,128,128]{3,2,1,0:T(8,128)(2,1)} %broadcast_in_dim.24), calls=%async_computation.1 | async-start | bytes 2097152 | tf_op jit(solution)/shard_map/all_to_all | solution.py:346
  30.4 15.1 %all-to-all-done.1.refs_2_ = bf16[16,2,128,128]{3,2,1,0:T(8,128)(2,1)S(1)} async-done(((bf16[16,2,128,128]{3,2,1,0:T(8,128)(2,1)}), bf16[16,2,128,128]{3,2,1,0:T(8,128)(2,1)S(1)}, u32[]{:S(2)}, u32[]{:S(2)}) %all-to-all-start.1) | async-done | bytes 1048608 | tf_op jit(solution)/shard_map/all_to_all | solution.py:346
  45.7 7.9 %plan.1.table = s32[144]{0:T(256)S(1)} custom-call(s32[2,16]{1,0:T(2,128)S(1)} %copy-done.2, s32[64,4]{1,0:T(8,128)S(1)} %copy.8.vertical, s32[64,4]{1,0:T(8,128)S(1)} %copy.9.slash), custom_call_target="tpu_custom_call" | custom-call | tf_op jit(solution)/shard_map/plan/pallas_call | solution.py:87
  53.7 11.5 %shard_map.75 = (bf16[128,8192]{1,0:T(8,128)(2,1)}, bf16[128,8192]{1,0:T(8,128)(2,1)}) custom-call(s32[144]{0:T(256)S(1)} %plan.1.table, bf16[2,256,512]{2,1,0:T(8,128)(2,1)} %q_hbm.3, bf16[16,2,128,128]{3,2,1,0:T(8,128)(2,1)S(1)} %all_to_all.10.refs_0_, bf16[16,2,128,128]{3,2,1,0:T(8,128)(2,1)S(1)} %collective-permute-done.refs_1_, ...), custom_call_target="tpu_custom_call" | custom-call | flops 2751463424 | bytes 16777216 | tf_op jit(solution)/shard_map/pallas_call | solution.py:226
  65.7 10.9 %shard_map.73 = (bf16[128,8192]{1,0:T(8,128)(2,1)}, bf16[128,8192]{1,0:T(8,128)(2,1)}) custom-call(s32[144]{0:T(256)S(1)} %plan.1.table, bf16[2,256,512]{2,1,0:T(8,128)(2,1)} %q_hbm.3, bf16[16,2,128,128]{3,2,1,0:T(8,128)(2,1)S(1)} %all_to_all.10.refs_0_, bf16[16,2,128,128]{3,2,1,0:T(8,128)(2,1)S(1)} %collective-permute-done.refs_1_, bf16[512,8192]{1,0:T(8,128)(2,1)} %refs_4_.1), custom_call_target="tpu_custom_call" | custom-call | flops 2751463424 | bytes 16777216 | tf_op jit(solution)/shard_map/pallas_call | solution.py:226
  76.8 1.3 %shard_map.76 = (bf16[2,16,4096]{2,1,0:T(8,128)(2,1)S(1)}, bf16[2,16,4096]{2,1,0:T(8,128)(2,1)S(1)}, bf16[2,16,4096]{2,1,0:T(8,128)(2,1)}, bf16[2,16,4096]{2,1,0...) custom-call(bf16[8,16,8192]{2,1,0:T(8,128)(2,1)S(1)} %bitcast.26, ...), custom_call_target="tpu_custom_call" | custom-call | bytes 6291456 | tf_op jit(solution)/shard_map/pallas_call | solution.py:310
  78.1 2.0 %collective-permute-start.12 = (bf16[2,16,4096]{2,1,0:T(8,128)(2,1)S(1)}, bf16[2,16,4096]{2,1,0:T(8,128)(2,1)S(1)}, u32[]{:S(2)}, u32[]{:S(2)}) collective-permute-start(bf16[2,16,4096]{2,1,0:T(8,128)(2,1)S(1)} %get-tuple-element.44), channel_id=1, source_target_pairs={{0,2},{1,3},{2,4},{3,5},{4,6},{5,7},{6,8},{7,9},{8,10},{9,11},{10,... | collective-permute-start | bytes 786440 | tf_op jit(solution)/shard_map/ppermute | solution.py:366
  80.1 4.0 %collective-permute-start.16 = (bf16[2,16,4096]{2,1,0:T(8,128)(2,1)S(1)}, bf16[2,16,4096]{2,1,0:T(8,128)(2,1)S(1)}, u32[]{:S(2)}, u32[]{:S(2)}) collective-permute-start(bf16[2,16,4096]{2,1,0:T(8,128)(2,1)S(1)} %get-tuple-element.47), channel_id=1, source_target_pairs={{0,14},{1,15},{2,0},{3,1},{4,2},{5,3},{6,4},{7,5},{8,6},{9,7},{10,... | collective-permute-start | bytes 786440 | tf_op jit(solution)/shard_map/ppermute | solution.py:366
  84.1 1.3 %shard_map.74 = (bf16[2,16,4096]{2,1,0:T(8,128)(2,1)S(1)}, bf16[2,16,4096]{2,1,0:T(8,128)(2,1)S(1)}, bf16[2,16,4096]{2,1,0:T(8,128)(2,1)}, bf16[2,16,4096]{2,1,0...) custom-call(bf16[8,16,8192]{2,1,0:T(8,128)(2,1)S(1)} %bitcast.24, ...), custom_call_target="tpu_custom_call" | custom-call | bytes 6291456 | tf_op jit(solution)/shard_map/pallas_call | solution.py:310
  85.6 3.2 %collective-permute-start.6 = (bf16[2,16,4096]{2,1,0:T(8,128)(2,1)S(1)}, bf16[2,16,4096]{2,1,0:T(8,128)(2,1)S(1)}, u32[]{:S(2)}, u32[]{:S(2)}) collective-permute-start(bf16[2,16,4096]{2,1,0:T(8,128)(2,1)S(1)} %get-tuple-element.36), channel_id=1, source_target_pairs={{0,14},{1,15},{2,0},{3,1},{4,2},{5,3},{6,4},{7,5},{8,6},{9,7},{10,... | collective-permute-start | bytes 786440 | tf_op jit(solution)/shard_map/ppermute | solution.py:366
  88.8 2.4 %collective-permute-done.12 = bf16[2,16,4096]{2,1,0:T(8,128)(2,1)S(1)} collective-permute-done((bf16[2,16,4096]{2,1,0:T(8,128)(2,1)S(1)}, bf16[2,16,4096]{2,1,0:T(8,128)(2,1)S(1)}, u32[]{:S(2)}, u32[]{:S(2)}) %collective-permute-start.12) | collective-permute-done | bytes 262176 | tf_op jit(solution)/shard_map/ppermute | solution.py:366
  91.4 3.3 %collective-permute-start.17 = (bf16[2,16,4096]{2,1,0:T(8,128)(2,1)S(1)}, bf16[2,16,4096]{2,1,0:T(8,128)(2,1)S(1)}, u32[]{:S(2)}, u32[]{:S(2)}) collective-permute-start(bf16[2,16,4096]{2,1,0:T(8,128)(2,1)S(1)} %add_convert_fusion.1), channel_id=1, source_target_pairs={{0,14},{1,15},{2,0},{3,1},{4,2},{5,3},{6,4},{7,5},{8,6},{9,7},{10,... | collective-permute-start | bytes 786440 | tf_op jit(solution)/shard_map/ppermute | solution.py:366
  94.7 2.1 %collective-permute-done.2 = bf16[2,16,4096]{2,1,0:T(8,128)(2,1)S(1)} collective-permute-done((bf16[2,16,4096]{2,1,0:T(8,128)(2,1)S(1)}, bf16[2,16,4096]{2,1,0:T(8,128)(2,1)S(1)}, u32[]{:S(2)}, u32[]{:S(2)}) %collective-permute-start.2) | collective-permute-done | bytes 262176 | tf_op jit(solution)/shard_map/ppermute | solution.py:366
  98.2 3.3 %collective-permute-start.7 = (bf16[2,16,4096]{2,1,0:T(8,128)(2,1)S(1)}, bf16[2,16,4096]{2,1,0:T(8,128)(2,1)S(1)}, u32[]{:S(2)}, u32[]{:S(2)}) collective-permute-start(bf16[2,16,4096]{2,1,0:T(8,128)(2,1)S(1)} %add_convert_fusion.5), channel_id=1, source_target_pairs={{0,14},{1,15},{2,0},{3,1},{4,2},{5,3},{6,4},{7,5},{8,6},{9,7},{10,... | collective-permute-start | bytes 786440 | tf_op jit(solution)/shard_map/ppermute | solution.py:366
  102.7 3.3 %collective-permute-start.18 = (bf16[2,16,4096]{2,1,0:T(8,128)(2,1)S(1)}, bf16[2,16,4096]{2,1,0:T(8,128)(2,1)S(1)}, u32[]{:S(2)}, u32[]{:S(2)}) collective-permute-start(bf16[2,16,4096]{2,1,0:T(8,128)(2,1)S(1)} %add_convert_fusion), channel_id=1, source_target_pairs={{0,14},{1,15},{2,0},{3,1},{4,2},{5,3},{6,4},{7,5},{8,6},{9,7},{10,... | collective-permute-start | bytes 786440 | tf_op jit(solution)/shard_map/ppermute | solution.py:366
  105.9 2.5 %collective-permute-done.3 = bf16[2,16,4096]{2,1,0:T(8,128)(2,1)S(1)} collective-permute-done((bf16[2,16,4096]{2,1,0:T(8,128)(2,1)S(1)}, bf16[2,16,4096]{2,1,0:T(8,128)(2,1)S(1)}, u32[]{:S(2)}, u32[]{:S(2)}) %collective-permute-start.3) | collective-permute-done | bytes 262176 | tf_op jit(solution)/shard_map/ppermute | solution.py:366
  108.7 3.3 %collective-permute-start.8 = (bf16[2,16,4096]{2,1,0:T(8,128)(2,1)S(1)}, bf16[2,16,4096]{2,1,0:T(8,128)(2,1)S(1)}, u32[]{:S(2)}, u32[]{:S(2)}) collective-permute-start(bf16[2,16,4096]{2,1,0:T(8,128)(2,1)S(1)} %add_convert_fusion.4), channel_id=1, source_target_pairs={{0,14},{1,15},{2,0},{3,1},{4,2},{5,3},{6,4},{7,5},{8,6},{9,7},{10,... | collective-permute-start | bytes 786440 | tf_op jit(solution)/shard_map/ppermute | solution.py:366
  112.0 2.1 %collective-permute-done.14 = bf16[2,16,4096]{2,1,0:T(8,128)(2,1)S(1)} collective-permute-done((bf16[2,16,4096]{2,1,0:T(8,128)(2,1)S(1)}, bf16[2,16,4096]{2,1,0:T(8,128)(2,1)S(1)}, u32[]{:S(2)}, u32[]{:S(2)}) %collective-permute-start.14) | collective-permute-done | bytes 262176 | tf_op jit(solution)/shard_map/ppermute | solution.py:366
  114.3 3.3 %collective-permute-start.19 = (bf16[1,16,4096]{2,1,0:T(8,128)(2,1)S(1)}, bf16[1,16,4096]{2,1,0:T(8,128)(2,1)S(1)}, u32[]{:S(2)}, u32[]{:S(2)}) collective-permute-start(bf16[1,16,4096]{2,1,0:T(8,128)(2,1)S(1)} %add_convert_fusion.9), channel_id=1, source_target_pairs={{0,14},{1,15},{2,0},{3,1},{4,2},{5,3},{6,4},{7,5},{8,6},{9,7},{10,... | collective-permute-start | bytes 393224 | tf_op jit(solution)/shard_map/ppermute | solution.py:366
  117.6 2.1 %collective-permute-done.4 = bf16[2,16,4096]{2,1,0:T(8,128)(2,1)S(1)} collective-permute-done((bf16[2,16,4096]{2,1,0:T(8,128)(2,1)S(1)}, bf16[2,16,4096]{2,1,0:T(8,128)(2,1)S(1)}, u32[]{:S(2)}, u32[]{:S(2)}) %collective-permute-start.4) | collective-permute-done | bytes 262176 | tf_op jit(solution)/shard_map/ppermute | solution.py:366
  119.9 3.3 %collective-permute-start.9 = (bf16[1,16,4096]{2,1,0:T(8,128)(2,1)S(1)}, bf16[1,16,4096]{2,1,0:T(8,128)(2,1)S(1)}, u32[]{:S(2)}, u32[]{:S(2)}) collective-permute-start(bf16[1,16,4096]{2,1,0:T(8,128)(2,1)S(1)} %add_convert_fusion.13), channel_id=1, source_target_pairs={{0,14},{1,15},{2,0},{3,1},{4,2},{5,3},{6,4},{7,5},{8,6},{9,7},{10,... | collective-permute-start | bytes 393224 | tf_op jit(solution)/shard_map/ppermute | solution.py:366
  123.3 2.6 %collective-permute-done.5 = bf16[1,16,4096]{2,1,0:T(8,128)(2,1)S(1)} collective-permute-done((bf16[1,16,4096]{2,1,0:T(8,128)(2,1)S(1)}, bf16[1,16,4096]{2,1,0:T(8,128)(2,1)S(1)}, u32[]{:S(2)}, u32[]{:S(2)}) %collective-permute-start.5) | collective-permute-done | bytes 131104 | tf_op jit(solution)/shard_map/ppermute | solution.py:366
  (83 shorter events, 6.5 us)
Async XLA Ops:
  24.2 21.4 %copy-start.17 = (s32[64,4]{0,1:T(4,128)S(1)}, s32[64,4]{0,1:T(4,128)}, u32[]{:S(2)}) copy-start(s32[64,4]{0,1:T(4,128)} %param.13) | copy-start | bytes 3076
  24.2 21.5 %copy-start.2 = (s32[2,16]{1,0:T(2,128)S(1)}, s32[2,16]{1,0:T(2,128)}, u32[]{:S(2)}) copy-start(s32[2,16]{1,0:T(2,128)} %owner.1) | copy-start | bytes 388
  25.5 20.0 %all-to-all-start.1 = ((bf16[16,2,128,128]{3,2,1,0:T(8,128)(2,1)}), bf16[16,2,128,128]{3,2,1,0:T(8,128)(2,1)S(1)}, u32[]{:S(2)}, u32[]{:S(2)}) async-start(bf16[16,2,128,128]{3,2,1,0:T(8,128)(2,1)} %broadcast_in_dim.24), calls=%async_computation.1 | async-start | bytes 2097152 | tf_op jit(solution)/shard_map/all_to_all | solution.py:346
  30.4 23.3 %collective-permute-start = (bf16[16,2,128,128]{3,2,1,0:T(8,128)(2,1)S(1)}, bf16[16,2,128,128]{3,2,1,0:T(8,128)(2,1)S(1)}, u32[]{:S(2)}, u32[]{:S(2)}) collective-permute-start(bf16[16,2,128,128]{3,2,1,0:T(8,128)(2,1)S(1)} %all_to_all.10.refs_0_), channel_id=1, source_target_pairs={{0,1},{1,0},{2,3},{3,2},{4,5},{5,4},{6,7},{7,6},{8,9},{9,8},{10,11... | collective-permute-start | bytes 3145736 | tf_op jit(solution)/shard_map/ppermute | solution.py:347
  45.5 8.1 %collective-permute-start.10 = (bf16[16,2,128,128]{3,2,1,0:T(8,128)(2,1)S(1)}, bf16[16,2,128,128]{3,2,1,0:T(8,128)(2,1)}, u32[]{:S(2)}, u32[]{:S(2)}) collective-permute-start(bf16[16,2,128,128]{3,2,1,0:T(8,128)(2,1)S(1)} %all-to-all-done.1.refs_2_), channel_id=1, source_target_pairs={{0,1},{1,0},{2,3},{3,2},{4,5},{5,4},{6,7},{7,6},{8,9},{9,8},{10,11... | collective-permute-start | bytes 3145736 | tf_op jit(solution)/shard_map/ppermute | solution.py:347
  65.1 11.6 %collective-permute-start.11 = (bf16[128,8192]{1,0:T(8,128)(2,1)}, bf16[128,8192]{1,0:T(8,128)(2,1)S(1)}, u32[]{:S(2)}, u32[]{:S(2)}) collective-permute-start(bf16[128,8192]{1,0:T(8,128)(2,1)} %get-tuple-element.39), channel_id=1, source_target_pairs={{0,1},{1,0},{2,3},{3,2},{4,5},{5,4},{6,7},{7,6},{8,9},{9,8},{10,11... | collective-permute-start | bytes 6291464 | tf_op jit(solution)/shard_map/ppermute | solution.py:349
  76.6 7.5 %collective-permute-start.1 = (bf16[128,8192]{1,0:T(8,128)(2,1)}, bf16[128,8192]{1,0:T(8,128)(2,1)S(1)}, u32[]{:S(2)}, u32[]{:S(2)}) collective-permute-start(bf16[128,8192]{1,0:T(8,128)(2,1)} %get-tuple-element.28), channel_id=1, source_target_pairs={{0,1},{1,0},{2,3},{3,2},{4,5},{5,4},{6,7},{7,6},{8,9},{9,8},{10,11... | collective-permute-start | bytes 6291464 | tf_op jit(solution)/shard_map/ppermute | solution.py:349
  78.1 13.1 %collective-permute-start.12 = (bf16[2,16,4096]{2,1,0:T(8,128)(2,1)S(1)}, bf16[2,16,4096]{2,1,0:T(8,128)(2,1)S(1)}, u32[]{:S(2)}, u32[]{:S(2)}) collective-permute-start(bf16[2,16,4096]{2,1,0:T(8,128)(2,1)S(1)} %get-tuple-element.44), channel_id=1, source_target_pairs={{0,2},{1,3},{2,4},{3,5},{4,6},{5,7},{6,8},{7,9},{8,10},{9,11},{10,... | collective-permute-start | bytes 786440 | tf_op jit(solution)/shard_map/ppermute | solution.py:366
  80.1 11.3 %collective-permute-start.16 = (bf16[2,16,4096]{2,1,0:T(8,128)(2,1)S(1)}, bf16[2,16,4096]{2,1,0:T(8,128)(2,1)S(1)}, u32[]{:S(2)}, u32[]{:S(2)}) collective-permute-start(bf16[2,16,4096]{2,1,0:T(8,128)(2,1)S(1)} %get-tuple-element.47), channel_id=1, source_target_pairs={{0,14},{1,15},{2,0},{3,1},{4,2},{5,3},{6,4},{7,5},{8,6},{9,7},{10,... | collective-permute-start | bytes 786440 | tf_op jit(solution)/shard_map/ppermute | solution.py:366
  85.5 11.3 %collective-permute-start.2 = (bf16[2,16,4096]{2,1,0:T(8,128)(2,1)S(1)}, bf16[2,16,4096]{2,1,0:T(8,128)(2,1)S(1)}, u32[]{:S(2)}, u32[]{:S(2)}) collective-permute-start(bf16[2,16,4096]{2,1,0:T(8,128)(2,1)S(1)} %get-tuple-element.33), channel_id=1, source_target_pairs={{0,2},{1,3},{2,4},{3,5},{4,6},{5,7},{6,8},{7,9},{8,10},{9,11},{10,... | collective-permute-start | bytes 786440 | tf_op jit(solution)/shard_map/ppermute | solution.py:366
  85.6 12.5 %collective-permute-start.6 = (bf16[2,16,4096]{2,1,0:T(8,128)(2,1)S(1)}, bf16[2,16,4096]{2,1,0:T(8,128)(2,1)S(1)}, u32[]{:S(2)}, u32[]{:S(2)}) collective-permute-start(bf16[2,16,4096]{2,1,0:T(8,128)(2,1)S(1)} %get-tuple-element.36), channel_id=1, source_target_pairs={{0,14},{1,15},{2,0},{3,1},{4,2},{5,3},{6,4},{7,5},{8,6},{9,7},{10,... | collective-permute-start | bytes 786440 | tf_op jit(solution)/shard_map/ppermute | solution.py:366
  91.2 11.2 %collective-permute-start.13 = (bf16[2,16,4096]{2,1,0:T(8,128)(2,1)S(1)}, bf16[2,16,4096]{2,1,0:T(8,128)(2,1)S(1)}, u32[]{:S(2)}, u32[]{:S(2)}) collective-permute-start(bf16[2,16,4096]{2,1,0:T(8,128)(2,1)S(1)} %add_convert_fusion.3), channel_id=1, source_target_pairs={{0,2},{1,3},{2,4},{3,5},{4,6},{5,7},{6,8},{7,9},{8,10},{9,11},{10,... | collective-permute-start | bytes 786440 | tf_op jit(solution)/shard_map/ppermute | solution.py:366
  91.4 11.1 %collective-permute-start.17 = (bf16[2,16,4096]{2,1,0:T(8,128)(2,1)S(1)}, bf16[2,16,4096]{2,1,0:T(8,128)(2,1)S(1)}, u32[]{:S(2)}, u32[]{:S(2)}) collective-permute-start(bf16[2,16,4096]{2,1,0:T(8,128)(2,1)S(1)} %add_convert_fusion.1), channel_id=1, source_target_pairs={{0,14},{1,15},{2,0},{3,1},{4,2},{5,3},{6,4},{7,5},{8,6},{9,7},{10,... | collective-permute-start | bytes 786440 | tf_op jit(solution)/shard_map/ppermute | solution.py:366
  97.8 10.6 %collective-permute-start.3 = (bf16[2,16,4096]{2,1,0:T(8,128)(2,1)S(1)}, bf16[2,16,4096]{2,1,0:T(8,128)(2,1)S(1)}, u32[]{:S(2)}, u32[]{:S(2)}) collective-permute-start(bf16[2,16,4096]{2,1,0:T(8,128)(2,1)S(1)} %add_convert_fusion.7), channel_id=1, source_target_pairs={{0,2},{1,3},{2,4},{3,5},{4,6},{5,7},{6,8},{7,9},{8,10},{9,11},{10,... | collective-permute-start | bytes 786440 | tf_op jit(solution)/shard_map/ppermute | solution.py:366
  98.2 21.5 %copy-start.15 = (bf16[1,16,4096]{2,1,0:T(8,128)(2,1)S(1)}, bf16[1,16,4096]{2,1,0:T(8,128)(2,1)}, u32[]{:S(2)}) copy-start(bf16[1,16,4096]{2,1,0:T(8,128)(2,1)} %get-tuple-element.30) | copy-start | bytes 393220
  98.2 10.4 %collective-permute-start.7 = (bf16[2,16,4096]{2,1,0:T(8,128)(2,1)S(1)}, bf16[2,16,4096]{2,1,0:T(8,128)(2,1)S(1)}, u32[]{:S(2)}, u32[]{:S(2)}) collective-permute-start(bf16[2,16,4096]{2,1,0:T(8,128)(2,1)S(1)} %add_convert_fusion.5), channel_id=1, source_target_pairs={{0,14},{1,15},{2,0},{3,1},{4,2},{5,3},{6,4},{7,5},{8,6},{9,7},{10,... | collective-permute-start | bytes 786440 | tf_op jit(solution)/shard_map/ppermute | solution.py:366
  102.5 11.6 %collective-permute-start.14 = (bf16[2,16,4096]{2,1,0:T(8,128)(2,1)S(1)}, bf16[2,16,4096]{2,1,0:T(8,128)(2,1)S(1)}, u32[]{:S(2)}, u32[]{:S(2)}) collective-permute-start(bf16[2,16,4096]{2,1,0:T(8,128)(2,1)S(1)} %add_convert_fusion.2), channel_id=1, source_target_pairs={{0,2},{1,3},{2,4},{3,5},{4,6},{5,7},{6,8},{7,9},{8,10},{9,11},{10,... | collective-permute-start | bytes 786440 | tf_op jit(solution)/shard_map/ppermute | solution.py:366
  102.7 11.5 %collective-permute-start.18 = (bf16[2,16,4096]{2,1,0:T(8,128)(2,1)S(1)}, bf16[2,16,4096]{2,1,0:T(8,128)(2,1)S(1)}, u32[]{:S(2)}, u32[]{:S(2)}) collective-permute-start(bf16[2,16,4096]{2,1,0:T(8,128)(2,1)S(1)} %add_convert_fusion), channel_id=1, source_target_pairs={{0,14},{1,15},{2,0},{3,1},{4,2},{5,3},{6,4},{7,5},{8,6},{9,7},{10,... | collective-permute-start | bytes 786440 | tf_op jit(solution)/shard_map/ppermute | solution.py:366
  108.5 11.2 %collective-permute-start.4 = (bf16[2,16,4096]{2,1,0:T(8,128)(2,1)S(1)}, bf16[2,16,4096]{2,1,0:T(8,128)(2,1)S(1)}, u32[]{:S(2)}, u32[]{:S(2)}) collective-permute-start(bf16[2,16,4096]{2,1,0:T(8,128)(2,1)S(1)} %add_convert_fusion.6), channel_id=1, source_target_pairs={{0,2},{1,3},{2,4},{3,5},{4,6},{5,7},{6,8},{7,9},{8,10},{9,11},{10,... | collective-permute-start | bytes 786440 | tf_op jit(solution)/shard_map/ppermute | solution.py:366
  108.7 11.1 %collective-permute-start.8 = (bf16[2,16,4096]{2,1,0:T(8,128)(2,1)S(1)}, bf16[2,16,4096]{2,1,0:T(8,128)(2,1)S(1)}, u32[]{:S(2)}, u32[]{:S(2)}) collective-permute-start(bf16[2,16,4096]{2,1,0:T(8,128)(2,1)S(1)} %add_convert_fusion.4), channel_id=1, source_target_pairs={{0,14},{1,15},{2,0},{3,1},{4,2},{5,3},{6,4},{7,5},{8,6},{9,7},{10,... | collective-permute-start | bytes 786440 | tf_op jit(solution)/shard_map/ppermute | solution.py:366
  114.1 9.1 %collective-permute-start.15 = (bf16[1,16,4096]{2,1,0:T(8,128)(2,1)S(1)}, bf16[1,16,4096]{2,1,0:T(8,128)(2,1)S(1)}, u32[]{:S(2)}, u32[]{:S(2)}) collective-permute-start(bf16[1,16,4096]{2,1,0:T(8,128)(2,1)S(1)} %add_convert_fusion.11), channel_id=1, source_target_pairs={{0,2},{1,3},{2,4},{3,5},{4,6},{5,7},{6,8},{7,9},{8,10},{9,11},{10,... | collective-permute-start | bytes 393224 | tf_op jit(solution)/shard_map/ppermute | solution.py:366
  114.3 8.9 %collective-permute-start.19 = (bf16[1,16,4096]{2,1,0:T(8,128)(2,1)S(1)}, bf16[1,16,4096]{2,1,0:T(8,128)(2,1)S(1)}, u32[]{:S(2)}, u32[]{:S(2)}) collective-permute-start(bf16[1,16,4096]{2,1,0:T(8,128)(2,1)S(1)} %add_convert_fusion.9), channel_id=1, source_target_pairs={{0,14},{1,15},{2,0},{3,1},{4,2},{5,3},{6,4},{7,5},{8,6},{9,7},{10,... | collective-permute-start | bytes 393224 | tf_op jit(solution)/shard_map/ppermute | solution.py:366
  119.7 6.3 %collective-permute-start.5 = (bf16[1,16,4096]{2,1,0:T(8,128)(2,1)S(1)}, bf16[1,16,4096]{2,1,0:T(8,128)(2,1)S(1)}, u32[]{:S(2)}, u32[]{:S(2)}) collective-permute-start(bf16[1,16,4096]{2,1,0:T(8,128)(2,1)S(1)} %add_convert_fusion.15), channel_id=1, source_target_pairs={{0,2},{1,3},{2,4},{3,5},{4,6},{5,7},{6,8},{7,9},{8,10},{9,11},{10,... | collective-permute-start | bytes 393224 | tf_op jit(solution)/shard_map/ppermute | solution.py:366
  119.9 6.1 %collective-permute-start.9 = (bf16[1,16,4096]{2,1,0:T(8,128)(2,1)S(1)}, bf16[1,16,4096]{2,1,0:T(8,128)(2,1)S(1)}, u32[]{:S(2)}, u32[]{:S(2)}) collective-permute-start(bf16[1,16,4096]{2,1,0:T(8,128)(2,1)S(1)} %add_convert_fusion.13), channel_id=1, source_target_pairs={{0,14},{1,15},{2,0},{3,1},{4,2},{5,3},{6,4},{7,5},{8,6},{9,7},{10,... | collective-permute-start | bytes 393224 | tf_op jit(solution)/shard_map/ppermute | solution.py:366
  (15 other events, 223.7 us)

commit v5 on v4

--- a/solution.py
+++ b/solution.py
@@ -94,14 +94,17 @@
     )(owner, vertical, slash)
 
 
-def attend_kernel(step, table, q_hbm, *refs):
+def attend_kernel(step, joined, table, q_hbm, *refs):
     stores = refs[: 2 * (step + 1)]
-    w_hbm = refs[2 * (step + 1)]
-    targets, scratch = refs[-14:-12], refs[-12:]
-    q_v, kv_v, s_0, s_1, m_0, m_1, p_0, p_1, out, w_v, out_v, all_sems = scratch
-    sems, w_sems, out_sems = all_sems.at[0], all_sems.at[1], all_sems.at[2:]
+    if joined:
+        w_hbm = refs[2 * (step + 1)]
+        targets, scratch = refs[-14:-12], refs[-12:]
+        q_v, kv_v, s_0, s_1, m_0, m_1, p_0, p_1, out, w_v, out_v, all_sems = scratch
+    else:
+        out, q_v, kv_v, s_0, s_1, m_0, m_1, p_0, p_1, all_sems = refs[-10:]
+    sems = all_sems.at[0]
     depth = LOCAL_HEADS * HD
-    w_parts = 8
+    w_parts = 8 if joined else 0
     core = lax.rem(lax.axis_index("head"), 2)
 
     copies = [pltpu.make_async_copy(q_hbm.at[step], q_v, sems.at[0])]
@@ -114,7 +117,7 @@
     w_copies = []
     for part in range(w_parts):
         rows = pl.ds(part * (depth // w_parts), depth // w_parts)
-        w_copies.append(pltpu.make_async_copy(w_hbm.at[rows], w_v.at[rows], w_sems.at[part]))
+        w_copies.append(pltpu.make_async_copy(w_hbm.at[rows], w_v.at[rows], all_sems.at[1, part]))
     for copy in copies + w_copies:
         copy.start()
     for copy in copies:
@@ -185,6 +188,14 @@
 
     lax.fori_loop(0, PAIRS // 2, two_pairs, 0)
 
+    if not joined:
+        return
+    for copy in w_copies:
+        copy.wait()
+    project_tiles(out, w_v, out_v, targets, all_sems.at[2:], lambda n: None)
+
+
+def project_tiles(left, w_v, out_v, targets, out_sems, ready):
     def copies_out(n):
         cols = pl.ds(pl.multiple_of(n * TILE, TILE), TILE)
         return [
@@ -197,13 +208,12 @@
         ]
 
     tiles = DW // TILE
-    for copy in w_copies:
-        copy.wait()
 
     def one_tile(n, carry):
         cols = pl.ds(pl.multiple_of(n * TILE, TILE), TILE)
+        ready(n)
         out_v[:, cols] = jnp.dot(
-            out[...], w_v[:, cols], preferred_element_type=jnp.float32
+            left[...], w_v[:, cols], preferred_element_type=jnp.float32
         ).astype(jnp.bfloat16)
         for copy in copies_out(n):
             copy.start()
@@ -219,36 +229,76 @@
     lax.fori_loop(0, tiles, end, 0)
 
 
+def project_kernel(attended, w_hbm, send, own, w_v, out_v, sems):
+    def copy_in(n):
+        cols = pl.ds(pl.multiple_of(n * TILE, TILE), TILE)
+        return pltpu.make_async_copy(w_hbm.at[:, cols], w_v.at[:, cols], sems.at[0, n])
+
+    for n in range(DW // TILE):
+        copy_in(n).start()
+    project_tiles(attended, w_v, out_v, (send, own), sems.at[1:], lambda n: copy_in(n).wait())
+
+
+def project(attended, weight):
+    depth = LOCAL_HEADS * HD
+    shape = pltpu.HBM((SPAN // 2, DW), jnp.bfloat16)
+    return pl.pallas_call(
+        project_kernel,
+        out_shape=[shape] * 2,
+        in_specs=[IN_VMEM, IN_HBM],
+        out_specs=[IN_HBM] * 2,
+        scratch_shapes=[
+            pltpu.VMEM((depth, DW), jnp.bfloat16),
+            pltpu.VMEM((SPAN, DW), jnp.bfloat16),
+            pltpu.SemaphoreType.DMA((3, DW // TILE)),
+        ],
+        cost_estimate=pl.CostEstimate(
+            flops=2 * SPAN * depth * DW, bytes_accessed=12 * MIB, transcendentals=0
+        ),
+        compiler_params=pltpu.CompilerParams(vmem_limit_bytes=GRANT),
+    )(attended, weight)
+
+
 def attend(step, table, queries, stores, weight):
     keys = TILES * BLK
     depth = LOCAL_HEADS * HD
-    shape = pltpu.HBM((SPAN // 2, DW), jnp.bfloat16)
-    return pl.pallas_call(
-        functools.partial(attend_kernel, step),
-        out_shape=[shape] * 2,
-        in_specs=[SCALARS] + [ANYWHERE] * (1 + len(stores)) + [IN_HBM],
-        out_specs=[IN_HBM] * 2,
-        scratch_shapes=[
-            pltpu.VMEM((SPAN, LOCAL_HEADS * HD), jnp.bfloat16),
-            pltpu.VMEM(((step + 1) * 2 * SPANS, 2, BLK, HD), jnp.bfloat16),
-            pltpu.VMEM((BLK, keys), jnp.float32),
-            pltpu.VMEM((BLK, keys), jnp.float32),
-            pltpu.VMEM((BLK, BLK), jnp.float32),
-            pltpu.VMEM((BLK, BLK), jnp.float32),
-            pltpu.VMEM((BLK, keys), jnp.bfloat16),
-            pltpu.VMEM((BLK, keys), jnp.bfloat16),
+    joined = weight is not None
+    scratch = [
+        pltpu.VMEM((SPAN, depth), jnp.bfloat16),
+        pltpu.VMEM(((step + 1) * 2 * SPANS, 2, BLK, HD), jnp.bfloat16),
+        pltpu.VMEM((BLK, keys), jnp.float32),
+        pltpu.VMEM((BLK, keys), jnp.float32),
+        pltpu.VMEM((BLK, BLK), jnp.float32),
+        pltpu.VMEM((BLK, BLK), jnp.float32),
+        pltpu.VMEM((BLK, keys), jnp.bfloat16),
+        pltpu.VMEM((BLK, keys), jnp.bfloat16),
+    ]
+    flops = 4 * PAIRS * TILES * BLK * BLK * HD
+    if joined:
+        scratch += [
             pltpu.VMEM((SPAN, depth), jnp.bfloat16),
             pltpu.VMEM((depth, DW), jnp.bfloat16),
             pltpu.VMEM((SPAN, DW), jnp.bfloat16),
-            pltpu.SemaphoreType.DMA((4, DW // TILE)),
-        ],
+        ]
+        out_shape = [pltpu.HBM((SPAN // 2, DW), jnp.bfloat16)] * 2
+        out_specs = [IN_HBM] * 2
+        flops += 2 * SPAN * depth * DW
+    else:
+        out_shape = jax.ShapeDtypeStruct((SPAN, depth), jnp.bfloat16)
+        out_specs = IN_VMEM
+    scratch.append(pltpu.SemaphoreType.DMA((4, DW // TILE)))
+    extra = [weight] if joined else []
+    return pl.pallas_call(
+        functools.partial(attend_kernel, step, joined),
+        out_shape=out_shape,
+        in_specs=[SCALARS] + [ANYWHERE] * (1 + len(stores)) + [IN_HBM] * len(extra),
+        out_specs=out_specs,
+        scratch_shapes=scratch,
         cost_estimate=pl.CostEstimate(
-            flops=2 * SPAN * depth * DW + 4 * PAIRS * TILES * BLK * BLK * HD,
-            bytes_accessed=16 * MIB,
-            transcendentals=0,
+            flops=flops, bytes_accessed=16 * MIB, transcendentals=0
         ),
         compiler_params=pltpu.CompilerParams(vmem_limit_bytes=GRANT),
-    )(table, queries, *stores, weight)
+    )(table, queries, *stores, *extra)
 
 
 def waves(chips):
@@ -270,17 +320,34 @@
     plan = waves(chips)
     near = 2
 
-    def kernel(own_ref, other_ref, *refs):
+    def kernel(own_hbm, other_ref, *refs):
         outs = refs[: len(plan)]
-        rest, sems = refs[len(plan) :]
+        rest, own_ref, sems = refs[len(plan) :]
         z = lax.axis_index("head") // 2
         copies = []
         row = 0
+        moves = [
+            [
+                pltpu.make_async_copy(
+                    own_hbm.at[
+                        lax.rem(z + distance + chips, chips), :, pl.ds(half * WIDTH, WIDTH)
+                    ],
+                    own_ref.at[entry, slot],
+                    sems.at[1, HALVES * entry + slot],
+                )
+                for slot, (half, distance) in enumerate(distances)
+            ]
+            for entry, (number, direction, distances) in enumerate(plan)
+        ]
+        for entry_moves in moves:
+            for move in entry_moves:
+                move.start()
         for entry, (number, direction, distances) in enumerate(plan):
             for slot, (half, distance) in enumerate(distances):
                 index = lax.rem(z + distance + chips, chips)
                 cols = slice(half * WIDTH, (half + 1) * WIDTH)
-                total = own_ref[index, :, cols].astype(jnp.float32)
+                moves[entry][slot].wait()
+                total = own_ref[entry, slot].astype(jnp.float32)
                 total = total + other_ref[index, :, cols].astype(jnp.float32)
                 total = total.astype(jnp.bfloat16)
                 if entry < near:
@@ -290,7 +357,7 @@
             if entry >= near:
                 copies.append(
                     pltpu.make_async_copy(
-                        rest.at[pl.ds(row, len(distances))], outs[entry], sems.at[entry]
+                        rest.at[pl.ds(row, len(distances))], outs[entry], sems.at[0, entry]
                     )
                 )
                 copies[-1].start()
@@ -310,15 +377,16 @@
     sums = pl.pallas_call(
         kernel,
         out_shape=out_shape,
-        in_specs=[IN_VMEM] * 2,
+        in_specs=[IN_HBM, IN_VMEM],
         out_specs=[IN_VMEM] * near + [IN_HBM] * (len(plan) - near),
         scratch_shapes=[
             pltpu.VMEM((later, shape[1], WIDTH), own.dtype),
-            pltpu.SemaphoreType.DMA((len(plan),)),
+            pltpu.VMEM((len(plan), HALVES, shape[1], WIDTH), own.dtype),
+            pltpu.SemaphoreType.DMA((2, HALVES * len(plan))),
         ],
         cost_estimate=pl.CostEstimate(flops=0, bytes_accessed=6 * MIB, transcendentals=0),
         compiler_params=pltpu.CompilerParams(vmem_limit_bytes=12 * MIB),
-    )(own.reshape(shape), other.reshape(shape))
+    )(pltpu.with_memory_space_constraint(own.reshape(shape), pltpu.HBM), other.reshape(shape))
     return {(number, direction): value for (number, direction, _), value in zip(plan, sums)}
 
 
@@ -345,7 +413,10 @@
         block = jnp.broadcast_to(blocks[step][None], (SPANS, 2, BLK, HD))
         mine = lax.all_to_all(block, "ctx", 0, 0, tiled=True)
         stores += [mine, lax.ppermute(mine, "head", swap)]
-        send, own = attend(step, table, queries, stores, weight)
+        if step == 0:
+            send, own = attend(step, table, queries, stores, weight)
+        else:
+            send, own = project(attend(step, table, queries, stores, None), weight)
         got = lax.ppermute(send, "head", swap)
         streams[step] = pair_sums(own, got, chips)
 
@@ -396,6 +467,4 @@
     )
     out_specs = P(None, ("ctx", "head"), None)
 
-    return jax.shard_map(
-        local, mesh=mesh, in_specs=in_specs, out_specs=out_specs, check_vma=False
-    )
+    return jax.shard_map(local, mesh=mesh, in_specs=in_specs, out_specs=out_specs, check_vma=False)

time: 129 us -> 132 us (1.023)
  Pallas kernels: 32.9 us -> 37.1 us
    pallas_call x4 -> x5, Pallas kernels: 25 us -> 29.2 us  [the longest x2 16.6 us: attend(): pl.pallas_call(functools.partial(attend_kernel, step, joined), out_shape=...]
  transfers between devices with their start and end apart: 21 -> 21, of which waited for: 8 -> 8; matrix products, arithmetic and copies ran while one was open for 1% -> 1% of each run, Pallas kernels for 17% -> 29%
where the time goes in v5:
time: 132 us; the launch traced here: 130 us
  Pallas kernels  37.1 us (28%)
  starting transfers between devices  35.4 us (27%)
  waiting for transfers between devices  28.8 us (22%)
  blocking collectives  23.1 us (18%)
  other arithmetic  2.73 us (2%)
  local copies, waits for them, and re-layouts  2.61 us (2%)
    ppermute x16, starting transfers between devices, local(): lax.ppermute(total, 'head', shift_z(heads, direction))  29.8 us
    all_to_all x1, blocking collectives, local(): mine = lax.all_to_all(block, 'ctx', 0, 0, tiled=True)  23.1 us
    pallas_call x2, Pallas kernels, attend(): pl.pallas_call(functools.partial(attend_kernel, step, joined), out_shape=...  16.6 us
    all_to_all x1, waiting for transfers between devices, local(): mine = lax.all_to_all(block, 'ctx', 0, 0, tiled=True)  15.1 us
    ppermute x16, waiting for transfers between devices, local(): lax.ppermute(total, 'head', shift_z(heads, direction))  13.7 us
    pallas_call x1, Pallas kernels, make_plan(): pl.pallas_call(plan_kernel, out_shape=jax.ShapeDtypeStruct((STEPS * PAIRS...  7.92 us
    pallas_call x1, Pallas kernels, project(): pl.pallas_call(project_kernel, out_shape=[shape] * 2, in_specs=[IN_VMEM,...  7.09 us
    pallas_call x2, Pallas kernels, pair_sums(): pl.pallas_call(kernel, out_shape=out_shape, in_specs=[IN_HBM, IN_VMEM], o...  5.45 us
  transfers between devices with their start and end apart: 21, of which 8 were waited for; matrix products, arithmetic and copies ran while one was open for 1% of the time, Pallas kernels for 29%

profile of v5, /device:TPU:2, one launch (start us, length us, event | category | flops | bytes accessed | tf_op | source)
XLA Modules:
  0.0 130.1 jit_solution(3144828922148817712)
XLA Ops:
  1.1 23.1 %all_to_all.10.refs_0_ = bf16[16,2,128,128]{3,2,1,0:T(8,128)(2,1)S(1)} all-to-all(bf16[16,2,128,128]{3,2,1,0:T(8,128)(2,1)S(1)} %broadcast_in_dim.21), channel_id=1, replica_groups=mesh['ctx'=16,'head'=16] {'ctx'}, dimensions={0} | all-to-all | bytes 2097152 | tf_op jit(solution)/shard_map/all_to_all | solution.py:414
  24.2 1.2 broadcast_in_dim.24
  25.5 4.9 %all-to-all-start.1 = ((bf16[16,2,128,128]{3,2,1,0:T(8,128)(2,1)}), bf16[16,2,128,128]{3,2,1,0:T(8,128)(2,1)S(1)}, u32[]{:S(2)}, u32[]{:S(2)}) async-start(bf16[16,2,128,128]{3,2,1,0:T(8,128)(2,1)} %broadcast_in_dim.24), calls=%async_computation.1 | async-start | bytes 2097152 | tf_op jit(solution)/shard_map/all_to_all | solution.py:414
  30.4 15.1 %all-to-all-done.1.refs_2_ = bf16[16,2,128,128]{3,2,1,0:T(8,128)(2,1)S(1)} async-done(((bf16[16,2,128,128]{3,2,1,0:T(8,128)(2,1)}), bf16[16,2,128,128]{3,2,1,0:T(8,128)(2,1)S(1)}, u32[]{:S(2)}, u32[]{:S(2)}) %all-to-all-start.1) | async-done | bytes 1048608 | tf_op jit(solution)/shard_map/all_to_all | solution.py:414
  45.7 7.9 %plan.1.table = s32[144]{0:T(256)S(1)} custom-call(s32[2,16]{1,0:T(2,128)S(1)} %copy-done, s32[64,4]{1,0:T(8,128)S(1)} %copy.8.vertical, s32[64,4]{1,0:T(8,128)S(1)} %copy.9.slash), custom_call_target="tpu_custom_call" | custom-call | tf_op jit(solution)/shard_map/plan/pallas_call | solution.py:87
  53.6 10.9 %shard_map.73 = (bf16[128,8192]{1,0:T(8,128)(2,1)}, bf16[128,8192]{1,0:T(8,128)(2,1)}) custom-call(s32[144]{0:T(256)S(1)} %plan.1.table, bf16[2,256,512]{2,1,0:T(8,128)(2,1)} %q_hbm.3, bf16[16,2,128,128]{3,2,1,0:T(8,128)(2,1)S(1)} %all_to_all.10.refs_0_, bf16[16,2,128,128]{3,2,1,0:T(8,128)(2,1)S(1)} %collective-permute-done.refs_1_, bf16[512,8192]{1,0:T(8,128)(2,1)} %w_hbm.1), custom_call_target="tpu_custom_call" | custom-call | flops 2751463424 | bytes 16777216 | tf_op jit(solution)/shard_map/pallas_call | solution.py:291
  65.1 5.8 %shard_map.75.attended = bf16[256,512]{1,0:T(8,128)(2,1)S(1)} custom-call(s32[144]{0:T(256)S(1)} %plan.1.table, bf16[2,256,512]{2,1,0:T(8,128)(2,1)} %q_hbm.3, bf16[16,2,128,128]{3,2,1,0:T(8,128)(2,1)S(1)} %all_to_all.10.refs_0_, bf16[16,2,128,128]{3,2,1,0:T(8,128)(2,1)S(1)} %collective-permute-done.refs_1_, ...), custom_call_target="tpu_custom_call" | custom-call | flops 603979776 | bytes 16777216 | tf_op jit(solution)/shard_map/pallas_call | solution.py:291
  70.9 7.1 %shard_map.76 = (bf16[128,8192]{1,0:T(8,128)(2,1)}, bf16[128,8192]{1,0:T(8,128)(2,1)}) custom-call(bf16[256,512]{1,0:T(8,128)(2,1)S(1)} %shard_map.75.attended, bf16[512,8192]{1,0:T(8,128)(2,1)} %w_hbm.1), custom_call_target="tpu_custom_call" | custom-call | flops 2147483648 | bytes 12582912 | tf_op jit(solution)/shard_map/pallas_call | solution.py:245
  78.1 2.7 %shard_map.74 = (bf16[2,16,4096]{2,1,0:T(8,128)(2,1)S(1)}, bf16[2,16,4096]{2,1,0:T(8,128)(2,1)S(1)}, bf16[2,16,4096]{2,1,0:T(8,128)(2,1)}, bf16[2,16,4096]{2,1,0...) custom-call(bf16[8,16,8192]{2,1,0:T(8,128)(2,1)} %bitcast.27, ...), custom_call_target="tpu_custom_call" | custom-call | bytes 6291456 | tf_op jit(solution)/shard_map/pallas_call | solution.py:377
  80.8 2.0 %collective-permute-start.2 = (bf16[2,16,4096]{2,1,0:T(8,128)(2,1)S(1)}, bf16[2,16,4096]{2,1,0:T(8,128)(2,1)S(1)}, u32[]{:S(2)}, u32[]{:S(2)}) collective-permute-start(bf16[2,16,4096]{2,1,0:T(8,128)(2,1)S(1)} %get-tuple-element.33), channel_id=1, source_target_pairs={{0,2},{1,3},{2,4},{3,5},{4,6},{5,7},{6,8},{7,9},{8,10},{9,11},{10,... | collective-permute-start | bytes 786440 | tf_op jit(solution)/shard_map/ppermute | solution.py:437
  82.8 4.0 %collective-permute-start.6 = (bf16[2,16,4096]{2,1,0:T(8,128)(2,1)S(1)}, bf16[2,16,4096]{2,1,0:T(8,128)(2,1)S(1)}, u32[]{:S(2)}, u32[]{:S(2)}) collective-permute-start(bf16[2,16,4096]{2,1,0:T(8,128)(2,1)S(1)} %get-tuple-element.36), channel_id=1, source_target_pairs={{0,14},{1,15},{2,0},{3,1},{4,2},{5,3},{6,4},{7,5},{8,6},{9,7},{10,... | collective-permute-start | bytes 786440 | tf_op jit(solution)/shard_map/ppermute | solution.py:437
  86.8 2.7 %shard_map.77 = (bf16[2,16,4096]{2,1,0:T(8,128)(2,1)S(1)}, bf16[2,16,4096]{2,1,0:T(8,128)(2,1)S(1)}, bf16[2,16,4096]{2,1,0:T(8,128)(2,1)}, bf16[2,16,4096]{2,1,0...) custom-call(bf16[8,16,8192]{2,1,0:T(8,128)(2,1)} %bitcast.26, ...), custom_call_target="tpu_custom_call" | custom-call | bytes 6291456 | tf_op jit(solution)/shard_map/pallas_call | solution.py:377
  89.7 3.2 %collective-permute-start.16 = (bf16[2,16,4096]{2,1,0:T(8,128)(2,1)S(1)}, bf16[2,16,4096]{2,1,0:T(8,128)(2,1)S(1)}, u32[]{:S(2)}, u32[]{:S(2)}) collective-permute-start(bf16[2,16,4096]{2,1,0:T(8,128)(2,1)S(1)} %get-tuple-element.47), channel_id=1, source_target_pairs={{0,14},{1,15},{2,0},{3,1},{4,2},{5,3},{6,4},{7,5},{8,6},{9,7},{10,... | collective-permute-start | bytes 786440 | tf_op jit(solution)/shard_map/ppermute | solution.py:437
  94.0 3.5 %collective-permute-start.7 = (bf16[2,16,4096]{2,1,0:T(8,128)(2,1)S(1)}, bf16[2,16,4096]{2,1,0:T(8,128)(2,1)S(1)}, u32[]{:S(2)}, u32[]{:S(2)}) collective-permute-start(bf16[2,16,4096]{2,1,0:T(8,128)(2,1)S(1)} %add_convert_fusion.5), channel_id=1, source_target_pairs={{0,14},{1,15},{2,0},{3,1},{4,2},{5,3},{6,4},{7,5},{8,6},{9,7},{10,... | collective-permute-start | bytes 786440 | tf_op jit(solution)/shard_map/ppermute | solution.py:437
  97.4 2.7 %collective-permute-done.12 = bf16[2,16,4096]{2,1,0:T(8,128)(2,1)S(1)} collective-permute-done((bf16[2,16,4096]{2,1,0:T(8,128)(2,1)S(1)}, bf16[2,16,4096]{2,1,0:T(8,128)(2,1)S(1)}, u32[]{:S(2)}, u32[]{:S(2)}) %collective-permute-start.12) | collective-permute-done | bytes 262176 | tf_op jit(solution)/shard_map/ppermute | solution.py:437
  101.3 3.3 %collective-permute-start.17 = (bf16[2,16,4096]{2,1,0:T(8,128)(2,1)S(1)}, bf16[2,16,4096]{2,1,0:T(8,128)(2,1)S(1)}, u32[]{:S(2)}, u32[]{:S(2)}) collective-permute-start(bf16[2,16,4096]{2,1,0:T(8,128)(2,1)S(1)} %add_convert_fusion.1), channel_id=1, source_target_pairs={{0,14},{1,15},{2,0},{3,1},{4,2},{5,3},{6,4},{7,5},{8,6},{9,7},{10,... | collective-permute-start | bytes 786440 | tf_op jit(solution)/shard_map/ppermute | solution.py:437
  106.0 3.3 %collective-permute-start.8 = (bf16[2,16,4096]{2,1,0:T(8,128)(2,1)S(1)}, bf16[2,16,4096]{2,1,0:T(8,128)(2,1)S(1)}, u32[]{:S(2)}, u32[]{:S(2)}) collective-permute-start(bf16[2,16,4096]{2,1,0:T(8,128)(2,1)S(1)} %add_convert_fusion.4), channel_id=1, source_target_pairs={{0,14},{1,15},{2,0},{3,1},{4,2},{5,3},{6,4},{7,5},{8,6},{9,7},{10,... | collective-permute-start | bytes 786440 | tf_op jit(solution)/shard_map/ppermute | solution.py:437
  109.3 2.3 %collective-permute-done.13 = bf16[2,16,4096]{2,1,0:T(8,128)(2,1)S(1)} collective-permute-done((bf16[2,16,4096]{2,1,0:T(8,128)(2,1)S(1)}, bf16[2,16,4096]{2,1,0:T(8,128)(2,1)S(1)}, u32[]{:S(2)}, u32[]{:S(2)}) %collective-permute-start.13) | collective-permute-done | bytes 262176 | tf_op jit(solution)/shard_map/ppermute | solution.py:437
  111.9 3.3 %collective-permute-start.18 = (bf16[2,16,4096]{2,1,0:T(8,128)(2,1)S(1)}, bf16[2,16,4096]{2,1,0:T(8,128)(2,1)S(1)}, u32[]{:S(2)}, u32[]{:S(2)}) collective-permute-start(bf16[2,16,4096]{2,1,0:T(8,128)(2,1)S(1)} %add_convert_fusion), channel_id=1, source_target_pairs={{0,14},{1,15},{2,0},{3,1},{4,2},{5,3},{6,4},{7,5},{8,6},{9,7},{10,... | collective-permute-start | bytes 786440 | tf_op jit(solution)/shard_map/ppermute | solution.py:437
  115.1 2.1 %collective-permute-done.4 = bf16[2,16,4096]{2,1,0:T(8,128)(2,1)S(1)} collective-permute-done((bf16[2,16,4096]{2,1,0:T(8,128)(2,1)S(1)}, bf16[2,16,4096]{2,1,0:T(8,128)(2,1)S(1)}, u32[]{:S(2)}, u32[]{:S(2)}) %collective-permute-start.4) | collective-permute-done | bytes 262176 | tf_op jit(solution)/shard_map/ppermute | solution.py:437
  117.4 3.3 %collective-permute-start.9 = (bf16[1,16,4096]{2,1,0:T(8,128)(2,1)S(1)}, bf16[1,16,4096]{2,1,0:T(8,128)(2,1)S(1)}, u32[]{:S(2)}, u32[]{:S(2)}) collective-permute-start(bf16[1,16,4096]{2,1,0:T(8,128)(2,1)S(1)} %add_convert_fusion.13), channel_id=1, source_target_pairs={{0,14},{1,15},{2,0},{3,1},{4,2},{5,3},{6,4},{7,5},{8,6},{9,7},{10,... | collective-permute-start | bytes 393224 | tf_op jit(solution)/shard_map/ppermute | solution.py:437
  120.7 2.1 %collective-permute-done.14 = bf16[2,16,4096]{2,1,0:T(8,128)(2,1)S(1)} collective-permute-done((bf16[2,16,4096]{2,1,0:T(8,128)(2,1)S(1)}, bf16[2,16,4096]{2,1,0:T(8,128)(2,1)S(1)}, u32[]{:S(2)}, u32[]{:S(2)}) %collective-permute-start.14) | collective-permute-done | bytes 262176 | tf_op jit(solution)/shard_map/ppermute | solution.py:437
  123.0 3.3 %collective-permute-start.19 = (bf16[1,16,4096]{2,1,0:T(8,128)(2,1)S(1)}, bf16[1,16,4096]{2,1,0:T(8,128)(2,1)S(1)}, u32[]{:S(2)}, u32[]{:S(2)}) collective-permute-start(bf16[1,16,4096]{2,1,0:T(8,128)(2,1)S(1)} %add_convert_fusion.9), channel_id=1, source_target_pairs={{0,14},{1,15},{2,0},{3,1},{4,2},{5,3},{6,4},{7,5},{8,6},{9,7},{10,... | collective-permute-start | bytes 393224 | tf_op jit(solution)/shard_map/ppermute | solution.py:437
  126.5 2.6 %collective-permute-done.15 = bf16[1,16,4096]{2,1,0:T(8,128)(2,1)S(1)} collective-permute-done((bf16[1,16,4096]{2,1,0:T(8,128)(2,1)S(1)}, bf16[1,16,4096]{2,1,0:T(8,128)(2,1)S(1)}, u32[]{:S(2)}, u32[]{:S(2)}) %collective-permute-start.15) | collective-permute-done | bytes 131104 | tf_op jit(solution)/shard_map/ppermute | solution.py:437
  (80 shorter events, 7.3 us)
Async XLA Ops:
  24.2 21.4 %copy-start.15 = (s32[64,4]{0,1:T(4,128)S(1)}, s32[64,4]{0,1:T(4,128)}, u32[]{:S(2)}) copy-start(s32[64,4]{0,1:T(4,128)} %param.13) | copy-start | bytes 3076
  24.2 21.5 %copy-start = (s32[2,16]{1,0:T(2,128)S(1)}, s32[2,16]{1,0:T(2,128)}, u32[]{:S(2)}) copy-start(s32[2,16]{1,0:T(2,128)} %owner.1) | copy-start | bytes 388
  25.5 20.0 %all-to-all-start.1 = ((bf16[16,2,128,128]{3,2,1,0:T(8,128)(2,1)}), bf16[16,2,128,128]{3,2,1,0:T(8,128)(2,1)S(1)}, u32[]{:S(2)}, u32[]{:S(2)}) async-start(bf16[16,2,128,128]{3,2,1,0:T(8,128)(2,1)} %broadcast_in_dim.24), calls=%async_computation.1 | async-start | bytes 2097152 | tf_op jit(solution)/shard_map/all_to_all | solution.py:414
  30.4 23.3 %collective-permute-start = (bf16[16,2,128,128]{3,2,1,0:T(8,128)(2,1)S(1)}, bf16[16,2,128,128]{3,2,1,0:T(8,128)(2,1)S(1)}, u32[]{:S(2)}, u32[]{:S(2)}) collective-permute-start(bf16[16,2,128,128]{3,2,1,0:T(8,128)(2,1)S(1)} %all_to_all.10.refs_0_), channel_id=1, source_target_pairs={{0,1},{1,0},{2,3},{3,2},{4,5},{5,4},{6,7},{7,6},{8,9},{9,8},{10,11... | collective-permute-start | bytes 3145736 | tf_op jit(solution)/shard_map/ppermute | solution.py:415
  45.5 19.6 %collective-permute-start.10 = (bf16[16,2,128,128]{3,2,1,0:T(8,128)(2,1)S(1)}, bf16[16,2,128,128]{3,2,1,0:T(8,128)(2,1)}, u32[]{:S(2)}, u32[]{:S(2)}) collective-permute-start(bf16[16,2,128,128]{3,2,1,0:T(8,128)(2,1)S(1)} %all-to-all-done.1.refs_2_), channel_id=1, source_target_pairs={{0,1},{1,0},{2,3},{3,2},{4,5},{5,4},{6,7},{7,6},{8,9},{9,8},{10,11... | collective-permute-start | bytes 3145736 | tf_op jit(solution)/shard_map/ppermute | solution.py:415
  64.5 13.6 %collective-permute-start.1 = (bf16[128,8192]{1,0:T(8,128)(2,1)}, bf16[128,8192]{1,0:T(8,128)(2,1)S(1)}, u32[]{:S(2)}, u32[]{:S(2)}) collective-permute-start(bf16[128,8192]{1,0:T(8,128)(2,1)} %get-tuple-element.28), channel_id=1, source_target_pairs={{0,1},{1,0},{2,3},{3,2},{4,5},{5,4},{6,7},{7,6},{8,9},{9,8},{10,11... | collective-permute-start | bytes 6291464 | tf_op jit(solution)/shard_map/ppermute | solution.py:420
  78.0 8.8 %collective-permute-start.11 = (bf16[128,8192]{1,0:T(8,128)(2,1)}, bf16[128,8192]{1,0:T(8,128)(2,1)S(1)}, u32[]{:S(2)}, u32[]{:S(2)}) collective-permute-start(bf16[128,8192]{1,0:T(8,128)(2,1)} %get-tuple-element.39), channel_id=1, source_target_pairs={{0,1},{1,0},{2,3},{3,2},{4,5},{5,4},{6,7},{7,6},{8,9},{9,8},{10,11... | collective-permute-start | bytes 6291464 | tf_op jit(solution)/shard_map/ppermute | solution.py:420
  80.8 12.9 %collective-permute-start.2 = (bf16[2,16,4096]{2,1,0:T(8,128)(2,1)S(1)}, bf16[2,16,4096]{2,1,0:T(8,128)(2,1)S(1)}, u32[]{:S(2)}, u32[]{:S(2)}) collective-permute-start(bf16[2,16,4096]{2,1,0:T(8,128)(2,1)S(1)} %get-tuple-element.33), channel_id=1, source_target_pairs={{0,2},{1,3},{2,4},{3,5},{4,6},{5,7},{6,8},{7,9},{8,10},{9,11},{10,... | collective-permute-start | bytes 786440 | tf_op jit(solution)/shard_map/ppermute | solution.py:437
  82.8 11.1 %collective-permute-start.6 = (bf16[2,16,4096]{2,1,0:T(8,128)(2,1)S(1)}, bf16[2,16,4096]{2,1,0:T(8,128)(2,1)S(1)}, u32[]{:S(2)}, u32[]{:S(2)}) collective-permute-start(bf16[2,16,4096]{2,1,0:T(8,128)(2,1)S(1)} %get-tuple-element.36), channel_id=1, source_target_pairs={{0,14},{1,15},{2,0},{3,1},{4,2},{5,3},{6,4},{7,5},{8,6},{9,7},{10,... | collective-permute-start | bytes 786440 | tf_op jit(solution)/shard_map/ppermute | solution.py:437
  89.6 10.5 %collective-permute-start.12 = (bf16[2,16,4096]{2,1,0:T(8,128)(2,1)S(1)}, bf16[2,16,4096]{2,1,0:T(8,128)(2,1)S(1)}, u32[]{:S(2)}, u32[]{:S(2)}) collective-permute-start(bf16[2,16,4096]{2,1,0:T(8,128)(2,1)S(1)} %get-tuple-element.44), channel_id=1, source_target_pairs={{0,2},{1,3},{2,4},{3,5},{4,6},{5,7},{6,8},{7,9},{8,10},{9,11},{10,... | collective-permute-start | bytes 786440 | tf_op jit(solution)/shard_map/ppermute | solution.py:437
  89.7 11.5 %collective-permute-start.16 = (bf16[2,16,4096]{2,1,0:T(8,128)(2,1)S(1)}, bf16[2,16,4096]{2,1,0:T(8,128)(2,1)S(1)}, u32[]{:S(2)}, u32[]{:S(2)}) collective-permute-start(bf16[2,16,4096]{2,1,0:T(8,128)(2,1)S(1)} %get-tuple-element.47), channel_id=1, source_target_pairs={{0,14},{1,15},{2,0},{3,1},{4,2},{5,3},{6,4},{7,5},{8,6},{9,7},{10,... | collective-permute-start | bytes 786440 | tf_op jit(solution)/shard_map/ppermute | solution.py:437
  93.8 11.9 %collective-permute-start.3 = (bf16[2,16,4096]{2,1,0:T(8,128)(2,1)S(1)}, bf16[2,16,4096]{2,1,0:T(8,128)(2,1)S(1)}, u32[]{:S(2)}, u32[]{:S(2)}) collective-permute-start(bf16[2,16,4096]{2,1,0:T(8,128)(2,1)S(1)} %add_convert_fusion.7), channel_id=1, source_target_pairs={{0,2},{1,3},{2,4},{3,5},{4,6},{5,7},{6,8},{7,9},{8,10},{9,11},{10,... | collective-permute-start | bytes 786440 | tf_op jit(solution)/shard_map/ppermute | solution.py:437
  94.0 11.9 %collective-permute-start.7 = (bf16[2,16,4096]{2,1,0:T(8,128)(2,1)S(1)}, bf16[2,16,4096]{2,1,0:T(8,128)(2,1)S(1)}, u32[]{:S(2)}, u32[]{:S(2)}) collective-permute-start(bf16[2,16,4096]{2,1,0:T(8,128)(2,1)S(1)} %add_convert_fusion.5), channel_id=1, source_target_pairs={{0,14},{1,15},{2,0},{3,1},{4,2},{5,3},{6,4},{7,5},{8,6},{9,7},{10,... | collective-permute-start | bytes 786440 | tf_op jit(solution)/shard_map/ppermute | solution.py:437
  101.1 10.5 %collective-permute-start.13 = (bf16[2,16,4096]{2,1,0:T(8,128)(2,1)S(1)}, bf16[2,16,4096]{2,1,0:T(8,128)(2,1)S(1)}, u32[]{:S(2)}, u32[]{:S(2)}) collective-permute-start(bf16[2,16,4096]{2,1,0:T(8,128)(2,1)S(1)} %add_convert_fusion.3), channel_id=1, source_target_pairs={{0,2},{1,3},{2,4},{3,5},{4,6},{5,7},{6,8},{7,9},{8,10},{9,11},{10,... | collective-permute-start | bytes 786440 | tf_op jit(solution)/shard_map/ppermute | solution.py:437
  101.3 21.5 %copy-start.13 = (bf16[1,16,4096]{2,1,0:T(8,128)(2,1)S(1)}, bf16[1,16,4096]{2,1,0:T(8,128)(2,1)}, u32[]{:S(2)}) copy-start(bf16[1,16,4096]{2,1,0:T(8,128)(2,1)} %get-tuple-element.41) | copy-start | bytes 393220
  101.3 10.4 %collective-permute-start.17 = (bf16[2,16,4096]{2,1,0:T(8,128)(2,1)S(1)}, bf16[2,16,4096]{2,1,0:T(8,128)(2,1)S(1)}, u32[]{:S(2)}, u32[]{:S(2)}) collective-permute-start(bf16[2,16,4096]{2,1,0:T(8,128)(2,1)S(1)} %add_convert_fusion.1), channel_id=1, source_target_pairs={{0,14},{1,15},{2,0},{3,1},{4,2},{5,3},{6,4},{7,5},{8,6},{9,7},{10,... | collective-permute-start | bytes 786440 | tf_op jit(solution)/shard_map/ppermute | solution.py:437
  105.8 11.4 %collective-permute-start.4 = (bf16[2,16,4096]{2,1,0:T(8,128)(2,1)S(1)}, bf16[2,16,4096]{2,1,0:T(8,128)(2,1)S(1)}, u32[]{:S(2)}, u32[]{:S(2)}) collective-permute-start(bf16[2,16,4096]{2,1,0:T(8,128)(2,1)S(1)} %add_convert_fusion.6), channel_id=1, source_target_pairs={{0,2},{1,3},{2,4},{3,5},{4,6},{5,7},{6,8},{7,9},{8,10},{9,11},{10,... | collective-permute-start | bytes 786440 | tf_op jit(solution)/shard_map/ppermute | solution.py:437
  106.0 11.4 %collective-permute-start.8 = (bf16[2,16,4096]{2,1,0:T(8,128)(2,1)S(1)}, bf16[2,16,4096]{2,1,0:T(8,128)(2,1)S(1)}, u32[]{:S(2)}, u32[]{:S(2)}) collective-permute-start(bf16[2,16,4096]{2,1,0:T(8,128)(2,1)S(1)} %add_convert_fusion.4), channel_id=1, source_target_pairs={{0,14},{1,15},{2,0},{3,1},{4,2},{5,3},{6,4},{7,5},{8,6},{9,7},{10,... | collective-permute-start | bytes 786440 | tf_op jit(solution)/shard_map/ppermute | solution.py:437
  111.7 11.1 %collective-permute-start.14 = (bf16[2,16,4096]{2,1,0:T(8,128)(2,1)S(1)}, bf16[2,16,4096]{2,1,0:T(8,128)(2,1)S(1)}, u32[]{:S(2)}, u32[]{:S(2)}) collective-permute-start(bf16[2,16,4096]{2,1,0:T(8,128)(2,1)S(1)} %add_convert_fusion.2), channel_id=1, source_target_pairs={{0,2},{1,3},{2,4},{3,5},{4,6},{5,7},{6,8},{7,9},{8,10},{9,11},{10,... | collective-permute-start | bytes 786440 | tf_op jit(solution)/shard_map/ppermute | solution.py:437
  111.9 11.1 %collective-permute-start.18 = (bf16[2,16,4096]{2,1,0:T(8,128)(2,1)S(1)}, bf16[2,16,4096]{2,1,0:T(8,128)(2,1)S(1)}, u32[]{:S(2)}, u32[]{:S(2)}) collective-permute-start(bf16[2,16,4096]{2,1,0:T(8,128)(2,1)S(1)} %add_convert_fusion), channel_id=1, source_target_pairs={{0,14},{1,15},{2,0},{3,1},{4,2},{5,3},{6,4},{7,5},{8,6},{9,7},{10,... | collective-permute-start | bytes 786440 | tf_op jit(solution)/shard_map/ppermute | solution.py:437
  117.2 9.1 %collective-permute-start.5 = (bf16[1,16,4096]{2,1,0:T(8,128)(2,1)S(1)}, bf16[1,16,4096]{2,1,0:T(8,128)(2,1)S(1)}, u32[]{:S(2)}, u32[]{:S(2)}) collective-permute-start(bf16[1,16,4096]{2,1,0:T(8,128)(2,1)S(1)} %add_convert_fusion.15), channel_id=1, source_target_pairs={{0,2},{1,3},{2,4},{3,5},{4,6},{5,7},{6,8},{7,9},{8,10},{9,11},{10,... | collective-permute-start | bytes 393224 | tf_op jit(solution)/shard_map/ppermute | solution.py:437
  117.4 8.9 %collective-permute-start.9 = (bf16[1,16,4096]{2,1,0:T(8,128)(2,1)S(1)}, bf16[1,16,4096]{2,1,0:T(8,128)(2,1)S(1)}, u32[]{:S(2)}, u32[]{:S(2)}) collective-permute-start(bf16[1,16,4096]{2,1,0:T(8,128)(2,1)S(1)} %add_convert_fusion.13), channel_id=1, source_target_pairs={{0,14},{1,15},{2,0},{3,1},{4,2},{5,3},{6,4},{7,5},{8,6},{9,7},{10,... | collective-permute-start | bytes 393224 | tf_op jit(solution)/shard_map/ppermute | solution.py:437
  122.9 6.3 %collective-permute-start.15 = (bf16[1,16,4096]{2,1,0:T(8,128)(2,1)S(1)}, bf16[1,16,4096]{2,1,0:T(8,128)(2,1)S(1)}, u32[]{:S(2)}, u32[]{:S(2)}) collective-permute-start(bf16[1,16,4096]{2,1,0:T(8,128)(2,1)S(1)} %add_convert_fusion.11), channel_id=1, source_target_pairs={{0,2},{1,3},{2,4},{3,5},{4,6},{5,7},{6,8},{7,9},{8,10},{9,11},{10,... | collective-permute-start | bytes 393224 | tf_op jit(solution)/shard_map/ppermute | solution.py:437
  123.0 6.1 %collective-permute-start.19 = (bf16[1,16,4096]{2,1,0:T(8,128)(2,1)S(1)}, bf16[1,16,4096]{2,1,0:T(8,128)(2,1)S(1)}, u32[]{:S(2)}, u32[]{:S(2)}) collective-permute-start(bf16[1,16,4096]{2,1,0:T(8,128)(2,1)S(1)} %add_convert_fusion.9), channel_id=1, source_target_pairs={{0,14},{1,15},{2,0},{3,1},{4,2},{5,3},{6,4},{7,5},{8,6},{9,7},{10,... | collective-permute-start | bytes 393224 | tf_op jit(solution)/shard_map/ppermute | solution.py:437
  (13 other events, 202.3 us)

commit v6 on v5

--- a/solution.py
+++ b/solution.py
@@ -301,24 +301,29 @@
     )(table, queries, *stores, *extra)
 
 
-def waves(chips):
+def waves(chips, merged):
     far = chips // 2
     plan = []
-    for number in range(far):
-        for direction in (1, -1):
+    for number in range(far + 1):
+        for direction in (1, -1) if number < far else (0,):
             distances = []
             for half in range(HALVES):
                 longest = far if (direction == 1) == (half == 0) else far - 1
-                if number < longest:
+                if direction == 0:
+                    distances.append((half, 0))
+                elif number < longest:
                     distances.append((half, direction * (longest - number)))
-            plan.append((number, direction, distances))
-    plan.append((far, 0, [(half, 0) for half in range(HALVES)]))
+            if merged:
+                plan.append((number, direction, distances))
+            else:
+                plan += [(number, direction, [entry]) for entry in distances]
     return plan
 
 
-def pair_sums(own, other, chips):
-    plan = waves(chips)
-    near = 2
+def pair_sums(step, own, other, chips):
+    merged = step == 0
+    plan = waves(chips, merged)
+    near = 2 if merged else 2 * HALVES
 
     def kernel(own_hbm, other_ref, *refs):
         outs = refs[: len(plan)]
@@ -381,13 +386,18 @@
         out_specs=[IN_VMEM] * near + [IN_HBM] * (len(plan) - near),
         scratch_shapes=[
             pltpu.VMEM((later, shape[1], WIDTH), own.dtype),
-            pltpu.VMEM((len(plan), HALVES, shape[1], WIDTH), own.dtype),
+            pltpu.VMEM((len(plan), HALVES if merged else 1, shape[1], WIDTH), own.dtype),
             pltpu.SemaphoreType.DMA((2, HALVES * len(plan))),
         ],
         cost_estimate=pl.CostEstimate(flops=0, bytes_accessed=6 * MIB, transcendentals=0),
         compiler_params=pltpu.CompilerParams(vmem_limit_bytes=12 * MIB),
     )(pltpu.with_memory_space_constraint(own.reshape(shape), pltpu.HBM), other.reshape(shape))
-    return {(number, direction): value for (number, direction, _), value in zip(plan, sums)}
+    if merged:
+        return {(number, direction): value for (number, direction, _), value in zip(plan, sums)}
+    return {
+        (number, direction, distances[0][0]): value
+        for (number, direction, distances), value in zip(plan, sums)
+    }
 
 
 def local(queries, key_rows, value_rows, out_weight, span_owner, vertical_blocks, slash_offsets):
@@ -418,37 +428,53 @@
         else:
             send, own = project(attend(step, table, queries, stores, None), weight)
         got = lax.ppermute(send, "head", swap)
-        streams[step] = pair_sums(own, got, chips)
+        streams[step] = pair_sums(step, own, got, chips)
 
     far = chips // 2
     moving = {}
     for number in range(far):
-        for step in range(STEPS):
-            for direction in (1, -1):
-                total = streams[step][number, direction]
+        for direction in (1, -1):
+            total = streams[0][number, direction]
+            if number > 0:
+                before = moving[number - 1, direction]
+                if total.shape[0] < before.shape[0]:
+                    keep = 0 if direction == 1 else 1
+                    moving["ended", direction] = before[1 - keep]
+                    before = before[keep : keep + 1]
+                total = total.astype(jnp.float32) + before.astype(jnp.float32)
+                total = total.astype(jnp.bfloat16)
+            moving[number, direction] = lax.ppermute(
+                total, "head", shift_z(heads, direction)
+            )
+    last = {}
+    for number in range(far):
+        for direction in (1, -1):
+            for half in range(HALVES):
+                if (number, direction, half) not in streams[1]:
+                    continue
+                total = streams[1][number, direction, half]
                 if number > 0:
-                    before = moving[step, number - 1, direction]
-                    if total.shape[0] < before.shape[0]:
-                        keep = 0 if direction == 1 else 1
-                        moving[step, "ended", direction] = before[1 - keep]
-                        before = before[keep : keep + 1]
-                    total = total.astype(jnp.float32) + before.astype(jnp.float32)
+                    total = total.astype(jnp.float32) + last[direction, half].astype(jnp.float32)
                     total = total.astype(jnp.bfloat16)
-                moving[step, number, direction] = lax.ppermute(
+                last[direction, half] = lax.ppermute(
                     total, "head", shift_z(heads, direction)
                 )
 
+    arrived = (
+        (moving[far - 1, 1][0], moving["ended", -1]),
+        (moving["ended", 1], moving[far - 1, -1][0]),
+    )
     outputs = []
     for step in range(STEPS):
-        last = far - 1
-        arrived = (
-            (moving[step, last, 1][0], moving[step, "ended", -1]),
-            (moving[step, "ended", 1], moving[step, last, -1][0]),
-        )
         columns = []
         for half in range(HALVES):
-            total = streams[step][far, 0][half].astype(jnp.float32)
-            for value in arrived[half]:
+            if step == 0:
+                total = streams[0][far, 0][half].astype(jnp.float32)
+                values = arrived[half]
+            else:
+                total = streams[1][far, 0, half][0].astype(jnp.float32)
+                values = (last[1, half][0], last[-1, half][0])
+            for value in values:
                 total = total + value.astype(jnp.float32)
             columns.append(total.astype(jnp.bfloat16))
         outputs.append(jnp.concatenate(columns, axis=1)[None])

time: 132 us -> 148 us (1.12)
  starting transfers between devices: 35.4 us -> 43.5 us
  waiting for transfers between devices: 28.8 us -> 36.3 us
    ppermute x16 -> x22, starting transfers between devices: 29.8 us -> 37.9 us  [local(): lax.ppermute(total, 'head', shift_z(heads, direction))]
    ppermute x16 -> x22, waiting for transfers between devices: 13.7 us -> 21.1 us  [local(): lax.ppermute(total, 'head', shift_z(heads, direction))]
  transfers between devices with their start and end apart: 21 -> 27, of which waited for: 8 -> 6; matrix products, arithmetic and copies ran while one was open for 1% -> 1% of each run, Pallas kernels for 29% -> 17%
where the time goes in v6:
time: 148 us; the launch traced here: 146 us
  starting transfers between devices  43.5 us (29%)
  Pallas kernels  37.5 us (25%)
  waiting for transfers between devices  36.3 us (25%)
  blocking collectives  23.1 us (16%)
  other arithmetic  2.72 us (2%)
  local copies, waits for them, and re-layouts  2.63 us (2%)
    ppermute x22, starting transfers between devices, local(): lax.ppermute(total, 'head', shift_z(heads, direction))  37.9 us
    all_to_all x1, blocking collectives, local(): mine = lax.all_to_all(block, 'ctx', 0, 0, tiled=True)  23.1 us
    ppermute x22, waiting for transfers between devices, local(): lax.ppermute(total, 'head', shift_z(heads, direction))  21.1 us
    pallas_call x2, Pallas kernels, attend(): pl.pallas_call(functools.partial(attend_kernel, step, joined), out_shape=...  16.6 us
    all_to_all x1, waiting for transfers between devices, local(): mine = lax.all_to_all(block, 'ctx', 0, 0, tiled=True)  15.1 us
    pallas_call x1, Pallas kernels, make_plan(): pl.pallas_call(plan_kernel, out_shape=jax.ShapeDtypeStruct((STEPS * PAIRS...  7.92 us
    pallas_call x1, Pallas kernels, project(): pl.pallas_call(project_kernel, out_shape=[shape] * 2, in_specs=[IN_VMEM,...  7.16 us
    pallas_call x2, Pallas kernels, pair_sums(): pl.pallas_call(kernel, out_shape=out_shape, in_specs=[IN_HBM, IN_VMEM], o...  5.74 us
  transfers between devices with their start and end apart: 27, of which 6 were waited for; matrix products, arithmetic and copies ran while one was open for 1% of the time, Pallas kernels for 17%

profile of v6, /device:TPU:2, one launch (start us, length us, event | category | flops | bytes accessed | tf_op | source)
XLA Modules:
  0.0 146.2 jit_solution(15199453390880850324)
XLA Ops:
  1.1 23.1 %all_to_all.10.refs_0_ = bf16[16,2,128,128]{3,2,1,0:T(8,128)(2,1)S(1)} all-to-all(bf16[16,2,128,128]{3,2,1,0:T(8,128)(2,1)S(1)} %broadcast_in_dim.21), channel_id=1, replica_groups=mesh['ctx'=16,'head'=16] {'ctx'}, dimensions={0} | all-to-all | bytes 2097152 | tf_op jit(solution)/shard_map/all_to_all | solution.py:424
  25.5 4.9 %all-to-all-start.1 = ((bf16[16,2,128,128]{3,2,1,0:T(8,128)(2,1)}), bf16[16,2,128,128]{3,2,1,0:T(8,128)(2,1)S(1)}, u32[]{:S(2)}, u32[]{:S(2)}) async-start(bf16[16,2,128,128]{3,2,1,0:T(8,128)(2,1)} %broadcast_in_dim.24), calls=%async_computation.1 | async-start | bytes 2097152 | tf_op jit(solution)/shard_map/all_to_all | solution.py:424
  30.4 15.1 %all-to-all-done.1.refs_2_ = bf16[16,2,128,128]{3,2,1,0:T(8,128)(2,1)S(1)} async-done(((bf16[16,2,128,128]{3,2,1,0:T(8,128)(2,1)}), bf16[16,2,128,128]{3,2,1,0:T(8,128)(2,1)S(1)}, u32[]{:S(2)}, u32[]{:S(2)}) %all-to-all-start.1) | async-done | bytes 1048608 | tf_op jit(solution)/shard_map/all_to_all | solution.py:424
  45.7 7.9 %plan.1.table = s32[144]{0:T(256)S(1)} custom-call(s32[2,16]{1,0:T(2,128)S(1)} %copy-done, s32[64,4]{1,0:T(8,128)S(1)} %copy.8.vertical, s32[64,4]{1,0:T(8,128)S(1)} %copy.9.slash), custom_call_target="tpu_custom_call" | custom-call | tf_op jit(solution)/shard_map/plan/pallas_call | solution.py:87
  53.7 5.8 %shard_map.75.attended = bf16[256,512]{1,0:T(8,128)(2,1)S(1)} custom-call(s32[144]{0:T(256)S(1)} %plan.1.table, bf16[2,256,512]{2,1,0:T(8,128)(2,1)} %q_hbm.3, bf16[16,2,128,128]{3,2,1,0:T(8,128)(2,1)S(1)} %all_to_all.10.refs_0_, bf16[16,2,128,128]{3,2,1,0:T(8,128)(2,1)S(1)} %collective-permute-done.refs_1_, ...), custom_call_target="tpu_custom_call" | custom-call | flops 603979776 | bytes 16777216 | tf_op jit(solution)/shard_map/pallas_call | solution.py:291
  59.4 7.2 %shard_map.76 = (bf16[128,8192]{1,0:T(8,128)(2,1)}, bf16[128,8192]{1,0:T(8,128)(2,1)}) custom-call(bf16[256,512]{1,0:T(8,128)(2,1)S(1)} %shard_map.75.attended, bf16[512,8192]{1,0:T(8,128)(2,1)} %w_hbm.1), custom_call_target="tpu_custom_call" | custom-call | flops 2147483648 | bytes 12582912 | tf_op jit(solution)/shard_map/pallas_call | solution.py:245
  67.2 10.9 %shard_map.73 = (bf16[128,8192]{1,0:T(8,128)(2,1)}, bf16[128,8192]{1,0:T(8,128)(2,1)}) custom-call(s32[144]{0:T(256)S(1)} %plan.1.table, bf16[2,256,512]{2,1,0:T(8,128)(2,1)} %q_hbm.3, bf16[16,2,128,128]{3,2,1,0:T(8,128)(2,1)S(1)} %all_to_all.10.refs_0_, bf16[16,2,128,128]{3,2,1,0:T(8,128)(2,1)S(1)} %collective-permute-done.refs_1_, bf16[512,8192]{1,0:T(8,128)(2,1)} %w_hbm.1), custom_call_target="tpu_custom_call" | custom-call | flops 2751463424 | bytes 16777216 | tf_op jit(solution)/shard_map/pallas_call | solution.py:291
  78.2 3.0 %shard_map.77 = (bf16[1,16,4096]{2,1,0:T(8,128)(2,1)S(1)}, bf16[1,16,4096]{2,1,0:T(8,128)(2,1)S(1)}, bf16[1,16,4096]{2,1,0:T(8,128)(2,1)S(1)}, bf16[1,16,4096]{2...) custom-call(bf16[8,16,8192]{2,1,0:T(8,128)(2,1)} %bitcast.27, ...), custom_call_target="tpu_custom_call" | custom-call | bytes 6291456 | tf_op jit(solution)/shard_map/pallas_call | solution.py:382
  81.2 2.0 %collective-permute-start.12 = (bf16[1,16,4096]{2,1,0:T(8,128)(2,1)S(1)}, bf16[1,16,4096]{2,1,0:T(8,128)(2,1)S(1)}, u32[]{:S(2)}, u32[]{:S(2)}) collective-permute-start(bf16[1,16,4096]{2,1,0:T(8,128)(2,1)S(1)} %get-tuple-element.51), channel_id=1, source_target_pairs={{0,2},{1,3},{2,4},{3,5},{4,6},{5,7},{6,8},{7,9},{8,10},{9,11},{10,... | collective-permute-start | bytes 393224 | tf_op jit(solution)/shard_map/ppermute | solution.py:459
  83.2 2.8 %shard_map.74 = (bf16[2,16,4096]{2,1,0:T(8,128)(2,1)S(1)}, bf16[2,16,4096]{2,1,0:T(8,128)(2,1)S(1)}, bf16[2,16,4096]{2,1,0:T(8,128)(2,1)}, bf16[2,16,4096]{2,1,0...) custom-call(bf16[8,16,8192]{2,1,0:T(8,128)(2,1)} %bitcast.26, ...), custom_call_target="tpu_custom_call" | custom-call | bytes 6291456 | tf_op jit(solution)/shard_map/pallas_call | solution.py:382
  88.0 3.4 %collective-permute-start.6 = (bf16[2,16,4096]{2,1,0:T(8,128)(2,1)S(1)}, bf16[2,16,4096]{2,1,0:T(8,128)(2,1)S(1)}, u32[]{:S(2)}, u32[]{:S(2)}) collective-permute-start(bf16[2,16,4096]{2,1,0:T(8,128)(2,1)S(1)} %get-tuple-element.43), channel_id=1, source_target_pairs={{0,14},{1,15},{2,0},{3,1},{4,2},{5,3},{6,4},{7,5},{8,6},{9,7},{10,... | collective-permute-start | bytes 786440 | tf_op jit(solution)/shard_map/ppermute | solution.py:446
  93.4 3.1 %collective-permute-start.22 = (bf16[1,16,4096]{2,1,0:T(8,128)(2,1)S(1)}, bf16[1,16,4096]{2,1,0:T(8,128)(2,1)S(1)}, u32[]{:S(2)}, u32[]{:S(2)}) collective-permute-start(bf16[1,16,4096]{2,1,0:T(8,128)(2,1)S(1)} %get-tuple-element.62), channel_id=1, source_target_pairs={{0,14},{1,15},{2,0},{3,1},{4,2},{5,3},{6,4},{7,5},{8,6},{9,7},{10,... | collective-permute-start | bytes 393224 | tf_op jit(solution)/shard_map/ppermute | solution.py:459
  96.6 4.3 %collective-permute-done.16 = bf16[1,16,4096]{2,1,0:T(8,128)(2,1)S(1)} collective-permute-done((bf16[1,16,4096]{2,1,0:T(8,128)(2,1)S(1)}, bf16[1,16,4096]{2,1,0:T(8,128)(2,1)S(1)}, u32[]{:S(2)}, u32[]{:S(2)}) %collective-permute-start.16) | collective-permute-done | bytes 131104 | tf_op jit(solution)/shard_map/ppermute | solution.py:459
  100.9 2.1 %collective-permute-start.13 = (bf16[1,16,4096]{2,1,0:T(8,128)(2,1)S(1)}, bf16[1,16,4096]{2,1,0:T(8,128)(2,1)S(1)}, u32[]{:S(2)}, u32[]{:S(2)}) collective-permute-start(bf16[1,16,4096]{2,1,0:T(8,128)(2,1)S(1)} %add_convert_fusion.15), channel_id=1, source_target_pairs={{0,2},{1,3},{2,4},{3,5},{4,6},{5,7},{6,8},{7,9},{8,10},{9,11},{10,... | collective-permute-start | bytes 393224 | tf_op jit(solution)/shard_map/ppermute | solution.py:459
  105.4 2.9 %collective-permute-start.23 = (bf16[1,16,4096]{2,1,0:T(8,128)(2,1)S(1)}, bf16[1,16,4096]{2,1,0:T(8,128)(2,1)S(1)}, u32[]{:S(2)}, u32[]{:S(2)}) collective-permute-start(bf16[1,16,4096]{2,1,0:T(8,128)(2,1)S(1)} %add_convert_fusion.7), channel_id=1, source_target_pairs={{0,14},{1,15},{2,0},{3,1},{4,2},{5,3},{6,4},{7,5},{8,6},{9,7},{10,... | collective-permute-start | bytes 393224 | tf_op jit(solution)/shard_map/ppermute | solution.py:459
  109.5 3.3 %collective-permute-start.7 = (bf16[2,16,4096]{2,1,0:T(8,128)(2,1)S(1)}, bf16[2,16,4096]{2,1,0:T(8,128)(2,1)S(1)}, u32[]{:S(2)}, u32[]{:S(2)}) collective-permute-start(bf16[2,16,4096]{2,1,0:T(8,128)(2,1)S(1)} %add_convert_fusion.1), channel_id=1, source_target_pairs={{0,14},{1,15},{2,0},{3,1},{4,2},{5,3},{6,4},{7,5},{8,6},{9,7},{10,... | collective-permute-start | bytes 786440 | tf_op jit(solution)/shard_map/ppermute | solution.py:446
  113.0 3.3 %collective-permute-start.18 = (bf16[1,16,4096]{2,1,0:T(8,128)(2,1)S(1)}, bf16[1,16,4096]{2,1,0:T(8,128)(2,1)S(1)}, u32[]{:S(2)}, u32[]{:S(2)}) collective-permute-start(bf16[1,16,4096]{2,1,0:T(8,128)(2,1)S(1)} %add_convert_fusion.11), channel_id=1, source_target_pairs={{0,14},{1,15},{2,0},{3,1},{4,2},{5,3},{6,4},{7,5},{8,6},{9,7},{10,... | collective-permute-start | bytes 393224 | tf_op jit(solution)/shard_map/ppermute | solution.py:459
  116.5 4.4 %collective-permute-done.14 = bf16[1,16,4096]{2,1,0:T(8,128)(2,1)S(1)} collective-permute-done((bf16[1,16,4096]{2,1,0:T(8,128)(2,1)S(1)}, bf16[1,16,4096]{2,1,0:T(8,128)(2,1)S(1)}, u32[]{:S(2)}, u32[]{:S(2)}) %collective-permute-start.14) | collective-permute-done | bytes 131104 | tf_op jit(solution)/shard_map/ppermute | solution.py:459
  122.2 4.2 %collective-permute-done.24 = bf16[1,16,4096]{2,1,0:T(8,128)(2,1)S(1)} collective-permute-done((bf16[1,16,4096]{2,1,0:T(8,128)(2,1)S(1)}, bf16[1,16,4096]{2,1,0:T(8,128)(2,1)S(1)}, u32[]{:S(2)}, u32[]{:S(2)}) %collective-permute-start.24) | collective-permute-done | bytes 131104 | tf_op jit(solution)/shard_map/ppermute | solution.py:459
  126.4 3.3 %collective-permute-start.25 = (bf16[1,16,4096]{2,1,0:T(8,128)(2,1)S(1)}, bf16[1,16,4096]{2,1,0:T(8,128)(2,1)S(1)}, u32[]{:S(2)}, u32[]{:S(2)}) collective-permute-start(bf16[1,16,4096]{2,1,0:T(8,128)(2,1)S(1)} %add_convert_fusion.5), channel_id=1, source_target_pairs={{0,14},{1,15},{2,0},{3,1},{4,2},{5,3},{6,4},{7,5},{8,6},{9,7},{10,... | collective-permute-start | bytes 393224 | tf_op jit(solution)/shard_map/ppermute | solution.py:459
  130.0 3.3 %collective-permute-start.8 = (bf16[2,16,4096]{2,1,0:T(8,128)(2,1)S(1)}, bf16[2,16,4096]{2,1,0:T(8,128)(2,1)S(1)}, u32[]{:S(2)}, u32[]{:S(2)}) collective-permute-start(bf16[2,16,4096]{2,1,0:T(8,128)(2,1)S(1)} %add_convert_fusion), channel_id=1, source_target_pairs={{0,14},{1,15},{2,0},{3,1},{4,2},{5,3},{6,4},{7,5},{8,6},{9,7},{10,... | collective-permute-start | bytes 786440 | tf_op jit(solution)/shard_map/ppermute | solution.py:446
  133.4 5.4 %collective-permute-done.4 = bf16[2,16,4096]{2,1,0:T(8,128)(2,1)S(1)} collective-permute-done((bf16[2,16,4096]{2,1,0:T(8,128)(2,1)S(1)}, bf16[2,16,4096]{2,1,0:T(8,128)(2,1)S(1)}, u32[]{:S(2)}, u32[]{:S(2)}) %collective-permute-start.4) | collective-permute-done | bytes 262176 | tf_op jit(solution)/shard_map/ppermute | solution.py:446
  139.1 3.3 %collective-permute-start.9 = (bf16[1,16,4096]{2,1,0:T(8,128)(2,1)S(1)}, bf16[1,16,4096]{2,1,0:T(8,128)(2,1)S(1)}, u32[]{:S(2)}, u32[]{:S(2)}) collective-permute-start(bf16[1,16,4096]{2,1,0:T(8,128)(2,1)S(1)} %add_convert_fusion.17), channel_id=1, source_target_pairs={{0,14},{1,15},{2,0},{3,1},{4,2},{5,3},{6,4},{7,5},{8,6},{9,7},{10,... | collective-permute-start | bytes 393224 | tf_op jit(solution)/shard_map/ppermute | solution.py:446
  142.4 2.8 %collective-permute-done.5 = bf16[1,16,4096]{2,1,0:T(8,128)(2,1)S(1)} collective-permute-done((bf16[1,16,4096]{2,1,0:T(8,128)(2,1)S(1)}, bf16[1,16,4096]{2,1,0:T(8,128)(2,1)S(1)}, u32[]{:S(2)}, u32[]{:S(2)}) %collective-permute-start.5) | collective-permute-done | bytes 131104 | tf_op jit(solution)/shard_map/ppermute | solution.py:446
  (107 shorter events, 14.0 us)
Async XLA Ops:
  25.5 20.0 %all-to-all-start.1 = ((bf16[16,2,128,128]{3,2,1,0:T(8,128)(2,1)}), bf16[16,2,128,128]{3,2,1,0:T(8,128)(2,1)S(1)}, u32[]{:S(2)}, u32[]{:S(2)}) async-start(bf16[16,2,128,128]{3,2,1,0:T(8,128)(2,1)} %broadcast_in_dim.24), calls=%async_computation.1 | async-start | bytes 2097152 | tf_op jit(solution)/shard_map/all_to_all | solution.py:424
  30.4 23.3 %collective-permute-start = (bf16[16,2,128,128]{3,2,1,0:T(8,128)(2,1)S(1)}, bf16[16,2,128,128]{3,2,1,0:T(8,128)(2,1)S(1)}, u32[]{:S(2)}, u32[]{:S(2)}) collective-permute-start(bf16[16,2,128,128]{3,2,1,0:T(8,128)(2,1)S(1)} %all_to_all.10.refs_0_), channel_id=1, source_target_pairs={{0,1},{1,0},{2,3},{3,2},{4,5},{5,4},{6,7},{7,6},{8,9},{9,8},{10,11... | collective-permute-start | bytes 3145736 | tf_op jit(solution)/shard_map/ppermute | solution.py:425
  45.5 8.1 %collective-permute-start.10 = (bf16[16,2,128,128]{3,2,1,0:T(8,128)(2,1)S(1)}, bf16[16,2,128,128]{3,2,1,0:T(8,128)(2,1)}, u32[]{:S(2)}, u32[]{:S(2)}) collective-permute-start(bf16[16,2,128,128]{3,2,1,0:T(8,128)(2,1)S(1)} %all-to-all-done.1.refs_2_), channel_id=1, source_target_pairs={{0,1},{1,0},{2,3},{3,2},{4,5},{5,4},{6,7},{7,6},{8,9},{9,8},{10,11... | collective-permute-start | bytes 3145736 | tf_op jit(solution)/shard_map/ppermute | solution.py:425
  66.6 11.6 %collective-permute-start.11 = (bf16[128,8192]{1,0:T(8,128)(2,1)}, bf16[128,8192]{1,0:T(8,128)(2,1)S(1)}, u32[]{:S(2)}, u32[]{:S(2)}) collective-permute-start(bf16[128,8192]{1,0:T(8,128)(2,1)} %get-tuple-element.46), channel_id=1, source_target_pairs={{0,1},{1,0},{2,3},{3,2},{4,5},{5,4},{6,7},{7,6},{8,9},{9,8},{10,11... | collective-permute-start | bytes 6291464 | tf_op jit(solution)/shard_map/ppermute | solution.py:430
  81.2 12.3 %collective-permute-start.12 = (bf16[1,16,4096]{2,1,0:T(8,128)(2,1)S(1)}, bf16[1,16,4096]{2,1,0:T(8,128)(2,1)S(1)}, u32[]{:S(2)}, u32[]{:S(2)}) collective-permute-start(bf16[1,16,4096]{2,1,0:T(8,128)(2,1)S(1)} %get-tuple-element.51), channel_id=1, source_target_pairs={{0,2},{1,3},{2,4},{3,5},{4,6},{5,7},{6,8},{7,9},{8,10},{9,11},{10,... | collective-permute-start | bytes 393224 | tf_op jit(solution)/shard_map/ppermute | solution.py:459
  86.0 19.4 %collective-permute-start.2 = (bf16[2,16,4096]{2,1,0:T(8,128)(2,1)S(1)}, bf16[2,16,4096]{2,1,0:T(8,128)(2,1)S(1)}, u32[]{:S(2)}, u32[]{:S(2)}) collective-permute-start(bf16[2,16,4096]{2,1,0:T(8,128)(2,1)S(1)} %get-tuple-element.40), channel_id=1, source_target_pairs={{0,2},{1,3},{2,4},{3,5},{4,6},{5,7},{6,8},{7,9},{8,10},{9,11},{10,... | collective-permute-start | bytes 786440 | tf_op jit(solution)/shard_map/ppermute | solution.py:446
  88.0 21.3 %collective-permute-start.6 = (bf16[2,16,4096]{2,1,0:T(8,128)(2,1)S(1)}, bf16[2,16,4096]{2,1,0:T(8,128)(2,1)S(1)}, u32[]{:S(2)}, u32[]{:S(2)}) collective-permute-start(bf16[2,16,4096]{2,1,0:T(8,128)(2,1)S(1)} %get-tuple-element.43), channel_id=1, source_target_pairs={{0,14},{1,15},{2,0},{3,1},{4,2},{5,3},{6,4},{7,5},{8,6},{9,7},{10,... | collective-permute-start | bytes 786440 | tf_op jit(solution)/shard_map/ppermute | solution.py:446
  91.4 9.5 %collective-permute-start.16 = (bf16[1,16,4096]{2,1,0:T(8,128)(2,1)S(1)}, bf16[1,16,4096]{2,1,0:T(8,128)(2,1)S(1)}, u32[]{:S(2)}, u32[]{:S(2)}) collective-permute-start(bf16[1,16,4096]{2,1,0:T(8,128)(2,1)S(1)} %get-tuple-element.54), channel_id=1, source_target_pairs={{0,14},{1,15},{2,0},{3,1},{4,2},{5,3},{6,4},{7,5},{8,6},{9,7},{10,... | collective-permute-start | bytes 393224 | tf_op jit(solution)/shard_map/ppermute | solution.py:459
  93.3 9.7 %collective-permute-start.19 = (bf16[1,16,4096]{2,1,0:T(8,128)(2,1)S(1)}, bf16[1,16,4096]{2,1,0:T(8,128)(2,1)S(1)}, u32[]{:S(2)}, u32[]{:S(2)}) collective-permute-start(bf16[1,16,4096]{2,1,0:T(8,128)(2,1)S(1)} %get-tuple-element.58), channel_id=1, source_target_pairs={{0,2},{1,3},{2,4},{3,5},{4,6},{5,7},{6,8},{7,9},{8,10},{9,11},{10,... | collective-permute-start | bytes 393224 | tf_op jit(solution)/shard_map/ppermute | solution.py:459
  93.4 11.4 %collective-permute-start.22 = (bf16[1,16,4096]{2,1,0:T(8,128)(2,1)S(1)}, bf16[1,16,4096]{2,1,0:T(8,128)(2,1)S(1)}, u32[]{:S(2)}, u32[]{:S(2)}) collective-permute-start(bf16[1,16,4096]{2,1,0:T(8,128)(2,1)S(1)} %get-tuple-element.62), channel_id=1, source_target_pairs={{0,14},{1,15},{2,0},{3,1},{4,2},{5,3},{6,4},{7,5},{8,6},{9,7},{10,... | collective-permute-start | bytes 393224 | tf_op jit(solution)/shard_map/ppermute | solution.py:459
  100.9 8.6 %collective-permute-start.13 = (bf16[1,16,4096]{2,1,0:T(8,128)(2,1)S(1)}, bf16[1,16,4096]{2,1,0:T(8,128)(2,1)S(1)}, u32[]{:S(2)}, u32[]{:S(2)}) collective-permute-start(bf16[1,16,4096]{2,1,0:T(8,128)(2,1)S(1)} %add_convert_fusion.15), channel_id=1, source_target_pairs={{0,2},{1,3},{2,4},{3,5},{4,6},{5,7},{6,8},{7,9},{8,10},{9,11},{10,... | collective-permute-start | bytes 393224 | tf_op jit(solution)/shard_map/ppermute | solution.py:459
  103.1 9.7 %collective-permute-start.17 = (bf16[1,16,4096]{2,1,0:T(8,128)(2,1)S(1)}, bf16[1,16,4096]{2,1,0:T(8,128)(2,1)S(1)}, u32[]{:S(2)}, u32[]{:S(2)}) collective-permute-start(bf16[1,16,4096]{2,1,0:T(8,128)(2,1)S(1)} %add_convert_fusion.12), channel_id=1, source_target_pairs={{0,14},{1,15},{2,0},{3,1},{4,2},{5,3},{6,4},{7,5},{8,6},{9,7},{10,... | collective-permute-start | bytes 393224 | tf_op jit(solution)/shard_map/ppermute | solution.py:459
  104.8 8.2 %collective-permute-start.20 = (bf16[1,16,4096]{2,1,0:T(8,128)(2,1)S(1)}, bf16[1,16,4096]{2,1,0:T(8,128)(2,1)S(1)}, u32[]{:S(2)}, u32[]{:S(2)}) collective-permute-start(bf16[1,16,4096]{2,1,0:T(8,128)(2,1)S(1)} %add_convert_fusion.9), channel_id=1, source_target_pairs={{0,2},{1,3},{2,4},{3,5},{4,6},{5,7},{6,8},{7,9},{8,10},{9,11},{10,... | collective-permute-start | bytes 393224 | tf_op jit(solution)/shard_map/ppermute | solution.py:459
  105.4 10.9 %collective-permute-start.23 = (bf16[1,16,4096]{2,1,0:T(8,128)(2,1)S(1)}, bf16[1,16,4096]{2,1,0:T(8,128)(2,1)S(1)}, u32[]{:S(2)}, u32[]{:S(2)}) collective-permute-start(bf16[1,16,4096]{2,1,0:T(8,128)(2,1)S(1)} %add_convert_fusion.7), channel_id=1, source_target_pairs={{0,14},{1,15},{2,0},{3,1},{4,2},{5,3},{6,4},{7,5},{8,6},{9,7},{10,... | collective-permute-start | bytes 393224 | tf_op jit(solution)/shard_map/ppermute | solution.py:459
  109.3 17.1 %collective-permute-start.3 = (bf16[2,16,4096]{2,1,0:T(8,128)(2,1)S(1)}, bf16[2,16,4096]{2,1,0:T(8,128)(2,1)S(1)}, u32[]{:S(2)}, u32[]{:S(2)}) collective-permute-start(bf16[2,16,4096]{2,1,0:T(8,128)(2,1)S(1)} %add_convert_fusion.3), channel_id=1, source_target_pairs={{0,2},{1,3},{2,4},{3,5},{4,6},{5,7},{6,8},{7,9},{8,10},{9,11},{10,... | collective-permute-start | bytes 786440 | tf_op jit(solution)/shard_map/ppermute | solution.py:446
  109.5 20.3 %collective-permute-start.7 = (bf16[2,16,4096]{2,1,0:T(8,128)(2,1)S(1)}, bf16[2,16,4096]{2,1,0:T(8,128)(2,1)S(1)}, u32[]{:S(2)}, u32[]{:S(2)}) collective-permute-start(bf16[2,16,4096]{2,1,0:T(8,128)(2,1)S(1)} %add_convert_fusion.1), channel_id=1, source_target_pairs={{0,14},{1,15},{2,0},{3,1},{4,2},{5,3},{6,4},{7,5},{8,6},{9,7},{10,... | collective-permute-start | bytes 786440 | tf_op jit(solution)/shard_map/ppermute | solution.py:446
  112.8 8.1 %collective-permute-start.14 = (bf16[1,16,4096]{2,1,0:T(8,128)(2,1)S(1)}, bf16[1,16,4096]{2,1,0:T(8,128)(2,1)S(1)}, u32[]{:S(2)}, u32[]{:S(2)}) collective-permute-start(bf16[1,16,4096]{2,1,0:T(8,128)(2,1)S(1)} %add_convert_fusion.14), channel_id=1, source_target_pairs={{0,2},{1,3},{2,4},{3,5},{4,6},{5,7},{6,8},{7,9},{8,10},{9,11},{10,... | collective-permute-start | bytes 393224 | tf_op jit(solution)/shard_map/ppermute | solution.py:459
  113.0 17.0 %collective-permute-start.18 = (bf16[1,16,4096]{2,1,0:T(8,128)(2,1)S(1)}, bf16[1,16,4096]{2,1,0:T(8,128)(2,1)S(1)}, u32[]{:S(2)}, u32[]{:S(2)}) collective-permute-start(bf16[1,16,4096]{2,1,0:T(8,128)(2,1)S(1)} %add_convert_fusion.11), channel_id=1, source_target_pairs={{0,14},{1,15},{2,0},{3,1},{4,2},{5,3},{6,4},{7,5},{8,6},{9,7},{10,... | collective-permute-start | bytes 393224 | tf_op jit(solution)/shard_map/ppermute | solution.py:459
  116.3 17.0 %collective-permute-start.21 = (bf16[1,16,4096]{2,1,0:T(8,128)(2,1)S(1)}, bf16[1,16,4096]{2,1,0:T(8,128)(2,1)S(1)}, u32[]{:S(2)}, u32[]{:S(2)}) collective-permute-start(bf16[1,16,4096]{2,1,0:T(8,128)(2,1)S(1)} %add_convert_fusion.8), channel_id=1, source_target_pairs={{0,2},{1,3},{2,4},{3,5},{4,6},{5,7},{6,8},{7,9},{8,10},{9,11},{10,... | collective-permute-start | bytes 393224 | tf_op jit(solution)/shard_map/ppermute | solution.py:459
  126.4 6.9 %collective-permute-start.15 = (bf16[1,16,4096]{2,1,0:T(8,128)(2,1)S(1)}, bf16[1,16,4096]{2,1,0:T(8,128)(2,1)S(1)}, u32[]{:S(2)}, u32[]{:S(2)}) collective-permute-start(bf16[1,16,4096]{2,1,0:T(8,128)(2,1)S(1)} %add_convert_fusion.13), channel_id=1, source_target_pairs={{0,2},{1,3},{2,4},{3,5},{4,6},{5,7},{6,8},{7,9},{8,10},{9,11},{10,... | collective-permute-start | bytes 393224 | tf_op jit(solution)/shard_map/ppermute | solution.py:459
  126.4 6.9 %collective-permute-start.25 = (bf16[1,16,4096]{2,1,0:T(8,128)(2,1)S(1)}, bf16[1,16,4096]{2,1,0:T(8,128)(2,1)S(1)}, u32[]{:S(2)}, u32[]{:S(2)}) collective-permute-start(bf16[1,16,4096]{2,1,0:T(8,128)(2,1)S(1)} %add_convert_fusion.5), channel_id=1, source_target_pairs={{0,14},{1,15},{2,0},{3,1},{4,2},{5,3},{6,4},{7,5},{8,6},{9,7},{10,... | collective-permute-start | bytes 393224 | tf_op jit(solution)/shard_map/ppermute | solution.py:459
  129.8 9.1 %collective-permute-start.4 = (bf16[2,16,4096]{2,1,0:T(8,128)(2,1)S(1)}, bf16[2,16,4096]{2,1,0:T(8,128)(2,1)S(1)}, u32[]{:S(2)}, u32[]{:S(2)}) collective-permute-start(bf16[2,16,4096]{2,1,0:T(8,128)(2,1)S(1)} %add_convert_fusion.2), channel_id=1, source_target_pairs={{0,2},{1,3},{2,4},{3,5},{4,6},{5,7},{6,8},{7,9},{8,10},{9,11},{10,... | collective-permute-start | bytes 786440 | tf_op jit(solution)/shard_map/ppermute | solution.py:446
  130.0 9.0 %collective-permute-start.8 = (bf16[2,16,4096]{2,1,0:T(8,128)(2,1)S(1)}, bf16[2,16,4096]{2,1,0:T(8,128)(2,1)S(1)}, u32[]{:S(2)}, u32[]{:S(2)}) collective-permute-start(bf16[2,16,4096]{2,1,0:T(8,128)(2,1)S(1)} %add_convert_fusion), channel_id=1, source_target_pairs={{0,14},{1,15},{2,0},{3,1},{4,2},{5,3},{6,4},{7,5},{8,6},{9,7},{10,... | collective-permute-start | bytes 786440 | tf_op jit(solution)/shard_map/ppermute | solution.py:446
  138.9 6.3 %collective-permute-start.5 = (bf16[1,16,4096]{2,1,0:T(8,128)(2,1)S(1)}, bf16[1,16,4096]{2,1,0:T(8,128)(2,1)S(1)}, u32[]{:S(2)}, u32[]{:S(2)}) collective-permute-start(bf16[1,16,4096]{2,1,0:T(8,128)(2,1)S(1)} %add_convert_fusion.19), channel_id=1, source_target_pairs={{0,2},{1,3},{2,4},{3,5},{4,6},{5,7},{6,8},{7,9},{8,10},{9,11},{10,... | collective-permute-start | bytes 393224 | tf_op jit(solution)/shard_map/ppermute | solution.py:446
  (24 other events, 479.2 us)
